TPU v7x, 32 devices: a whole 2x2x4 slice. The times are simulated.
32 devices in a mesh: dp: 16 (over z, y, x), seq: 2 (over core).
Axes of the slice: x: 2, y: 2, z: 4, core: 2. Of those that a mesh axis runs over, the one named last changes fastest.
Arguments:
- hidden_in: bfloat16 [2, 16, 512, 768], P(None, 'dp', 'seq'), may hold values from -6 to 6
- cotangent: bfloat16 [2, 16, 512, 768], P(None, 'dp', 'seq'), may hold values from -6 to 6
- attention_keep: int32 [2, 16, 12, 512, 128], P(None, 'dp', None, 'seq'), may hold values from 0 to 4095
- output_keep: int32 [2, 16, 512, 192], P(None, 'dp', 'seq'), may hold values from 0 to 4095
- feed_keep: int32 [2, 16, 512, 192], P(None, 'dp', 'seq'), may hold values from 0 to 4095
- qkv_weight: bfloat16 [768, 2304], P(('dp', 'seq')), may hold values from -0.21875 to 0.21875
- qkv_bias: bfloat16 [1536], P(('dp', 'seq')), may hold values from -3 to 3
- out_weight: bfloat16 [768, 768], P(('dp', 'seq')), may hold values from -3 to 3
- out_bias: bfloat16 [768], P(('dp', 'seq')), may hold values from -3 to 3
- first_gain: bfloat16 [768], P(('dp', 'seq')), may hold values from 0.099609375 to 1.8984375
- first_shift: bfloat16 [768], P(('dp', 'seq')), may hold values from -3 to 3
- up_weight: bfloat16 [768, 3072], P(('dp', 'seq')), may hold values from -0.21875 to 0.21875
- up_bias: bfloat16 [3072], P(('dp', 'seq')), may hold values from -3 to 3
- down_weight: bfloat16 [3072, 768], P(('dp', 'seq')), may hold values from -0.109375 to 0.109375
- down_bias: bfloat16 [768], P(('dp', 'seq')), may hold values from -3 to 3
- second_gain: bfloat16 [768], P(('dp', 'seq')), may hold values from 0.099609375 to 1.8984375
- second_shift: bfloat16 [768], P(('dp', 'seq')), may hold values from -3 to 3
Outputs:
- layer_out: bfloat16 [2, 16, 512, 768], P(None, 'dp', 'seq')
- grad_input: bfloat16 [2, 16, 512, 768], P(None, 'dp', 'seq')
- grad_qkv_weight: float32 [768, 2304], P(('dp', 'seq'))
- grad_qkv_bias: float32 [1536], P(('dp', 'seq'))
- grad_out_weight: float32 [768, 768], P(('dp', 'seq'))
- grad_out_bias: float32 [768], P(('dp', 'seq'))
- grad_first_gain: float32 [768], P(('dp', 'seq'))
- grad_first_shift: float32 [768], P(('dp', 'seq'))
- grad_up_weight: float32 [768, 3072], P(('dp', 'seq'))
- grad_up_bias: float32 [3072], P(('dp', 'seq'))
- grad_down_weight: float32 [3072, 768], P(('dp', 'seq'))
- grad_down_bias: float32 [768], P(('dp', 'seq'))
- grad_second_gain: float32 [768], P(('dp', 'seq'))
- grad_second_shift: float32 [768], P(('dp', 'seq'))
Inputs may be any that keep to these rules, and one draw needn't show every extreme that they name: `attention_keep`: each word packs four 3-bit values, lowest bits first. `output_keep`: each word packs four 3-bit values, lowest bits first. `feed_keep`: each word packs four 3-bit values, lowest bits first.
All inputs are finite; a program needn't handle non-finite values.
Results may differ from a plain program's by a relative error of at most 0.015.
Values may be sent and summed in bfloat16 or wider, within the bound.
No kernel may reach another device: no remote copies, remote signals or barrier semaphores. Data moves between devices by JAX's collectives and lax.ppermute only.
A program may use at most 192 MiB of HBM per device.

v0:
```python
import jax
import jax.numpy as jnp
from jax import lax
from jax.sharding import PartitionSpec as P

H = 12
MICRO = 2


epsilon = 1e-12
keep_scale = 8.0 / 7.0
root_half = 0.7071067811865476
inverse_root_tau = 0.3989422804014327


def unpack_keep(packed_words):
    shifts = jnp.arange(4, dtype=jnp.int32) * 3
    nibble = jnp.right_shift(packed_words[..., None], shifts) & 7
    keep_value = (nibble >= 1).astype(jnp.float32) * keep_scale
    return keep_value.reshape(packed_words.shape[:-1] + (packed_words.shape[-1] * 4,))


def normalize(values, norm_gain, norm_shift):
    centred = values - jnp.mean(values, axis=-1, keepdims=True)
    inverse = lax.rsqrt(jnp.mean(centred * centred, axis=-1, keepdims=True) + epsilon)
    scaled = centred * inverse
    return (scaled * norm_gain + norm_shift, scaled, inverse)


def norm_back(upstream, scaled, inverse, norm_gain):
    weighted = upstream * norm_gain
    centre_term = jnp.mean(weighted, axis=-1, keepdims=True)
    slope_term = jnp.mean(weighted * scaled, axis=-1, keepdims=True)
    return inverse * (weighted - centre_term - scaled * slope_term)


def gelu_slope(inner_sum):
    normal_cdf = 0.5 * (1.0 + lax.erf(inner_sum * root_half))
    density = jnp.exp(-0.5 * inner_sum * inner_sum) * inverse_root_tau
    return normal_cdf + inner_sum * density


def matmul(left_side, right_side):
    return jnp.dot(left_side, right_side, preferred_element_type=jnp.float32)


def local(
    hidden_in,
    cotangent,
    attention_keep,
    output_keep,
    feed_keep,
    qkv_weight,
    qkv_bias,
    out_weight,
    out_bias,
    first_gain,
    first_shift,
    up_weight,
    up_bias,
    down_weight,
    down_bias,
    second_gain,
    second_shift,
):
    model_width = hidden_in.shape[-1]
    sequence_count = hidden_in.shape[1]
    local_tokens = hidden_in.shape[2]
    token_rows = sequence_count * local_tokens
    head_count = H
    head_size = model_width // head_count
    held_params = (
        lax.all_gather(qkv_weight, ("dp", "seq"), axis=0, tiled=True),
        lax.all_gather(qkv_bias, ("dp", "seq"), axis=0, tiled=True),
        lax.all_gather(out_weight, ("dp", "seq"), axis=0, tiled=True),
        lax.all_gather(out_bias, ("dp", "seq"), axis=0, tiled=True),
        lax.all_gather(first_gain, ("dp", "seq"), axis=0, tiled=True),
        lax.all_gather(first_shift, ("dp", "seq"), axis=0, tiled=True),
        lax.all_gather(up_weight, ("dp", "seq"), axis=0, tiled=True),
        lax.all_gather(up_bias, ("dp", "seq"), axis=0, tiled=True),
        lax.all_gather(down_weight, ("dp", "seq"), axis=0, tiled=True),
        lax.all_gather(down_bias, ("dp", "seq"), axis=0, tiled=True),
        lax.all_gather(second_gain, ("dp", "seq"), axis=0, tiled=True),
        lax.all_gather(second_shift, ("dp", "seq"), axis=0, tiled=True),
    )
    totals = None
    outputs = []
    inputs_grad = []
    for micro_step in range(MICRO):
        (
            full_qkv_w,
            full_qkv_b,
            full_out_w,
            full_out_b,
            full_gain_one,
            full_shift_one,
            full_up_w,
            full_up_b,
            full_down_w,
            full_down_b,
            full_gain_two,
            full_shift_two,
        ) = held_params
        rows_in = hidden_in[micro_step].reshape(token_rows, model_width)
        qkv_float = full_qkv_b.astype(jnp.float32)
        bias_full = jnp.concatenate(
            [
                qkv_float[:model_width],
                jnp.zeros((model_width,), jnp.float32),
                qkv_float[model_width:],
            ]
        )
        projected = (matmul(rows_in, full_qkv_w) + bias_full).astype(jnp.bfloat16)
        queries = projected[:, :model_width].reshape(
            sequence_count, local_tokens, head_count, head_size
        )
        keys_local = projected[:, model_width : 2 * model_width].reshape(
            sequence_count, local_tokens, model_width
        )
        values_local = projected[:, 2 * model_width :].reshape(
            sequence_count, local_tokens, model_width
        )
        keys_all, values_all = (
            lax.all_gather(keys_local, "seq", axis=1, tiled=True),
            lax.all_gather(values_local, "seq", axis=1, tiled=True),
        )
        keys_heads = keys_all.reshape(sequence_count, -1, head_count, head_size)
        values_heads = values_all.reshape(sequence_count, -1, head_count, head_size)
        scores = (
            jnp.einsum("sqhd,skhd->shqk", queries, keys_heads, preferred_element_type=jnp.float32)
            * 0.125
        )
        row_peak = jnp.max(scores, axis=-1, keepdims=True)
        exponent = jnp.exp(scores - row_peak)
        row_total = jnp.sum(exponent, axis=-1, keepdims=True)
        log_total = row_peak + jnp.log(row_total)
        softmax_weights = exponent / row_total
        keep_attention = unpack_keep(attention_keep[micro_step])
        dropped = (softmax_weights * keep_attention).astype(jnp.bfloat16)
        context = jnp.einsum(
            "shqk,skhd->sqhd", dropped, values_heads, preferred_element_type=jnp.float32
        )
        context = context.reshape(token_rows, model_width).astype(jnp.bfloat16)
        attended = matmul(context, full_out_w) + full_out_b.astype(jnp.float32)
        keep_output = unpack_keep(output_keep[micro_step]).reshape(token_rows, model_width)
        first_sum = rows_in.astype(jnp.float32) + attended * keep_output
        gain_one = full_gain_one.astype(jnp.float32)
        normed, scaled_one, inverse_one = normalize(
            first_sum, gain_one, full_shift_one.astype(jnp.float32)
        )
        normed_low = normed.astype(jnp.bfloat16)
        inner_sum = matmul(normed_low, full_up_w) + full_up_b.astype(jnp.float32)
        activated = jax.nn.gelu(inner_sum, approximate=False).astype(jnp.bfloat16)
        outer_sum = matmul(activated, full_down_w) + full_down_b.astype(jnp.float32)
        keep_feed = unpack_keep(feed_keep[micro_step]).reshape(token_rows, model_width)
        second_sum = normed + outer_sum * keep_feed
        gain_two = full_gain_two.astype(jnp.float32)
        result, scaled_two, inverse_two = normalize(
            second_sum, gain_two, full_shift_two.astype(jnp.float32)
        )
        outputs.append(
            result.astype(jnp.bfloat16).reshape(sequence_count, local_tokens, model_width)
        )
        (
            back_qkv_w,
            back_qkv_b,
            back_out_w,
            back_out_b,
            back_gain_one,
            back_shift_one,
            back_up_w,
            back_up_b,
            back_down_w,
            back_down_b,
            back_gain_two,
            back_shift_two,
        ) = held_params
        upstream = cotangent[micro_step].reshape(token_rows, model_width).astype(jnp.float32)
        g_second = norm_back(upstream, scaled_two, inverse_two, back_gain_two.astype(jnp.float32))
        grad_gain_two = jnp.sum(upstream * scaled_two, axis=0)
        grad_shift_two = jnp.sum(upstream, axis=0)
        g_outer = (g_second * keep_feed).astype(jnp.bfloat16)
        grad_down_b = jnp.sum(g_outer.astype(jnp.float32), axis=0)
        grad_down_w = matmul(activated.T, g_outer)
        g_inner = (matmul(g_outer, back_down_w.T) * gelu_slope(inner_sum)).astype(jnp.bfloat16)
        grad_up_b = jnp.sum(g_inner.astype(jnp.float32), axis=0)
        grad_up_w = matmul(normed_low.T, g_inner)
        g_normed = g_second + matmul(g_inner, back_up_w.T)
        g_first = norm_back(g_normed, scaled_one, inverse_one, back_gain_one.astype(jnp.float32))
        grad_gain_one = jnp.sum(g_normed * scaled_one, axis=0)
        grad_shift_one = jnp.sum(g_normed, axis=0)
        g_attended = (g_first * keep_output).astype(jnp.bfloat16)
        grad_out_b = jnp.sum(g_attended.astype(jnp.float32), axis=0)
        grad_out_w = matmul(context.T, g_attended)
        g_context = matmul(g_attended, back_out_w.T).astype(jnp.bfloat16)
        g_context = g_context.reshape(sequence_count, local_tokens, head_count, head_size)
        keys_again, values_again = (
            lax.all_gather(keys_local, "seq", axis=1, tiled=True),
            lax.all_gather(values_local, "seq", axis=1, tiled=True),
        )
        keys_heads = keys_again.reshape(sequence_count, -1, head_count, head_size)
        values_heads = values_again.reshape(sequence_count, -1, head_count, head_size)
        scores_again = (
            jnp.einsum("sqhd,skhd->shqk", queries, keys_heads, preferred_element_type=jnp.float32)
            * 0.125
        )
        weights_again = jnp.exp(scores_again - log_total)
        dropped_again = (weights_again * keep_attention).astype(jnp.bfloat16)
        g_values_all = jnp.einsum(
            "shqk,sqhd->skhd", dropped_again, g_context, preferred_element_type=jnp.float32
        )
        g_dropped = jnp.einsum(
            "sqhd,skhd->shqk", g_context, values_heads, preferred_element_type=jnp.float32
        )
        g_weights = g_dropped * keep_attention
        row_delta = jnp.sum(g_weights * weights_again, axis=-1, keepdims=True)
        g_scores = (weights_again * (g_weights - row_delta)).astype(jnp.bfloat16)
        g_queries = (
            jnp.einsum("shqk,skhd->sqhd", g_scores, keys_heads, preferred_element_type=jnp.float32)
            * 0.125
        )
        g_keys_all = (
            jnp.einsum("shqk,sqhd->skhd", g_scores, queries, preferred_element_type=jnp.float32)
            * 0.125
        )
        g_keys, g_values = (
            lax.psum_scatter(
                g_keys_all.reshape(sequence_count, -1, model_width).astype(jnp.bfloat16),
                "seq",
                scatter_dimension=1,
                tiled=True,
            ).astype(jnp.float32),
            lax.psum_scatter(
                g_values_all.reshape(sequence_count, -1, model_width).astype(jnp.bfloat16),
                "seq",
                scatter_dimension=1,
                tiled=True,
            ).astype(jnp.float32),
        )
        g_projected = jnp.concatenate(
            [
                g_queries.reshape(token_rows, model_width),
                g_keys.reshape(token_rows, model_width),
                g_values.reshape(token_rows, model_width),
            ],
            axis=1,
        ).astype(jnp.bfloat16)
        g_projected_float = g_projected.astype(jnp.float32)
        grad_qkv_b = jnp.concatenate(
            [
                jnp.sum(g_projected_float[:, :model_width], axis=0),
                jnp.sum(g_projected_float[:, 2 * model_width :], axis=0),
            ]
        )
        grad_qkv_w = matmul(rows_in.T, g_projected)
        input_grad = g_first + matmul(g_projected, back_qkv_w.T)
        inputs_grad.append(
            input_grad.astype(jnp.bfloat16).reshape(sequence_count, local_tokens, model_width)
        )
        grads_now = (
            grad_qkv_w,
            grad_qkv_b,
            grad_out_w,
            grad_out_b,
            grad_gain_one,
            grad_shift_one,
            grad_up_w,
            grad_up_b,
            grad_down_w,
            grad_down_b,
            grad_gain_two,
            grad_shift_two,
        )
        if totals is None:
            totals = grads_now
        else:
            totals = tuple((before + added for before, added in zip(totals, grads_now)))
    summed = (
        lax.psum_scatter(totals[0], ("dp", "seq"), scatter_dimension=0, tiled=True),
        lax.psum_scatter(totals[1], ("dp", "seq"), scatter_dimension=0, tiled=True),
        lax.psum_scatter(totals[2], ("dp", "seq"), scatter_dimension=0, tiled=True),
        lax.psum_scatter(totals[3], ("dp", "seq"), scatter_dimension=0, tiled=True),
        lax.psum_scatter(totals[4], ("dp", "seq"), scatter_dimension=0, tiled=True),
        lax.psum_scatter(totals[5], ("dp", "seq"), scatter_dimension=0, tiled=True),
        lax.psum_scatter(totals[6], ("dp", "seq"), scatter_dimension=0, tiled=True),
        lax.psum_scatter(totals[7], ("dp", "seq"), scatter_dimension=0, tiled=True),
        lax.psum_scatter(totals[8], ("dp", "seq"), scatter_dimension=0, tiled=True),
        lax.psum_scatter(totals[9], ("dp", "seq"), scatter_dimension=0, tiled=True),
        lax.psum_scatter(totals[10], ("dp", "seq"), scatter_dimension=0, tiled=True),
        lax.psum_scatter(totals[11], ("dp", "seq"), scatter_dimension=0, tiled=True),
    )
    return (
        jnp.stack(outputs, axis=0),
        jnp.stack(inputs_grad, axis=0),
        summed[0],
        summed[1],
        summed[2],
        summed[3],
        summed[4],
        summed[5],
        summed[6],
        summed[7],
        summed[8],
        summed[9],
        summed[10],
        summed[11],
    )


def solution(mesh):
    return jax.shard_map(
        local,
        mesh=mesh,
        in_specs=(
            P(None, "dp", "seq", None),
            P(None, "dp", "seq", None),
            P(None, "dp", None, "seq", None),
            P(None, "dp", "seq", None),
            P(None, "dp", "seq", None),
            P(("dp", "seq"), None),
            P(("dp", "seq")),
            P(("dp", "seq"), None),
            P(("dp", "seq")),
            P(("dp", "seq")),
            P(("dp", "seq")),
            P(("dp", "seq"), None),
            P(("dp", "seq")),
            P(("dp", "seq"), None),
            P(("dp", "seq")),
            P(("dp", "seq")),
            P(("dp", "seq")),
        ),
        out_specs=(
            P(None, "dp", "seq", None),
            P(None, "dp", "seq", None),
            P(("dp", "seq"), None),
            P(("dp", "seq")),
            P(("dp", "seq"), None),
            P(("dp", "seq")),
            P(("dp", "seq")),
            P(("dp", "seq")),
            P(("dp", "seq"), None),
            P(("dp", "seq")),
            P(("dp", "seq"), None),
            P(("dp", "seq")),
            P(("dp", "seq")),
            P(("dp", "seq")),
        ),
        check_vma=False,
    )
```

profile of v0, /device:TPU:0, one launch (start us, length us, event | category | flops | bytes accessed | tf_op | source)
XLA Modules:
  0.0 880.0 jit_solution(11111580387961747564)
XLA Ops:
  16.8 42.7 %all-reduce.17 = (bf16[1536]{0:T(1024)(128)(2,1)S(1)}, bf16[3072]{0:T(1024)(128)(2,1)S(1)}, bf16[768]{0:T(1024)(128)(2,1)S(1)}, bf16[768]{0:T(1024)(128)(2,1)S(1...) all-reduce(bf16[1536]{0:T(1024)(128)(2,1)S(1)} %dynamic-update-slic, ...), channel_id=1, replica_groups=mesh['dp'=16,'seq'=2] {'dp','seq'}, use_global_device_ids=true, to_apply=%add | all-reduce | flops 9216 | bytes 36864
  70.0 2.1 slice_bitcast_fusion.1
  72.1 1.6 copy.72
  74.2 3.7 shift_right_arithmetic.167
  78.0 7.7 shift_right_arithmetic.168
  85.7 6.7 copy.80
  92.4 3.7 shift_right_arithmetic.149
  96.1 7.7 shift_right_arithmetic.150
  103.7 6.6 copy.73
  110.4 6.1 and_compare_fusion.1
  116.5 1.9 and_compare_fusion.4
  118.4 3.2 fusion.9
  122.6 2.9 all-gather.3
  125.5 2.3 copy.78
  129.0 4.2 fusion.8
  133.2 2.5 all-gather.2
  135.7 2.3 copy.76
  138.1 2.2 fusion.130
  140.3 2.5 all-gather.1
  142.8 2.3 copy.71
  145.1 1.9 copy.70
  147.0 4.1 all-gather
  151.1 2.3 copy.69
  153.4 2.4 multiply_reduce_fusion.3
  155.8 1.6 fusion.4
  158.4 3.4 fusion.64
  161.9 2.2 fusion.133
  168.8 2.8 fusion.67
  175.1 20.0 %all-gather.13.cloned.1.call-done = bf16[768,3072]{1,0:T(8,128)(2,1)} async-done(((bf16[24,3072]{1,0:T(8,128)(2,1)}), bf16[768,3072]{1,0:T(8,128)(2,1)}) %all-gather.13.cloned.1.call-update) | async-done | bytes 4718608 | tf_op jit(solution)/shard_map/all_gather | solution.py:79
  195.1 11.2 %fusion.12 = (bf16[256,3072]{1,0:T(8,128)(2,1)}, f32[256,3072]{1,0:T(8,128)}) fusion(f32[3072]{0:T(1024)} %convert_element_type.284, bf16[768,3072]{1,0:T(8,128)(2,1)} %all-gather.13.cloned.1.call-done, f32[256,768]{1,0:T(8,128)S(1)} %copy-done.30, f32[768]{0:T(1024)S(1)} %convert_element_type.282, f32[768]{0:T(1024)S(1)} %convert_element_type.281, ...), kind=kOutput, calls=%fused_computation.43 | convolution fusion | flops 1260847104 | bytes 10244096 | tf_op jit(solution)/shard_map/dot_general | solution.py:44
  206.3 54.0 %all-gather.15.cloned.1.call-done = bf16[3072,768]{1,0:T(8,128)(2,1)} async-done(((bf16[96,768]{1,0:T(8,128)(2,1)}), bf16[3072,768]{1,0:T(8,128)(2,1)}) %all-gather.15.cloned.1.call-update) | async-done | bytes 4718608 | tf_op jit(solution)/shard_map/all_gather | solution.py:81
  260.3 4.5 fusion.134
  265.2 8.1 fusion.15
  273.3 1.6 fusion.136
  276.6 2.6 convert_reduce_fusion.4
  279.2 3.0 convert_reduce_fusion.1
  282.2 2.5 multiply_reduce_fusion.5
  284.7 3.0 convert_reduce_fusion
  287.7 3.8 convert_reduce_fusion.7
  293.0 5.4 fusion.46
  298.4 6.9 multiply_reduce_fusion.1
  308.4 6.5 multiply_reduce_fusion
  316.3 7.6 multiply_convert_fusion
  323.9 1.7 copy-done.3
  327.3 6.3 fusion.49
  335.4 1.6 fusion.137
  337.0 1.9 convolution_add_fusion.6
  339.0 3.3 fusion.62
  342.3 1.8 fusion.63
  344.1 5.3 fusion.100
  349.4 9.1 %reduce-scatter.15.cloned.1.call-done = bf16[1,256,768]{1,2,0:T(8,128)(2,1)} async-done(((bf16[1,512,768]{1,2,0:T(8,128)(2,1)}), bf16[1,256,768]{1,2,0:T(8,128)(2,1)}) %reduce-scatter.15.cloned.1.call-update) | async-done | bytes 393232 | tf_op jit(solution)/shard_map/reduce_scatter | solution.py:227
  358.5 7.2 add_bitcast_fusion
  365.7 8.0 copy.86
  374.9 3.1 fusion.123
  378.1 5.3 convolution_add_fusion.1
  383.4 3.1 fusion.138
  386.5 5.2 convolution_add_fusion
  400.0 2.0 pad_maximum_fusion.2
  403.0 42.0 %all-reduce.16 = (f32[1536]{0:T(1024)S(1)}, f32[768]{0:T(1024)S(1)}, f32[768]{0:T(1024)S(1)}, f32[768]{0:T(1024)S(1)}, f32[3072]{0:T(1024)S(1)}, /*index=5*/f32[...) all-reduce(f32[1536]{0:T(1024)S(1)} %maximum_add_fusion, ...), channel_id=11, replica_groups=mesh['dp'=16,'seq'=2] {'dp','seq'}, use_global_device_ids=true, to_apply=%region_31.0.clone | all-reduce | flops 9216 | bytes 73728
  449.8 3.7 fusion.70
  455.9 8.8 %reduce-scatter.19.cloned.1.call-done = f32[24,768]{1,0:T(8,128)} async-done(((f32[768,768]{1,0:T(8,128)}), f32[24,768]{1,0:T(8,128)}) %reduce-scatter.19.cloned.1.call-update) | async-done | bytes 73744 | tf_op jit(solution)/shard_map/reduce_scatter | solution.py:281
  464.7 125.0 %reduce-scatter.25.cloned.1.call-done = f32[24,2304]{1,0:T(8,128)} async-done(((f32[768,2304]{1,0:T(8,128)}), f32[24,2304]{1,0:T(8,128)}) %reduce-scatter.25.cloned.1.call-update) | async-done | bytes 221200
  589.7 141.2 %reduce-scatter.21.cloned.1.call-done = f32[24,3072]{1,0:T(8,128)} async-done(((f32[768,3072]{1,0:T(8,128)}), f32[24,3072]{1,0:T(8,128)}) %reduce-scatter.21.cloned.1.call-update) | async-done | bytes 294928 | tf_op jit(solution)/shard_map/reduce_scatter | solution.py:285
  730.9 142.0 %reduce-scatter.23.cloned.1.call-done = f32[96,768]{1,0:T(8,128)} async-done(((f32[3072,768]{1,0:T(8,128)}), f32[96,768]{1,0:T(8,128)}) %reduce-scatter.23.cloned.1.call-update) | async-done | bytes 294928 | tf_op jit(solution)/shard_map/reduce_scatter | solution.py:287
  (345 shorter events, 59.9 us)
Async XLA Ops:
  7.2 111.3 %all-gather.9.cloned.1.call-start = ((), (), s32[]{:S(2)}) async-start(), calls=%async_computation.8 | async-start | bytes 3649536 | tf_op jit(solution)/shard_map/all_gather | solution.py:73
  7.9 153.9 %all-gather.11.cloned.1.call-start = ((), (), s32[]{:S(2)}) async-start(), calls=%async_computation.9 | async-start | bytes 1216512 | tf_op jit(solution)/shard_map/all_gather | solution.py:75
  8.7 186.4 %all-gather.13.cloned.1.call-start = ((), (), s32[]{:S(2)}) async-start(), calls=%async_computation.10 | async-start | bytes 4866048 | tf_op jit(solution)/shard_map/all_gather | solution.py:79
  9.4 250.9 %all-gather.15.cloned.1.call-start = ((), (), s32[]{:S(2)}) async-start(), calls=%async_computation.11 | async-start | bytes 4866048 | tf_op jit(solution)/shard_map/all_gather | solution.py:81
  10.0 334.1 %reduce-scatter.13.cloned.1.call-start = ((), (), s32[]{:S(2)}) async-start(), calls=%async_computation.13 | async-start | bytes 1179648 | tf_op jit(solution)/shard_map/reduce_scatter | solution.py:233
  85.7 6.7 copy-start.15
  110.3 8.1 copy-start.81
  110.3 6.2 copy-start.25
  110.3 6.2 copy-start.26
  110.3 6.2 copy-start.27
  110.4 6.2 copy-start.28
  116.5 51.3 %copy-start.4 = (pred[12,256,512]{2,1,0:T(32,128)(4,1)}, pred[12,256,512]{2,1,0:T(32,128)(4,1)S(1)}, u32[]{:S(2)}) copy-start(pred[12,256,512]{2,1,0:T(32,128)(4,1)S(1)} %get-tuple-element.130) | copy-start | bytes 4718596
  116.5 181.8 %copy-start.6 = (pred[12,256,512]{2,1,0:T(32,128)(4,1)}, pred[12,256,512]{2,1,0:T(32,128)(4,1)S(1)}, u32[]{:S(2)}) copy-start(pred[12,256,512]{2,1,0:T(32,128)(4,1)S(1)} %get-tuple-element.129) | copy-start | bytes 4718596
  129.0 4.2 copy-start.43
  171.7 23.4 %copy-start.30 = (f32[256,768]{1,0:T(8,128)S(1)}, f32[256,768]{1,0:T(8,128)}, u32[]{:S(2)}) copy-start(f32[256,768]{1,0:T(8,128)} %copy-done.29) | copy-start | bytes 2359300
  172.4 115.3 %copy-start.8 = (f32[256,768]{1,0:T(8,128)}, f32[256,768]{1,0:T(8,128)S(1)}, u32[]{:S(2)}) copy-start(f32[256,768]{1,0:T(8,128)S(1)} %get-tuple-element.142) | copy-start | bytes 2359300
  172.4 205.6 %copy-start.69 = (f32[256]{0:T(256)}, f32[256]{0:T(256)S(1)}, u32[]{:S(2)}) copy-start(f32[256]{0:T(256)S(1)} %broadcast_multiply_fusion.9) | copy-start | bytes 3076
  260.3 4.8 copy-start.77
  260.3 4.8 copy-start.80
  260.3 4.8 copy-start.94
  260.3 12.9 %slice-start.4 = ((s8[4718592]{0:T(1024)(128)(4,1)}), s8[4194304]{0:T(1024)(128)(4,1)S(1)}, s32[]{:S(2)}) async-start(s8[4718592]{0:T(1024)(128)(4,1)} %bitcast.251), calls=%async_computation.24 | async-start | bytes 8388608
  265.1 8.2 copy-start.52
  265.1 8.1 copy-start.87
  265.2 8.1 slice-start.5
  275.2 3.9 copy-start.98
  279.2 5.5 copy-start.37
  287.7 3.8 copy-start.49
  287.7 4.6 copy-start.19
  293.0 5.4 copy-start.36
  293.0 5.4 copy-start.64
  298.3 7.0 copy-start.93
  298.4 7.0 copy-start.92
  298.4 7.0 copy-start.9
  298.4 7.0 copy-start.54
  298.4 7.0 copy-start.57
  298.4 7.0 copy-start.78
  298.4 8.0 copy-start.20
  305.4 9.6 %slice-start.2 = ((s8[6291456]{0:T(1024)(128)(4,1)}), s8[2097152]{0:T(1024)(128)(4,1)S(1)}, s32[]{:S(2)}) async-start(s8[6291456]{0:T(1024)(128)(4,1)} %bitcast.207), calls=%async_computation.22 | async-start | bytes 4194304
  306.4 8.6 copy-start.23
  307.8 36.2 %reduce-scatter.11.cloned.1.call-start = ((), (), s32[]{:S(2)}) async-start(), calls=%async_computation.12 | async-start | bytes 1179648 | tf_op jit(solution)/shard_map/reduce_scatter | solution.py:227
  308.3 6.6 slice-start
  308.3 6.6 slice-start.1
  308.4 7.0 slice-start.3
  308.4 7.5 copy-start.5
  308.4 7.9 copy-start.7
  308.4 7.9 copy-start.65
  308.4 7.9 copy-start.68
  316.3 9.4 %copy-start.21 = (bf16[256,768]{0,1:T(8,128)(2,1)S(1)}, bf16[256,768]{0,1:T(8,128)(2,1)}, u32[]{:S(2)}) copy-start(bf16[256,768]{0,1:T(8,128)(2,1)} %copy.70) | copy-start | bytes 1179652
  327.3 6.5 copy-start.2
  327.3 22.1 %reduce-scatter.17.cloned.1.call-start = ((), (), s32[]{:S(2)}) async-start(), calls=%async_computation.15 | async-start | bytes 1179648 | tf_op jit(solution)/shard_map/reduce_scatter | solution.py:233
  333.7 24.8 %reduce-scatter.15.cloned.1.call-start = ((), (), s32[]{:S(2)}) async-start(), calls=%async_computation.14 | async-start | bytes 1179648 | tf_op jit(solution)/shard_map/reduce_scatter | solution.py:227
  335.3 129.4 %reduce-scatter.19.cloned.1.call-start = ((), (), s32[]{:S(2)}) async-start(), calls=%async_computation.16 | async-start | bytes 2433024 | tf_op jit(solution)/shard_map/reduce_scatter | solution.py:281
  338.9 250.8 %reduce-scatter.25.cloned.1.call-start = ((), (), s32[]{:S(2)}) async-start(), calls=%async_computation.19 | async-start | bytes 7299072
  344.1 14.4 %copy-start.22 = (bf16[12,64,256]{2,1,0:T(8,128)(2,1)S(1)}, bf16[12,64,256]{2,1,0:T(8,128)(2,1)}, u32[]{:S(2)}) copy-start(bf16[12,64,256]{2,1,0:T(8,128)(2,1)} %fusion.63) | copy-start | bytes 1179652
  344.1 14.4 %copy-start.56 = (bf16[2,1,256,768]{3,2,1,0:T(8,128)(2,1)S(1)}, bf16[2,1,256,768]{3,2,1,0:T(8,128)(2,1)}, u32[]{:S(2)}) copy-start(bf16[2,1,256,768]{3,2,1,0:T(8,128)(2,1)} %param.17) | copy-start | bytes 2359300
  373.8 4.3 copy-start.10
  373.8 4.3 copy-start.79
  373.8 357.1 %reduce-scatter.21.cloned.1.call-start = ((), (), s32[]{:S(2)}) async-start(), calls=%async_computation.17 | async-start | bytes 9732096 | tf_op jit(solution)/shard_map/reduce_scatter | solution.py:285
  383.4 489.5 %reduce-scatter.23.cloned.1.call-start = ((), (), s32[]{:S(2)}) async-start(), calls=%async_computation.18 | async-start | bytes 9732096 | tf_op jit(solution)/shard_map/reduce_scatter | solution.py:287
  391.7 8.3 copy-start.42
  391.7 10.3 %copy-start.40 = (bf16[1,256,768]{1,2,0:T(8,128)(2,1)S(1)}, bf16[1,256,768]{1,2,0:T(8,128)(2,1)}, u32[]{:S(2)}) copy-start(bf16[1,256,768]{1,2,0:T(8,128)(2,1)} %reduce-scatter.13.cloned.1.call-done) | copy-start | bytes 1179652
  391.7 10.3 %copy-start.41 = (bf16[1,256,768]{1,2,0:T(8,128)(2,1)S(1)}, bf16[1,256,768]{1,2,0:T(8,128)(2,1)}, u32[]{:S(2)}) copy-start(bf16[1,256,768]{1,2,0:T(8,128)(2,1)} %reduce-scatter.11.cloned.1.call-done) | copy-start | bytes 1179652
  402.2 47.5 %copy-start.47 = (bf16[1,256,768]{1,2,0:T(8,128)(2,1)S(1)}, bf16[1,256,768]{1,2,0:T(8,128)(2,1)}, u32[]{:S(2)}) copy-start(bf16[1,256,768]{1,2,0:T(8,128)(2,1)} %reduce-scatter.17.cloned.1.call-done) | copy-start | bytes 1179652
  449.8 3.9 copy-start.97
  (53 other events, 130.4 us)
Sparse Core Ops, SparseCore 0:
  10.9 62.8 all-gather.8
  76.7 52.8 all-gather.10
  132.5 62.5 all-gather.12
  197.9 62.4 all-gather.14
  308.0 7.0 reduce-scatter.12
  327.4 7.0 reduce-scatter.10
  337.3 9.4 reduce-scatter.16
  349.1 9.3 reduce-scatter.14
  364.4 100.3 reduce-scatter.18
  471.8 117.9 reduce-scatter.24
  596.2 134.6 reduce-scatter.20
  738.3 134.6 reduce-scatter.22
where the time goes:
time: 891 us; the launch traced here: 880 us
  waiting for transfers between devices  503 us (56%)
  matrix products  130 us (15%)
  blocking collectives  96.7 us (11%)
  local copies, waits for them, and re-layouts  93.9 us (11%)
  other arithmetic  39.9 us (4%)
  between operations  15.8 us (2%)
    reduce_scatter x1, waiting for transfers between devices, local(): lax.psum_scatter(totals[8], ('dp', 'seq'), scatter_dimension=0, tiled=True)  142 us
    reduce_scatter x1, waiting for transfers between devices, local(): lax.psum_scatter(totals[6], ('dp', 'seq'), scatter_dimension=0, tiled=True)  141 us
    unnamed x13, waiting for transfers between devices  128 us
    dot_general x24, matrix products, matmul(): return jnp.dot(left_side, right_side, preferred_element_type=jnp.float32)  86.6 us
    unnamed x2, blocking collectives  84.7 us
    all_gather x1, waiting for transfers between devices, local(): lax.all_gather(down_weight, ('dp', 'seq'), axis=0, tiled=True)  54 us
    shift_right_arithmetic x27, local copies, waits for them, and re-layouts, unpack_keep(): nibble = jnp.right_shift(packed_words[..., None], shifts) & 7  48.9 us
    unnamed x235, local copies, waits for them, and re-layouts  28.4 us
  transfers between devices with their start and end apart: 12, of which 7 were waited for; matrix products, arithmetic and copies ran while one was open for 24% of the time, Pallas kernels for 0%

commit v1 on v0

v1 whole, which is shorter than its diff:
```python
import functools

import jax
import jax.numpy as jnp
from jax import lax
from jax.experimental import pallas as pl
from jax.experimental.pallas import tpu as pltpu
from jax.sharding import Mesh
from jax.sharding import PartitionSpec as P

H = 12
MICRO = 2
epsilon = 1e-12
keep_scale = 8.0 / 7.0
root_half = 0.7071067811865476
inverse_root_tau = 0.3989422804014327
f32 = jnp.float32
bf16 = jnp.bfloat16
ANY = pl.BlockSpec(memory_space=pl.ANY)


def matmul(left_side, right_side):
    return jnp.dot(left_side, right_side, preferred_element_type=f32)


def matmul_t(left_side, right_side):
    return lax.dot_general(left_side, right_side, (((1,), (1,)), ((), ())), preferred_element_type=f32)


def t_matmul(left_side, right_side):
    return lax.dot_general(left_side, right_side, (((0,), (0,)), ((), ())), preferred_element_type=f32)


def pp(value, axis, step=1):
    size = lax.axis_size(axis)
    return lax.ppermute(value, axis, [(i, i ^ step) for i in range(size)])


def pick(value, axis, index):
    return lax.dynamic_index_in_dim(value, index, axis, keepdims=False)


def swap_if(flag, value, axis):
    low = lax.slice_in_dim(value, 0, 1, axis=axis)
    high = lax.slice_in_dim(value, 1, 2, axis=axis)
    return jnp.where(flag, lax.concatenate([high, low], axis), value)


def gather_z(shard):
    if lax.axis_size("z") != 4:
        return lax.all_gather(shard, "z", axis=0)
    z = lax.axis_index("z")
    parts = [shard] + [pp(shard, "z", k) for k in (1, 2, 3)]
    square = jnp.stack(parts).reshape((2, 2) + shard.shape)
    square = swap_if((z & 1) == 1, square, 1)
    square = swap_if((z & 2) == 2, square, 0)
    return square.reshape((4,) + shard.shape)


def gather_pieces(shard, order):
    own = gather_z(shard)
    across_x = pp(own, "x")
    across_y = pp(own, "y")
    if order == "xy":
        corner = pp(across_x, "y")
    else:
        corner = pp(across_y, "x")
    here = (own, across_x, across_y, corner)
    return here + tuple(pp(piece, "seq") for piece in here)


def assemble_body(plan, ids, *refs):
    pieces, outs, sem = refs[:8], refs[8:-1], refs[-1]
    copies = []
    for number, piece in enumerate(pieces):
        c = ids[0] ^ (number >> 2)
        y = ids[1] ^ ((number >> 1) & 1)
        x = ids[2] ^ (number & 1)
        for start, rows, out, column in plan:
            src = piece.at[:, pl.ds(start, rows), :]
            dst = outs[out].at[:, y, x, c, :, pl.ds(column, 768)]
            copies.append(pltpu.make_async_copy(src, dst, sem.at[len(copies)]))
    for copy in copies:
        copy.start()
    for copy in copies:
        copy.wait()


def assemble(pieces, plan, shapes):
    depth, height, width = pieces[0].shape
    if all(start % 8 == 0 and rows % 8 == 0 for start, rows, _, _ in plan):
        ids = jnp.stack([lax.axis_index("seq"), lax.axis_index("y"), lax.axis_index("x")]).astype(jnp.int32)
        return pl.pallas_call(
            functools.partial(assemble_body, plan),
            grid_spec=pltpu.PrefetchScalarGridSpec(
                num_scalar_prefetch=1,
                grid=(1,),
                in_specs=[ANY] * 8,
                out_specs=[pl.BlockSpec(memory_space=pltpu.VMEM)] * len(shapes),
                scratch_shapes=[pltpu.SemaphoreType.DMA((8 * len(plan),))],
            ),
            out_shape=[
                jax.ShapeDtypeStruct((depth, 2, 2, 2, rows, columns), bf16) for rows, columns in shapes
            ],
        )(ids, *pieces)
    whole = jnp.stack(pieces).reshape((2, 2, 2) + pieces[0].shape)
    whole = swap_if(lax.axis_index("seq") == 1, whole, 0)
    whole = swap_if(lax.axis_index("y") == 1, whole, 1)
    whole = swap_if(lax.axis_index("x") == 1, whole, 2)
    whole = whole.transpose(3, 1, 2, 0, 4, 5)
    outs = []
    for number in range(len(shapes)):
        chosen = [(column, start, rows) for start, rows, out, column in plan if out == number]
        outs.append(
            jnp.concatenate([whole[..., start : start + rows, :] for _, start, rows in sorted(chosen)], axis=-1)
        )
    return outs


def add_up(*terms):
    total = terms[0].astype(f32)
    for term in terms[1:]:
        total = total + term.astype(f32)
    return total


def reduce_core(partial):
    c = lax.axis_index("seq")
    received = pp(pick(partial, 3, 1 - c), "seq")
    return add_up(pick(partial, 3, c), received).astype(bf16)


def reduce_z(partial):
    if lax.axis_size("z") != 4:
        return lax.psum_scatter(partial, "z", scatter_dimension=0, tiled=False).astype(f32)
    z = lax.axis_index("z")
    received = [pp(pick(partial, 0, z ^ k), "z", k) for k in (1, 2, 3)]
    return add_up(pick(partial, 0, z), *received)


def reduce_scatter(partial, order):
    y, x = lax.axis_index("y"), lax.axis_index("x")
    partial = reduce_core(partial)
    if order == "xy":
        received = pp(pick(partial, 2, 1 - x), "x")
        partial = add_up(pick(partial, 2, x), received).astype(bf16)
        received = pp(pick(partial, 1, 1 - y), "y")
        partial = add_up(pick(partial, 1, y), received).astype(bf16)
    else:
        received = pp(pick(partial, 1, 1 - y), "y")
        partial = add_up(pick(partial, 1, y), received).astype(bf16)
        received = pp(pick(partial, 1, 1 - x), "x")
        partial = add_up(pick(partial, 1, x), received).astype(bf16)
    return reduce_z(partial)


def lane_half(shape):
    return lax.broadcasted_iota(jnp.int32, shape, len(shape) - 1) < 64


def join_keys(core, near, far, buffer):
    for i in range(4):
        buffer[pl.ds(pl.multiple_of(i * 128 + core * 64, 64), 64), :] = near[0, i * 64 : (i + 1) * 64, :]
        buffer[pl.ds(pl.multiple_of(i * 128 + (1 - core) * 64, 64), 64), :] = far[0, i * 64 : (i + 1) * 64, :]


def attention_body(ids, q, k_near, v_near, k_far, v_far, words, context, signed, keys, values):
    core = ids[0]
    join_keys(core, k_near, k_far, keys)
    join_keys(core, v_near, v_far, values)
    queries = q[0]
    left = lane_half(queries.shape)
    zero = jnp.zeros_like(queries)
    outs = []
    for h in range(2):
        masked = jnp.where(left if h == 0 else ~left, queries, zero) * 0.125
        scores = lax.dot_general(masked, keys[...], (((1,), (1,)), ((), ())), preferred_element_type=f32)
        blocks = [scores[:, i * 128 : (i + 1) * 128] for i in range(4)]
        peak = jnp.maximum(jnp.maximum(blocks[0], blocks[1]), jnp.maximum(blocks[2], blocks[3]))
        peak = jnp.max(peak, axis=1, keepdims=True)
        blocks = [jnp.exp(block - peak) for block in blocks]
        total = jnp.sum((blocks[0] + blocks[1]) + (blocks[2] + blocks[3]), axis=1, keepdims=True)
        scale = 1.0 / total
        word = words[0, 0, h]
        dropped = []
        for i in range(4):
            weight = blocks[i] * scale
            keep = (word & (7 << (3 * i))) != 0
            weight = jnp.where(keep, weight, -weight).astype(bf16)
            signed[0, 0, h, i] = weight
            dropped.append(jnp.maximum(weight, jnp.zeros_like(weight)))
        outs.append(
            jnp.dot(jnp.concatenate(dropped, axis=1), values[...], preferred_element_type=f32) * keep_scale
        )
    context[0] = jnp.where(left, outs[0], outs[1]).astype(bf16)


def attention(ids, queries, near, far, words):
    micro, tokens, width = queries.shape
    pairs = width // 128
    qkv = lambda offset: pl.BlockSpec((1, tokens, 128), lambda m, p, ids, offset=offset: (m, 0, p + offset))
    return pl.pallas_call(
        attention_body,
        grid_spec=pltpu.PrefetchScalarGridSpec(
            num_scalar_prefetch=1,
            grid=(micro, pairs),
            in_specs=[
                qkv(0),
                qkv(0),
                qkv(pairs),
                qkv(0),
                qkv(pairs),
                pl.BlockSpec((1, 1, 2, tokens, 128), lambda m, p, ids: (m, 0, p, 0, 0)),
            ],
            out_specs=[
                qkv(0),
                pl.BlockSpec((1, 1, 2, 4, tokens, 128), lambda m, p, ids: (m, p, 0, 0, 0, 0)),
            ],
            scratch_shapes=[pltpu.VMEM((512, 128), bf16), pltpu.VMEM((512, 128), bf16)],
        ),
        out_shape=[
            jax.ShapeDtypeStruct((micro, tokens, width), bf16),
            jax.ShapeDtypeStruct((micro, pairs, 2, 4, tokens, 128), bf16),
        ],
        cost_estimate=pl.CostEstimate(flops=4 * 10**9, bytes_accessed=12 * 10**6, transcendentals=3 * 10**6),
        name="attention",
    )(ids, queries, near, near, far, far, words)


def attention_back_body(
    ids, q, k_near, v_near, k_far, v_far, signed, upstream, g_q, g_near, g_far, keys, values, sums
):
    core = ids[0]
    join_keys(core, k_near, k_far, keys)
    join_keys(core, v_near, v_far, values)
    queries = q[0]
    above = upstream[0]
    left = lane_half(queries.shape)
    left_long = lane_half((512, 128))
    zero = jnp.zeros_like(queries)
    grads = []
    for h in range(2):
        masked = jnp.where(left if h == 0 else ~left, above, zero)
        g_dropped = lax.dot_general(masked, values[...], (((1,), (1,)), ((), ())), preferred_element_type=f32)
        weights, kept, g_weights = [], [], []
        delta = None
        for i in range(4):
            both = signed[0, 0, h, i].astype(f32)
            weight = jnp.abs(both)
            g_weight = jnp.where(both > 0.0, g_dropped[:, i * 128 : (i + 1) * 128], 0.0)
            term = g_weight * weight
            delta = term if delta is None else delta + term
            weights.append(weight)
            g_weights.append(g_weight)
            kept.append(jnp.maximum(both, 0.0).astype(bf16))
        delta = jnp.sum(delta, axis=1, keepdims=True)
        g_scores = jnp.concatenate(
            [(weights[i] * (g_weights[i] - delta)).astype(bf16) for i in range(4)], axis=1
        )
        dropped = jnp.concatenate(kept, axis=1)
        grads.append(
            (
                jnp.dot(g_scores, keys[...], preferred_element_type=f32),
                t_matmul(g_scores, queries),
                t_matmul(dropped, above),
            )
        )
    g_q[0] = (jnp.where(left, grads[0][0], grads[1][0]) * (0.125 * keep_scale)).astype(bf16)
    for kind, factor in ((0, 0.125 * keep_scale), (1, keep_scale)):
        sums[...] = jnp.where(left_long, grads[0][kind + 1], grads[1][kind + 1]) * factor
        for i in range(4):
            g_near[0, kind, i * 64 : (i + 1) * 64, :] = sums[
                pl.ds(pl.multiple_of(i * 128 + core * 64, 64), 64), :
            ]
            g_far[0, kind, i * 64 : (i + 1) * 64, :] = sums[
                pl.ds(pl.multiple_of(i * 128 + (1 - core) * 64, 64), 64), :
            ].astype(bf16)


def attention_back(ids, queries, near, far, signed, upstream):
    micro, tokens, width = queries.shape
    pairs = width // 128
    qkv = lambda offset: pl.BlockSpec((1, tokens, 128), lambda m, p, ids, offset=offset: (m, 0, p + offset))
    both = pl.BlockSpec((1, 2, tokens, 128), lambda m, p, ids: (m, 0, 0, p))
    return pl.pallas_call(
        attention_back_body,
        grid_spec=pltpu.PrefetchScalarGridSpec(
            num_scalar_prefetch=1,
            grid=(micro, pairs),
            in_specs=[
                qkv(0),
                qkv(0),
                qkv(pairs),
                qkv(0),
                qkv(pairs),
                pl.BlockSpec((1, 1, 2, 4, tokens, 128), lambda m, p, ids: (m, p, 0, 0, 0, 0)),
                qkv(0),
            ],
            out_specs=[qkv(0), both, both],
            scratch_shapes=[
                pltpu.VMEM((512, 128), bf16),
                pltpu.VMEM((512, 128), bf16),
                pltpu.VMEM((512, 128), f32),
            ],
        ),
        out_shape=[
            jax.ShapeDtypeStruct((micro, tokens, width), bf16),
            jax.ShapeDtypeStruct((micro, 2, tokens, width), f32),
            jax.ShapeDtypeStruct((micro, 2, tokens, width), bf16),
        ],
        cost_estimate=pl.CostEstimate(flops=8 * 10**9, bytes_accessed=20 * 10**6, transcendentals=0),
        name="attention_back",
    )(ids, queries, near, near, far, far, signed, upstream)


def unpack_keep(packed_words):
    shifts = jnp.arange(4, dtype=jnp.int32) * 3
    nibble = jnp.right_shift(packed_words[..., None], shifts) & 7
    keep_value = (nibble >= 1).astype(f32) * keep_scale
    return keep_value.reshape(packed_words.shape[:-1] + (packed_words.shape[-1] * 4,))


def normalize(values, norm_gain, norm_shift):
    centred = values - jnp.mean(values, axis=-1, keepdims=True)
    inverse = lax.rsqrt(jnp.mean(centred * centred, axis=-1, keepdims=True) + epsilon)
    scaled = centred * inverse
    return (scaled * norm_gain + norm_shift, scaled, inverse)


def norm_back(upstream, scaled, inverse, norm_gain):
    weighted = upstream * norm_gain
    centre_term = jnp.mean(weighted, axis=-1, keepdims=True)
    slope_term = jnp.mean(weighted * scaled, axis=-1, keepdims=True)
    return inverse * (weighted - centre_term - scaled * slope_term)


def gelu_slope(inner_sum):
    normal_cdf = 0.5 * (1.0 + lax.erf(inner_sum * root_half))
    density = jnp.exp(-0.5 * inner_sum * inner_sum) * inverse_root_tau
    return normal_cdf + inner_sum * density


def local(
    hidden_in,
    cotangent,
    attention_keep,
    output_keep,
    feed_keep,
    qkv_weight,
    qkv_bias,
    out_weight,
    out_bias,
    first_gain,
    first_shift,
    up_weight,
    up_bias,
    down_weight,
    down_bias,
    second_gain,
    second_shift,
):
    micro, _, tokens, width = hidden_in.shape
    rows = micro * tokens
    own = qkv_weight.shape[0]
    depth = lax.axis_size("z")
    devices = depth * 8
    wide = up_weight.shape[1] // width
    ids = lax.axis_index("seq").astype(jnp.int32).reshape(1)

    bias_parts = (
        qkv_bias, out_bias, first_gain, first_shift, up_bias, down_bias, second_gain, second_shift
    )
    bias_row = jnp.concatenate(bias_parts)
    bias_block = jnp.zeros((8, width), bf16).at[0, : bias_row.shape[0]].set(bias_row)
    qkv_shard = jnp.concatenate([qkv_weight[:, i * width : (i + 1) * width] for i in range(3)] + [bias_block])
    up_shard = jnp.concatenate(
        [out_weight] + [up_weight[:, i * width : (i + 1) * width] for i in range(wide)]
    )
    qkv_pieces = gather_pieces(qkv_shard, "xy")
    up_pieces = gather_pieces(up_shard, "yx")
    down_pieces = gather_pieces(down_weight, "xy")

    q_w, k_w, v_w, bias_all = assemble(
        qkv_pieces,
        [(i * own, own, i, 0) for i in range(3)] + [(3 * own, 8, 3, 0)],
        [(own, width)] * 3 + [(8, width)],
    )
    out_w, up_w = assemble(
        up_pieces,
        [(0, own, 0, 0)] + [((i + 1) * own, own, 1, i * width) for i in range(wide)],
        [(own, width), (own, wide * width)],
    )
    (down_w,) = assemble(
        down_pieces, [(0, down_weight.shape[0], 0, 0)], [(down_weight.shape[0], width)]
    )
    q_w, k_w, v_w, out_w = (w.reshape(width, width) for w in (q_w, k_w, v_w, out_w))
    up_w = up_w.reshape(width, wide * width)
    down_w = down_w.reshape(wide * width, width)
    bias_all = bias_all.reshape(devices, 8, width)[:, 0]
    vectors, start = [], 0
    for part in bias_parts:
        vectors.append(bias_all[:, start : start + part.shape[0]].reshape(-1).astype(f32))
        start += part.shape[0]
    qkv_b, out_b, gain_one, shift_one, up_b, down_b, gain_two, shift_two = vectors

    hidden = hidden_in.reshape(rows, width)
    turned = hidden_in.reshape(micro, tokens // 4, 4, width).transpose(0, 2, 1, 3).reshape(rows, width)
    queries = (matmul(hidden, q_w) + qkv_b[:width]).astype(bf16).reshape(micro, tokens, width)
    keys = matmul(turned, k_w).astype(bf16)
    values = (matmul(turned, v_w) + qkv_b[width:]).astype(bf16)
    near = jnp.concatenate([keys, values], axis=1).reshape(micro, tokens, 2 * width)
    far = pp(near, "seq")
    context, signed = attention(ids, queries, near, far, attention_keep.reshape(micro, 1, H, tokens, -1))
    context = context.reshape(rows, width)

    attended = matmul(context, out_w) + out_b
    keep_output = unpack_keep(output_keep).reshape(rows, width)
    first_sum = hidden.astype(f32) + attended * keep_output
    normed, scaled_one, inverse_one = normalize(first_sum, gain_one, shift_one)
    normed_low = normed.astype(bf16)
    inner_sum = matmul(normed_low, up_w) + up_b
    activated = jax.nn.gelu(inner_sum, approximate=False).astype(bf16)
    outer_sum = matmul(activated, down_w) + down_b
    keep_feed = unpack_keep(feed_keep).reshape(rows, width)
    second_sum = normed + outer_sum * keep_feed
    result, scaled_two, inverse_two = normalize(second_sum, gain_two, shift_two)
    layer_out = result.astype(bf16).reshape(hidden_in.shape)

    upstream = cotangent.reshape(rows, width).astype(f32)
    g_second = norm_back(upstream, scaled_two, inverse_two, gain_two)
    grad_gain_two = jnp.sum(upstream * scaled_two, axis=0)
    grad_shift_two = jnp.sum(upstream, axis=0)
    g_outer = (g_second * keep_feed).astype(bf16)
    grad_down_b = jnp.sum(g_outer.astype(f32), axis=0)
    block = (depth, 2, 2, 2)
    grad_down = t_matmul(activated, g_outer).astype(bf16).reshape(block + (-1, width))
    grad_down = reduce_scatter(grad_down, "xy")
    g_inner = (matmul_t(g_outer, down_w) * gelu_slope(inner_sum)).astype(bf16)
    grad_up_b = jnp.sum(g_inner.astype(f32), axis=0)
    grad_up = t_matmul(normed_low, g_inner).astype(bf16)
    g_normed = g_second + matmul_t(g_inner, up_w)
    g_first = norm_back(g_normed, scaled_one, inverse_one, gain_one)
    grad_gain_one = jnp.sum(g_normed * scaled_one, axis=0)
    grad_shift_one = jnp.sum(g_normed, axis=0)
    g_attended = (g_first * keep_output).astype(bf16)
    grad_out_b = jnp.sum(g_attended.astype(f32), axis=0)
    grad_out = t_matmul(context, g_attended).astype(bf16)
    mid = jnp.concatenate(
        [grad_out.reshape(block + (own, width))]
        + [grad_up[:, i * width : (i + 1) * width].reshape(block + (own, width)) for i in range(wide)],
        axis=4,
    )
    mid = reduce_scatter(mid, "yx")
    grad_out = mid[:own]
    grad_up = jnp.concatenate([mid[(i + 1) * own : (i + 2) * own] for i in range(wide)], axis=1)

    g_context = matmul_t(g_attended, out_w).astype(bf16).reshape(micro, tokens, width)
    g_q, g_near, g_far = attention_back(ids, queries, near, far, signed, g_context)
    g_kv = (g_near + pp(g_far, "seq").astype(f32)).astype(bf16)
    g_q = g_q.reshape(rows, width)
    g_k = g_kv[:, 0].reshape(rows, width)
    g_v = g_kv[:, 1].reshape(rows, width)
    grad_qkv_b = jnp.concatenate([jnp.sum(g_q.astype(f32), axis=0), jnp.sum(g_v.astype(f32), axis=0)])
    bias_grads = (
        grad_qkv_b, grad_out_b, grad_gain_one, grad_shift_one, grad_up_b, grad_down_b, grad_gain_two, grad_shift_two
    )
    bias_rows = jnp.concatenate([g.reshape(devices, -1) for g in bias_grads], axis=1)
    high = bias_rows.astype(bf16)
    pair = jnp.stack([high, (bias_rows - high.astype(f32)).astype(bf16)], axis=1)
    pair = jnp.pad(pair, ((0, 0), (0, 6), (0, width - pair.shape[2])))
    last = jnp.concatenate(
        [t_matmul(hidden, g_q).astype(bf16).reshape(block + (own, width))]
        + [t_matmul(turned, g).astype(bf16).reshape(block + (own, width)) for g in (g_k, g_v)]
        + [pair.reshape(block + (8, width))],
        axis=4,
    )
    last = reduce_scatter(last, "xy")
    grad_qkv = jnp.concatenate([last[i * own : (i + 1) * own] for i in range(3)], axis=1)
    bias_sums = last[3 * own] + last[3 * own + 1]
    vector_grads, start = [], 0
    for part in bias_parts:
        vector_grads.append(bias_sums[start : start + part.shape[0]])
        start += part.shape[0]

    back = g_kv.reshape(micro, 2, 4, tokens // 4, width).transpose(0, 3, 2, 1, 4).reshape(rows, 2, width)
    grad_in = (
        g_first + matmul_t(g_q, q_w) + matmul_t(back[:, 0], k_w) + matmul_t(back[:, 1], v_w)
    ).astype(bf16).reshape(hidden_in.shape)
    return (
        layer_out,
        grad_in,
        grad_qkv,
        vector_grads[0],
        grad_out,
        vector_grads[1],
        vector_grads[2],
        vector_grads[3],
        grad_up,
        vector_grads[4],
        grad_down,
        vector_grads[5],
        vector_grads[6],
        vector_grads[7],
    )


def solution(mesh):
    groups, cores = mesh.devices.shape
    split = Mesh(mesh.devices.reshape(groups // 4, 2, 2, cores), ("z", "y", "x", "seq"))
    dp = ("z", "y", "x")
    every = ("z", "y", "x", "seq")
    tokens = P(None, dp, "seq", None)
    matrix = P(every, None)
    vector = P(every)
    params = (matrix, vector, matrix, vector, vector, vector, matrix, vector, matrix, vector, vector, vector)
    return jax.shard_map(
        local,
        mesh=split,
        in_specs=(tokens, tokens, P(None, dp, None, "seq", None), tokens, tokens) + params,
        out_specs=(tokens, tokens) + params,
        check_vma=False,
    )
```

time: 891 us -> 391 us (0.44)
  waiting for transfers between devices: 503 us -> 144 us
  blocking collectives: 96.7 us -> 0 us
  matrix products: 130 us -> 56.4 us
  starting transfers between devices: 1.06 us -> 61 us
  Pallas kernels: 0 us -> 49.6 us
  local copies, waits for them, and re-layouts: 93.9 us -> 48.2 us
  other arithmetic: 39.9 us -> 23.2 us
  between operations: 15.8 us -> 2.15 us
    reduce_scatter x7 -> x0, waiting for transfers between devices: 301 us -> none  [the longest x1 142 us: local(): lax.psum_scatter(totals[8], ('dp', 'seq'), scatter_dimension=0, tiled=True)]
    ppermute x0 -> x50, waiting for transfers between devices: none -> 144 us  [pp(): return lax.ppermute(value, axis, [(i, i ^ step) for i in range(size)])]
    unnamed x13 -> x0, waiting for transfers between devices: 128 us -> none
    unnamed x2 -> x0, blocking collectives: 84.7 us -> none
    all_gather x4 -> x0, waiting for transfers between devices: 74.1 us -> none  [the longest x1 54 us: local(): lax.all_gather(down_weight, ('dp', 'seq'), axis=0, tiled=True)]
    dot_general x36 -> x18, matrix products: 130 us -> 56.4 us  [the longest x6 28.2 us: matmul(): return jnp.dot(left_side, right_side, preferred_element_type=f32)]
    ppermute x0 -> x50, starting transfers between devices: none -> 61 us  [pp(): return lax.ppermute(value, axis, [(i, i ^ step) for i in range(size)])]
    pallas_call x0 -> x5, Pallas kernels: none -> 49.6 us  [the longest x1 17.6 us: attention_back(): pl.pallas_call(attention_back_body, grid_spec=pltpu.PrefetchScalarGridSpe...]
  transfers between devices with their start and end apart: 12 -> 50, of which waited for: 7 -> 20; matrix products, arithmetic and copies ran while one was open for 24% -> 18% of each run, Pallas kernels for 0% -> 4%
where the time goes in v1:
time: 391 us; the launch traced here: 385 us
  waiting for transfers between devices  144 us (37%)
  starting transfers between devices  61 us (16%)
  matrix products  56.4 us (14%)
  Pallas kernels  49.6 us (13%)
  local copies, waits for them, and re-layouts  48.2 us (12%)
  other arithmetic  23.2 us (6%)
    ppermute x50, waiting for transfers between devices, pp(): return lax.ppermute(value, axis, [(i, i ^ step) for i in range(size)])  144 us
    ppermute x50, starting transfers between devices, pp(): return lax.ppermute(value, axis, [(i, i ^ step) for i in range(size)])  61 us
    dot_general x6, matrix products, matmul(): return jnp.dot(left_side, right_side, preferred_element_type=f32)  28.2 us
    pallas_call x1, Pallas kernels, attention_back(): pl.pallas_call(attention_back_body, grid_spec=pltpu.PrefetchScalarGridSpe...  17.6 us
    pallas_call x3, Pallas kernels, assemble(): pl.pallas_call(functools.partial(assemble_body, plan), grid_spec=pltpu.Pr...  16.6 us
    unnamed x99, local copies, waits for them, and re-layouts  16 us
    pallas_call x1, Pallas kernels, attention(): pl.pallas_call(attention_body, grid_spec=pltpu.PrefetchScalarGridSpec(num...  15.4 us
    dot_general x6, matrix products, t_matmul(): lax.dot_general(left_side, right_side, (((0,), (0,)), ((), ())), preferre...  14.8 us
  transfers between devices with their start and end apart: 50, of which 20 were waited for; matrix products, arithmetic and copies ran while one was open for 18% of the time, Pallas kernels for 4%

profile of v1, /device:TPU:0, one launch (start us, length us, event | category | flops | bytes accessed | tf_op | source)
XLA Modules:
  0.0 384.6 jit_solution(6882847539560561920)
XLA Ops:
  0.6 5.4 %concatenate.100 = bf16[288]{0:T(512)(128)(2,1)S(1)} concatenate(bf16[48]{0:T(256)(128)(2,1)} %param.25, bf16[24]{0:T(256)(128)(2,1)} %param.27, bf16[24]{0:T(256)(128)(2,1)} %param.28, bf16[24]{0:T(256)(128)(2,1)} %param.29, bf16[96]{0:T(256)(128)(2,1)} %param.31, bf16[24]{0:T(256)(128)(2,1)} %param.33, bf16[24]{0:T(256)(128)(2,1)} %param.34, bf16[24]{0:T(256)(128)(2,1)} %param.35), dimensions={0} | concatenate | bytes 1152 | tf_op jit(solution)/shard_map/concatenate | solution.py:373
  6.9 5.1 %collective-permute-start.2 = (bf16[80,768]{1,0:T(8,128)(2,1)S(1)}, bf16[80,768]{1,0:T(8,128)(2,1)S(1)}, u32[]{:S(2)}, u32[]{:S(2)}) collective-permute-start(bf16[80,768]{1,0:T(8,128)(2,1)S(1)} %fusion.63), channel_id=1, source_target_pairs={{0,24},{8,16},{16,8},{24,0},{1,25},{9,17},{17,9},{25,1},{2,26},{10... | collective-permute-start | bytes 368648 | tf_op jit(solution)/shard_map/ppermute | solution.py:36
  16.5 3.7 collective-permute-start.13
  21.8 14.2 %collective-permute-done.1 = bf16[80,768]{1,0:T(8,128)(2,1)S(1)} collective-permute-done((bf16[80,768]{1,0:T(8,128)(2,1)S(1)}, bf16[80,768]{1,0:T(8,128)(2,1)S(1)}, u32[]{:S(2)}, u32[]{:S(2)}) %collective-permute-start.1) | collective-permute-done | bytes 122912 | tf_op jit(solution)/shard_map/ppermute | solution.py:36
  36.0 1.6 collective-permute-start.21
  38.1 11.1 %collective-permute-start.11 = (bf16[120,768]{1,0:T(8,128)(2,1)S(1)}, bf16[120,768]{1,0:T(8,128)(2,1)S(1)}, u32[]{:S(2)}, u32[]{:S(2)}) collective-permute-start(bf16[120,768]{1,0:T(8,128)(2,1)S(1)} %slice_dynamic-update-slice_fusion), channel_id=1, source_target_pairs={{0,8},{8,0},{16,24},{24,16},{1,9},{9,1},{17,25},{25,17},{2,10},{10... | collective-permute-start | bytes 552968 | tf_op jit(solution)/shard_map/ppermute | solution.py:36
  49.3 1.7 collective-permute-done.22
  55.1 8.2 %collective-permute-done.3.refs_1_ = bf16[4,80,768]{2,1,0:T(8,128)(2,1)S(1)} collective-permute-done((bf16[4,80,768]{2,1,0:T(8,128)(2,1)S(1)}, bf16[4,80,768]{2,1,0:T(8,128)(2,1)S(1)}, u32[]{:S(2)}, u32[]{:S(2)}) %collective-permute-start.3) | collective-permute-done | bytes 491552 | tf_op jit(solution)/shard_map/ppermute | solution.py:36
  69.4 8.0 %collective-permute-done.5.refs_3_ = bf16[4,80,768]{2,1,0:T(8,128)(2,1)} collective-permute-done((bf16[4,80,768]{2,1,0:T(8,128)(2,1)S(1)}, bf16[4,80,768]{2,1,0:T(8,128)(2,1)}, u32[]{:S(2)}, u32[]{:S(2)}) %collective-permute-start.5) | collective-permute-done | bytes 491552 | tf_op jit(solution)/shard_map/ppermute | solution.py:36
  82.0 11.2 %collective-permute-done.15.refs_2_ = bf16[4,120,768]{2,1,0:T(8,128)(2,1)} collective-permute-done((bf16[4,120,768]{2,1,0:T(8,128)(2,1)}, bf16[4,120,768]{2,1,0:T(8,128)(2,1)}, u32[]{:S(2)}, u32[]{:S(2)}) %collective-permute-start.15) | collective-permute-done | bytes 737312 | tf_op jit(solution)/shard_map/ppermute | solution.py:36
  96.8 5.0 %shard_map.272 = (bf16[4,2,2,2,24,768]{5,4,3,2,1,0:T(8,128)(2,1)}, bf16[4,2,2,2,24,768]{5,4,3,2,1,0:T(8,128)(2,1)}, bf16[4,2,2,2,24,768]{5,4,3,2,1,0:T(8,128)(2,1)}, bf16[4,2,2,2,8,768]{5,4,3,2,1,0:T(8,128)(2,1)}) custom-call(s32[3]{0:T(128)} %pad_add_fusion.ids, bf16[4,80,768]{2,1,0:T(8,128)(2,1)} %copy-done.6, bf16[4,80,768]{2,1,0:T(8,128)(2,1)} %copy-done.25, ...), custom_call_target="tpu_custom_call" | custom-call | tf_op jit(solution)/shard_map/pallas_call | solution.py:93
  103.1 2.2 fusion.35
  106.2 1.8 copy.76
  110.8 1.6 copy.80
  113.0 3.2 collective-permute-done.26.refs_3_
  116.2 2.0 and_compare_fusion.1
  120.4 7.9 %collective-permute-done.16.refs_3_ = bf16[4,120,768]{2,1,0:T(8,128)(2,1)} collective-permute-done((bf16[4,120,768]{2,1,0:T(8,128)(2,1)}, bf16[4,120,768]{2,1,0:T(8,128)(2,1)}, u32[]{:S(2)}, u32[]{:S(2)}) %collective-permute-start.16) | collective-permute-done | bytes 737312 | tf_op jit(solution)/shard_map/ppermute | solution.py:36
  130.1 3.2 add_convert_fusion.4
  133.3 5.2 %shard_map.274 = bf16[4,2,2,2,96,768]{5,4,3,2,1,0:T(8,128)(2,1)} custom-call(s32[3]{0:T(128)} %pad_add_fusion.ids, bf16[4,96,768]{2,1,0:T(8,128)(2,1)} %fusion.53.refs_0_, bf16[4,96,768]{2,1,0:T(8,128)(2,1)} %collective-permute-done.24.refs_1_, bf16[4,96,768]{2,1,0:T(8,128)(2,1)} %copy-done.21, bf16[4,96,768]{2,1,0:T(8,128)(2,1)} %collective-permute-done.26.refs_3_, ...), custom_call_target="tpu_custom_call" | custom-call | tf_op jit(solution)/shard_map/pallas_call | solution.py:93
  139.6 6.3 %shard_map.273 = (bf16[4,2,2,2,24,768]{5,4,3,2,1,0:T(8,128)(2,1)}, bf16[4,2,2,2,24,3072]{5,4,3,2,1,0:T(8,128)(2,1)}) custom-call(s32[3]{0:T(128)} %pad_add_fusion.ids, bf16[4,120,768]{2,1,0:T(8,128)(2,1)} %fusion.50.refs_0_, bf16[4,120,768]{2,1,0:T(8,128)(2,1)} %collective-permute-done.14.refs_1_, bf16[4,120,768]{2,1,0:T(8,128)(2,1)} %collective-permute-done.15.refs_2_, ...), custom_call_target="tpu_custom_call" | custom-call | tf_op jit(solution)/shard_map/pallas_call | solution.py:93
  146.0 15.4 %attention.1 = (bf16[2,256,768]{2,1,0:T(8,128)(2,1)}, bf16[2,6,2,4,256,128]{5,4,3,2,1,0:T(8,128)(2,1)}) custom-call(s32[1]{0:T(128)} %bitcast.1.ids, bf16[2,256,768]{2,1,0:T(8,128)(2,1)} %bitcast.353, bf16[2,256,1536]{2,1,0:T(8,128)(2,1)} %bitcast.23.k_near.v_near, bf16[2,256,1536]{2,1,0:T(8,128)(2,1)} %bitcast.23.k_near.v_near, ...), custom_call_target="tpu_custom_call" | custom-call | flops 4000000000 | bytes 12000000 | tf_op jit(solution)/shard_map/attention/pallas_call | solution.py:202
  161.4 2.8 fusion.84
  164.6 16.2 %fusion.2 = (bf16[512,3072]{1,0:T(8,128)(2,1)S(1)}, f32[512,3072]{1,0:T(8,128)S(1)}) fusion(f32[3072]{0:T(1024)S(1)} %reshape.667, bf16[768,3072]{1,0:T(8,128)(2,1)S(1)} %bitcast.345, f32[512,768]{1,0:T(8,128)S(1)} %get-tuple-element.175, f32[768]{0:T(1024)S(1)} %reshape.666, f32[768]{0:T(1024)S(1)} %reshape.665, f32[512]{0:T(512)S(1)} %add_rsqrt_fusion.1, ...), kind=kOutput, calls=%fused_computation.4 | convolution fusion | flops 2521694208 | bytes 15751168 | tf_op jit(solution)/shard_map/dot_general | solution.py:23
  180.8 3.0 fusion.85
  184.9 1.8 convert_reduce_fusion.2
  186.6 4.8 %convert_reduce_fusion = (f32[3072]{0:T(1024)S(1)}, bf16[512,3072]{1,0:T(8,128)(2,1)S(1)}) fusion(f32[512,3072]{1,0:T(8,128)S(1)} %get-tuple-element.177, f32[3072]{0:T(1024)S(1)} %reshape.667, bf16[512,768]{1,0:T(8,128)(2,1)S(1)} %get-tuple-element.99, bf16[3072,768]{1,0:T(8,128)(2,1)S(1)} %bitcast.283), kind=kOutput, calls=%fused_computation.11 | convolution fusion | flops 2436363264 | bytes 14966784 | tf_op jit(solution)/shard_map/dot_general | solution.py:27
  191.5 3.1 multiply_reduce_fusion
  196.5 1.7 convolution_convert_fusion.6
  198.2 1.9 convolution_convert_fusion.2
  200.1 4.8 %convolution_convert_fusion.1 = bf16[768,3072]{1,0:T(8,128)(2,1)} fusion(bf16[512,3072]{1,0:T(8,128)(2,1)S(1)} %get-tuple-element.182, f32[512,768]{1,0:T(8,128)S(1)} %get-tuple-element.175, f32[768]{0:T(1024)S(1)} %reshape.666, f32[768]{0:T(1024)S(1)} %reshape.665, f32[512]{0:T(512)S(1)} %add_rsqrt_fusion.1, f32[512]{0:T(512)S(1)} %broadcast_multiply_fusion.4), kind=kOutput, calls=%fused_computation.30 | convolution fusion | flops 2420244480 | bytes 9447424 | tf_op jit(solution)/shard_map/dot_general | solution.py:31
  204.8 17.6 %attention_back.1 = (bf16[2,256,768]{2,1,0:T(8,128)(2,1)}, f32[2,2,256,768]{3,2,1,0:T(8,128)}, bf16[2,2,256,768]{3,2,1,0:T(8,128)(2,1)}) custom-call(s32[1]{0:T(128)} %bitcast.1.ids, bf16[2,256,768]{2,1,0:T(8,128)(2,1)} %bitcast.354, bf16[2,256,1536]{2,1,0:T(8,128)(2,1)} %bitcast.23.k_near.v_near, bf16[2,256,1536]{2,1,0:T(8,128)(2,1)} %bitcast.23.k_near.v_near, ...), custom_call_target="tpu_custom_call" | custom-call | flops 8000000000 | bytes 20000000 | tf_op jit(solution)/shard_map/attention_back/pallas_call | solution.py:285
  225.7 2.7 fusion.70
  228.8 2.0 constant_dynamic-slice_fusion.3
  230.8 1.8 copy.135
  234.0 3.1 convolution_convert_fusion
  237.1 1.7 constant_dynamic-slice_fusion.1
  240.9 1.9 convolution_convert_fusion.5
  243.9 1.9 add_convert_fusion
  248.0 2.3 convolution_convert_fusion.3
  254.5 1.6 copy.81
  256.2 2.5 fusion.72
  258.7 2.4 fusion.17
  261.1 1.6 collective-permute-start.45
  264.5 2.5 fusion.16
  268.8 21.2 %collective-permute-done.45 = bf16[4,2,96,768]{3,2,0,1:T(8,128)(2,1)S(1)} collective-permute-done((bf16[4,2,96,768]{3,2,0,1:T(8,128)(2,1)S(1)}, bf16[4,2,96,768]{3,2,0,1:T(8,128)(2,1)S(1)}, u32[]{:S(2)}, u32[]{:S(2)}) %collective-permute-start.45) | collective-permute-done | bytes 1179680 | tf_op jit(solution)/shard_map/ppermute | solution.py:36
  290.4 1.6 collective-permute-start.46
  292.6 2.0 add_convert_fusion.1
  294.7 12.0 %collective-permute-done.46 = bf16[4,96,768]{2,1,0:T(8,128)(2,1)S(1)} collective-permute-done((bf16[4,96,768]{2,1,0:T(8,128)(2,1)S(1)}, bf16[4,96,768]{2,1,0:T(8,128)(2,1)S(1)}, u32[]{:S(2)}, u32[]{:S(2)}) %collective-permute-start.46) | collective-permute-done | bytes 589856 | tf_op jit(solution)/shard_map/ppermute | solution.py:36
  306.9 2.3 collective-permute-start.49
  309.2 2.2 collective-permute-start.47
  311.7 1.6 collective-permute-start.34
  314.4 4.5 %collective-permute-done.48 = bf16[96,768]{1,0:T(8,128)(2,1)S(1)} collective-permute-done((bf16[96,768]{1,0:T(8,128)(2,1)S(1)}, bf16[96,768]{1,0:T(8,128)(2,1)S(1)}, u32[]{:S(2)}, u32[]{:S(2)}) %collective-permute-start.48) | collective-permute-done | bytes 147488 | tf_op jit(solution)/shard_map/ppermute | solution.py:36
  319.7 18.6 %collective-permute-done.39 = bf16[4,2,120,768]{3,2,0,1:T(8,128)(2,1)S(1)} collective-permute-done((bf16[4,2,120,768]{3,2,0,1:T(8,128)(2,1)S(1)}, bf16[4,2,120,768]{3,2,0,1:T(8,128)(2,1)S(1)}, u32[]{:S(2)}, u32[]{:S(2)}) %collective-permute-start.39) | collective-permute-done | bytes 1474592 | tf_op jit(solution)/shard_map/ppermute | solution.py:36
  338.7 8.3 %collective-permute-done.34 = bf16[4,80,768]{2,1,0:T(8,128)(2,1)S(1)} collective-permute-done((bf16[4,80,768]{2,1,0:T(8,128)(2,1)S(1)}, bf16[4,80,768]{2,1,0:T(8,128)(2,1)S(1)}, u32[]{:S(2)}, u32[]{:S(2)}) %collective-permute-start.34) | collective-permute-done | bytes 491552 | tf_op jit(solution)/shard_map/ppermute | solution.py:36
  347.2 2.3 collective-permute-start.37
  349.5 2.1 collective-permute-start.35
  351.7 1.6 collective-permute-start.40
  353.3 1.9 collective-permute-done.37
  355.3 3.8 collective-permute-done.36
  361.0 6.7 %collective-permute-done.40 = bf16[4,120,768]{2,1,0:T(8,128)(2,1)S(1)} collective-permute-done((bf16[4,120,768]{2,1,0:T(8,128)(2,1)S(1)}, bf16[4,120,768]{2,1,0:T(8,128)(2,1)S(1)}, u32[]{:S(2)}, u32[]{:S(2)}) %collective-permute-start.40) | collective-permute-done | bytes 737312 | tf_op jit(solution)/shard_map/ppermute | solution.py:36
  367.9 2.4 collective-permute-start.43
  370.3 2.1 collective-permute-start.41
  372.9 4.0 %collective-permute-done.43 = bf16[120,768]{1,0:T(8,128)(2,1)S(1)} collective-permute-done((bf16[120,768]{1,0:T(8,128)(2,1)S(1)}, bf16[120,768]{1,0:T(8,128)(2,1)S(1)}, u32[]{:S(2)}, u32[]{:S(2)}) %collective-permute-start.43) | collective-permute-done | bytes 184352 | tf_op jit(solution)/shard_map/ppermute | solution.py:36
  376.9 6.0 %collective-permute-done.42 = bf16[120,768]{1,0:T(8,128)(2,1)S(1)} collective-permute-done((bf16[120,768]{1,0:T(8,128)(2,1)S(1)}, bf16[120,768]{1,0:T(8,128)(2,1)S(1)}, u32[]{:S(2)}, u32[]{:S(2)}) %collective-permute-start.42) | collective-permute-done | bytes 184352 | tf_op jit(solution)/shard_map/ppermute | solution.py:36
  (279 shorter events, 65.5 us)
Async XLA Ops:
  6.9 13.4 %collective-permute-start.2 = (bf16[80,768]{1,0:T(8,128)(2,1)S(1)}, bf16[80,768]{1,0:T(8,128)(2,1)S(1)}, u32[]{:S(2)}, u32[]{:S(2)}) collective-permute-start(bf16[80,768]{1,0:T(8,128)(2,1)S(1)} %fusion.63), channel_id=1, source_target_pairs={{0,24},{8,16},{16,8},{24,0},{1,25},{9,17},{17,9},{25,1},{2,26},{10... | collective-permute-start | bytes 368648 | tf_op jit(solution)/shard_map/ppermute | solution.py:36
  12.0 24.0 %collective-permute-start.1 = (bf16[80,768]{1,0:T(8,128)(2,1)S(1)}, bf16[80,768]{1,0:T(8,128)(2,1)S(1)}, u32[]{:S(2)}, u32[]{:S(2)}) collective-permute-start(bf16[80,768]{1,0:T(8,128)(2,1)S(1)} %fusion.63), channel_id=1, source_target_pairs={{0,16},{8,24},{16,0},{24,8},{1,17},{9,25},{17,1},{25,9},{2,18},{10... | collective-permute-start | bytes 368648 | tf_op jit(solution)/shard_map/ppermute | solution.py:36
  12.0 24.0 %collective-permute-start = (bf16[80,768]{1,0:T(8,128)(2,1)S(1)}, bf16[80,768]{1,0:T(8,128)(2,1)S(1)}, u32[]{:S(2)}, u32[]{:S(2)}) collective-permute-start(bf16[80,768]{1,0:T(8,128)(2,1)S(1)} %fusion.63), channel_id=1, source_target_pairs={{0,8},{8,0},{16,24},{24,16},{1,9},{9,1},{17,25},{25,17},{2,10},{10... | collective-permute-start | bytes 368648 | tf_op jit(solution)/shard_map/ppermute | solution.py:36
  16.5 37.8 %collective-permute-start.13 = (bf16[120,768]{1,0:T(8,128)(2,1)S(1)}, bf16[120,768]{1,0:T(8,128)(2,1)S(1)}, u32[]{:S(2)}, u32[]{:S(2)}) collective-permute-start(bf16[120,768]{1,0:T(8,128)(2,1)S(1)} %slice_dynamic-update-slice_fusion), channel_id=1, source_target_pairs={{0,24},{8,16},{16,8},{24,0},{1,25},{9,17},{17,9},{25,1},{2,26},{10... | collective-permute-start | bytes 552968 | tf_op jit(solution)/shard_map/ppermute | solution.py:36
  20.3 34.2 %collective-permute-start.12 = (bf16[120,768]{1,0:T(8,128)(2,1)S(1)}, bf16[120,768]{1,0:T(8,128)(2,1)S(1)}, u32[]{:S(2)}, u32[]{:S(2)}) collective-permute-start(bf16[120,768]{1,0:T(8,128)(2,1)S(1)} %slice_dynamic-update-slice_fusion), channel_id=1, source_target_pairs={{0,16},{8,24},{16,0},{24,8},{1,17},{9,25},{17,1},{25,9},{2,18},{10... | collective-permute-start | bytes 552968 | tf_op jit(solution)/shard_map/ppermute | solution.py:36
  20.3 17.8 %collective-permute-start.23 = (bf16[96,768]{1,0:T(8,128)(2,1)}, bf16[96,768]{1,0:T(8,128)(2,1)S(1)}, u32[]{:S(2)}, u32[]{:S(2)}) collective-permute-start(bf16[96,768]{1,0:T(8,128)(2,1)} %param.32), channel_id=1, source_target_pairs={{0,24},{8,16},{16,8},{24,0},{1,25},{9,17},{17,9},{25,1},{2,26},{10... | collective-permute-start | bytes 442376 | tf_op jit(solution)/shard_map/ppermute | solution.py:36
  36.0 15.0 %collective-permute-start.22 = (bf16[96,768]{1,0:T(8,128)(2,1)}, bf16[96,768]{1,0:T(8,128)(2,1)S(1)}, u32[]{:S(2)}, u32[]{:S(2)}) collective-permute-start(bf16[96,768]{1,0:T(8,128)(2,1)} %param.32), channel_id=1, source_target_pairs={{0,16},{8,24},{16,0},{24,8},{1,17},{9,25},{17,1},{25,9},{2,18},{10... | collective-permute-start | bytes 442376 | tf_op jit(solution)/shard_map/ppermute | solution.py:36
  36.0 16.5 %collective-permute-start.21 = (bf16[96,768]{1,0:T(8,128)(2,1)}, bf16[96,768]{1,0:T(8,128)(2,1)S(1)}, u32[]{:S(2)}, u32[]{:S(2)}) collective-permute-start(bf16[96,768]{1,0:T(8,128)(2,1)} %param.32), channel_id=1, source_target_pairs={{0,8},{8,0},{16,24},{24,16},{1,9},{9,1},{17,25},{25,17},{2,10},{10... | collective-permute-start | bytes 442376 | tf_op jit(solution)/shard_map/ppermute | solution.py:36
  37.9 16.1 %copy-start.24 = (bf16[96,768]{1,0:T(8,128)(2,1)S(1)}, bf16[96,768]{1,0:T(8,128)(2,1)}, u32[]{:S(2)}) copy-start(bf16[96,768]{1,0:T(8,128)(2,1)} %param.32) | copy-start | bytes 442372
  38.1 16.2 %copy-start.6 = (bf16[4,80,768]{2,1,0:T(8,128)(2,1)}, bf16[4,80,768]{2,1,0:T(8,128)(2,1)S(1)}, u32[]{:S(2)}) copy-start(bf16[4,80,768]{2,1,0:T(8,128)(2,1)S(1)} %fusion.54.refs_0_) | copy-start | bytes 1474564
  38.1 16.5 %collective-permute-start.11 = (bf16[120,768]{1,0:T(8,128)(2,1)S(1)}, bf16[120,768]{1,0:T(8,128)(2,1)S(1)}, u32[]{:S(2)}, u32[]{:S(2)}) collective-permute-start(bf16[120,768]{1,0:T(8,128)(2,1)S(1)} %slice_dynamic-update-slice_fusion), channel_id=1, source_target_pairs={{0,8},{8,0},{16,24},{24,16},{1,9},{9,1},{17,25},{25,17},{2,10},{10... | collective-permute-start | bytes 552968 | tf_op jit(solution)/shard_map/ppermute | solution.py:36
  51.0 12.2 %collective-permute-start.3 = (bf16[4,80,768]{2,1,0:T(8,128)(2,1)S(1)}, bf16[4,80,768]{2,1,0:T(8,128)(2,1)S(1)}, u32[]{:S(2)}, u32[]{:S(2)}) collective-permute-start(bf16[4,80,768]{2,1,0:T(8,128)(2,1)S(1)} %fusion.54.refs_0_), channel_id=1, source_target_pairs={{0,2},{2,0},{1,3},{3,1},{4,6},{6,4},{5,7},{7,5},{8,10},{10,8},{9,1... | collective-permute-start | bytes 1474568 | tf_op jit(solution)/shard_map/ppermute | solution.py:36
  52.5 16.4 %collective-permute-start.4 = (bf16[4,80,768]{2,1,0:T(8,128)(2,1)S(1)}, bf16[4,80,768]{2,1,0:T(8,128)(2,1)S(1)}, u32[]{:S(2)}, u32[]{:S(2)}) collective-permute-start(bf16[4,80,768]{2,1,0:T(8,128)(2,1)S(1)} %fusion.54.refs_0_), channel_id=1, source_target_pairs={{0,4},{4,0},{1,5},{5,1},{2,6},{6,2},{3,7},{7,3},{8,12},{12,8},{9,1... | collective-permute-start | bytes 1474568 | tf_op jit(solution)/shard_map/ppermute | solution.py:36
  54.4 14.6 %collective-permute-start.6 = (bf16[4,80,768]{2,1,0:T(8,128)(2,1)S(1)}, bf16[4,80,768]{2,1,0:T(8,128)(2,1)S(1)}, u32[]{:S(2)}, u32[]{:S(2)}) collective-permute-start(bf16[4,80,768]{2,1,0:T(8,128)(2,1)S(1)} %fusion.54.refs_0_), channel_id=1, source_target_pairs={{0,1},{1,0},{2,3},{3,2},{4,5},{5,4},{6,7},{7,6},{8,9},{9,8},{10,11... | collective-permute-start | bytes 1474568 | tf_op jit(solution)/shard_map/ppermute | solution.py:36
  63.2 5.6 %copy-start.25 = (bf16[4,80,768]{2,1,0:T(8,128)(2,1)}, bf16[4,80,768]{2,1,0:T(8,128)(2,1)S(1)}, u32[]{:S(2)}) copy-start(bf16[4,80,768]{2,1,0:T(8,128)(2,1)S(1)} %collective-permute-done.3.refs_1_) | copy-start | bytes 1474564
  63.2 14.3 %collective-permute-start.5 = (bf16[4,80,768]{2,1,0:T(8,128)(2,1)S(1)}, bf16[4,80,768]{2,1,0:T(8,128)(2,1)}, u32[]{:S(2)}, u32[]{:S(2)}) collective-permute-start(bf16[4,80,768]{2,1,0:T(8,128)(2,1)S(1)} %collective-permute-done.3.refs_1_), channel_id=1, source_target_pairs={{0,4},{4,0},{1,5},{5,1},{2,6},{6,2},{3,7},{7,3},{8,12},{12,8},{9,1... | collective-permute-start | bytes 1474568 | tf_op jit(solution)/shard_map/ppermute | solution.py:36
  65.8 11.6 %copy-start.12 = (bf16[2,1,256,768]{3,2,1,0:T(8,128)(2,1)S(1)}, bf16[2,1,256,768]{3,2,1,0:T(8,128)(2,1)}, u32[]{:S(2)}) copy-start(bf16[2,1,256,768]{3,2,1,0:T(8,128)(2,1)} %param.19) | copy-start | bytes 2359300
  65.9 27.4 %collective-permute-start.15 = (bf16[4,120,768]{2,1,0:T(8,128)(2,1)}, bf16[4,120,768]{2,1,0:T(8,128)(2,1)}, u32[]{:S(2)}, u32[]{:S(2)}) collective-permute-start(bf16[4,120,768]{2,1,0:T(8,128)(2,1)} %fusion.50.refs_0_), channel_id=1, source_target_pairs={{0,4},{4,0},{1,5},{5,1},{2,6},{6,2},{3,7},{7,3},{8,12},{12,8},{9,1... | collective-permute-start | bytes 2211848 | tf_op jit(solution)/shard_map/ppermute | solution.py:36
  67.4 13.2 %collective-permute-start.24 = (bf16[4,96,768]{2,1,0:T(8,128)(2,1)}, bf16[4,96,768]{2,1,0:T(8,128)(2,1)}, u32[]{:S(2)}, u32[]{:S(2)}) collective-permute-start(bf16[4,96,768]{2,1,0:T(8,128)(2,1)} %fusion.53.refs_0_), channel_id=1, source_target_pairs={{0,2},{2,0},{1,3},{3,1},{4,6},{6,4},{5,7},{7,5},{8,10},{10,8},{9,1... | collective-permute-start | bytes 1769480 | tf_op jit(solution)/shard_map/ppermute | solution.py:36
  68.9 9.6 %copy-start.26 = (bf16[4,80,768]{2,1,0:T(8,128)(2,1)}, bf16[4,80,768]{2,1,0:T(8,128)(2,1)S(1)}, u32[]{:S(2)}) copy-start(bf16[4,80,768]{2,1,0:T(8,128)(2,1)S(1)} %collective-permute-done.4.refs_2_) | copy-start | bytes 1474564
  68.9 24.4 %collective-permute-start.7 = (bf16[4,80,768]{2,1,0:T(8,128)(2,1)S(1)}, bf16[4,80,768]{2,1,0:T(8,128)(2,1)}, u32[]{:S(2)}, u32[]{:S(2)}) collective-permute-start(bf16[4,80,768]{2,1,0:T(8,128)(2,1)S(1)} %collective-permute-done.3.refs_1_), channel_id=1, source_target_pairs={{0,1},{1,0},{2,3},{3,2},{4,5},{5,4},{6,7},{7,6},{8,9},{9,8},{10,11... | collective-permute-start | bytes 1474568 | tf_op jit(solution)/shard_map/ppermute | solution.py:36
  68.9 9.5 %copy-start.27 = (bf16[4,80,768]{2,1,0:T(8,128)(2,1)}, bf16[4,80,768]{2,1,0:T(8,128)(2,1)S(1)}, u32[]{:S(2)}) copy-start(bf16[4,80,768]{2,1,0:T(8,128)(2,1)S(1)} %collective-permute-done.6.refs_4_) | copy-start | bytes 1474564
  69.0 25.8 %collective-permute-start.8 = (bf16[4,80,768]{2,1,0:T(8,128)(2,1)S(1)}, bf16[4,80,768]{2,1,0:T(8,128)(2,1)}, u32[]{:S(2)}, u32[]{:S(2)}) collective-permute-start(bf16[4,80,768]{2,1,0:T(8,128)(2,1)S(1)} %collective-permute-done.4.refs_2_), channel_id=1, source_target_pairs={{0,1},{1,0},{2,3},{3,2},{4,5},{5,4},{6,7},{7,6},{8,9},{9,8},{10,11... | collective-permute-start | bytes 1474568 | tf_op jit(solution)/shard_map/ppermute | solution.py:36
  77.5 18.8 %collective-permute-start.9 = (bf16[4,80,768]{2,1,0:T(8,128)(2,1)}, bf16[4,80,768]{2,1,0:T(8,128)(2,1)}, u32[]{:S(2)}, u32[]{:S(2)}) collective-permute-start(bf16[4,80,768]{2,1,0:T(8,128)(2,1)} %collective-permute-done.5.refs_3_), channel_id=1, source_target_pairs={{0,1},{1,0},{2,3},{3,2},{4,5},{5,4},{6,7},{7,6},{8,9},{9,8},{10,11... | collective-permute-start | bytes 1474568 | tf_op jit(solution)/shard_map/ppermute | solution.py:36
  78.5 26.8 %copy-start.14 = (bf16[2,4,64,768]{3,2,1,0:T(8,128)(2,1)}, bf16[2,4,64,768]{3,2,1,0:T(8,128)(2,1)S(1)}, u32[]{:S(2)}) copy-start(bf16[2,4,64,768]{3,2,1,0:T(8,128)(2,1)S(1)} %copy.75) | copy-start | bytes 2359300
  80.5 27.5 %collective-permute-start.25 = (bf16[4,96,768]{2,1,0:T(8,128)(2,1)}, bf16[4,96,768]{2,1,0:T(8,128)(2,1)S(1)}, u32[]{:S(2)}, u32[]{:S(2)}) collective-permute-start(bf16[4,96,768]{2,1,0:T(8,128)(2,1)} %fusion.53.refs_0_), channel_id=1, source_target_pairs={{0,4},{4,0},{1,5},{5,1},{2,6},{6,2},{3,7},{7,3},{8,12},{12,8},{9,1... | collective-permute-start | bytes 1769480 | tf_op jit(solution)/shard_map/ppermute | solution.py:36
  93.3 19.2 %collective-permute-start.27 = (bf16[4,96,768]{2,1,0:T(8,128)(2,1)}, bf16[4,96,768]{2,1,0:T(8,128)(2,1)}, u32[]{:S(2)}, u32[]{:S(2)}) collective-permute-start(bf16[4,96,768]{2,1,0:T(8,128)(2,1)} %fusion.53.refs_0_), channel_id=1, source_target_pairs={{0,1},{1,0},{2,3},{3,2},{4,5},{5,4},{6,7},{7,6},{8,9},{9,8},{10,11... | collective-permute-start | bytes 1769480 | tf_op jit(solution)/shard_map/ppermute | solution.py:36
  93.3 19.6 %collective-permute-start.14 = (bf16[4,120,768]{2,1,0:T(8,128)(2,1)}, bf16[4,120,768]{2,1,0:T(8,128)(2,1)}, u32[]{:S(2)}, u32[]{:S(2)}) collective-permute-start(bf16[4,120,768]{2,1,0:T(8,128)(2,1)} %fusion.50.refs_0_), channel_id=1, source_target_pairs={{0,2},{2,0},{1,3},{3,1},{4,6},{6,4},{5,7},{7,5},{8,10},{10,8},{9,1... | collective-permute-start | bytes 2211848 | tf_op jit(solution)/shard_map/ppermute | solution.py:36
  94.8 21.4 %collective-permute-start.26 = (bf16[4,96,768]{2,1,0:T(8,128)(2,1)}, bf16[4,96,768]{2,1,0:T(8,128)(2,1)}, u32[]{:S(2)}, u32[]{:S(2)}) collective-permute-start(bf16[4,96,768]{2,1,0:T(8,128)(2,1)} %collective-permute-done.24.refs_1_), channel_id=1, source_target_pairs={{0,4},{4,0},{1,5},{5,1},{2,6},{6,2},{3,7},{7,3},{8,12},{12,8},{9,1... | collective-permute-start | bytes 1769480 | tf_op jit(solution)/shard_map/ppermute | solution.py:36
  96.3 32.0 %collective-permute-start.16 = (bf16[4,120,768]{2,1,0:T(8,128)(2,1)}, bf16[4,120,768]{2,1,0:T(8,128)(2,1)}, u32[]{:S(2)}, u32[]{:S(2)}) collective-permute-start(bf16[4,120,768]{2,1,0:T(8,128)(2,1)} %collective-permute-done.15.refs_2_), channel_id=1, source_target_pairs={{0,2},{2,0},{1,3},{3,1},{4,6},{6,4},{5,7},{7,5},{8,10},{10,8},{9,1... | collective-permute-start | bytes 2211848 | tf_op jit(solution)/shard_map/ppermute | solution.py:36
  108.0 37.9 %collective-permute-start.10 = (bf16[2,256,1536]{2,1,0:T(8,128)(2,1)}, bf16[2,256,1536]{2,1,0:T(8,128)(2,1)}, u32[]{:S(2)}, u32[]{:S(2)}) collective-permute-start(bf16[2,256,1536]{2,1,0:T(8,128)(2,1)} %bitcast.23.k_near.v_near), channel_id=1, source_target_pairs={{0,1},{1,0},{2,3},{3,2},{4,5},{5,4},{6,7},{7,6},{8,9},{9,8},{10,11... | collective-permute-start | bytes 4718600 | tf_op jit(solution)/shard_map/ppermute | solution.py:36
  112.4 5.7 %copy-start.31 = (bf16[32,1,768]{2,0,1:T(8,128)(2,1)S(1)}, bf16[32,1,768]{2,0,1:T(8,128)(2,1)}, u32[]{:S(2)}) copy-start(bf16[32,1,768]{2,0,1:T(8,128)(2,1)} %copy-done.30) | copy-start | bytes 147460
  112.4 17.0 %copy-start.2 = (bf16[2,1,256,768]{3,2,1,0:T(8,128)(2,1)S(1)}, bf16[2,1,256,768]{3,2,1,0:T(8,128)(2,1)}, u32[]{:S(2)}) copy-start(bf16[2,1,256,768]{3,2,1,0:T(8,128)(2,1)} %param.20) | copy-start | bytes 2359300
  112.4 5.8 %collective-permute-start.28 = (bf16[4,96,768]{2,1,0:T(8,128)(2,1)}, bf16[4,96,768]{2,1,0:T(8,128)(2,1)S(1)}, u32[]{:S(2)}, u32[]{:S(2)}) collective-permute-start(bf16[4,96,768]{2,1,0:T(8,128)(2,1)} %collective-permute-done.24.refs_1_), channel_id=1, source_target_pairs={{0,1},{1,0},{2,3},{3,2},{4,5},{5,4},{6,7},{7,6},{8,9},{9,8},{10,11... | collective-permute-start | bytes 1769480 | tf_op jit(solution)/shard_map/ppermute | solution.py:36
  112.9 6.2 %collective-permute-start.29 = (bf16[4,96,768]{2,1,0:T(8,128)(2,1)}, bf16[4,96,768]{2,1,0:T(8,128)(2,1)S(1)}, u32[]{:S(2)}, u32[]{:S(2)}) collective-permute-start(bf16[4,96,768]{2,1,0:T(8,128)(2,1)} %copy-done.21), channel_id=1, source_target_pairs={{0,1},{1,0},{2,3},{3,2},{4,5},{5,4},{6,7},{7,6},{8,9},{9,8},{10,11... | collective-permute-start | bytes 1769480 | tf_op jit(solution)/shard_map/ppermute | solution.py:36
  116.1 12.2 %collective-permute-start.30 = (bf16[4,96,768]{2,1,0:T(8,128)(2,1)}, bf16[4,96,768]{2,1,0:T(8,128)(2,1)}, u32[]{:S(2)}, u32[]{:S(2)}) collective-permute-start(bf16[4,96,768]{2,1,0:T(8,128)(2,1)} %collective-permute-done.26.refs_3_), channel_id=1, source_target_pairs={{0,1},{1,0},{2,3},{3,2},{4,5},{5,4},{6,7},{7,6},{8,9},{9,8},{10,11... | collective-permute-start | bytes 1769480 | tf_op jit(solution)/shard_map/ppermute | solution.py:36
  118.3 20.2 %collective-permute-start.17 = (bf16[4,120,768]{2,1,0:T(8,128)(2,1)}, bf16[4,120,768]{2,1,0:T(8,128)(2,1)S(1)}, u32[]{:S(2)}, u32[]{:S(2)}) collective-permute-start(bf16[4,120,768]{2,1,0:T(8,128)(2,1)} %fusion.50.refs_0_), channel_id=1, source_target_pairs={{0,1},{1,0},{2,3},{3,2},{4,5},{5,4},{6,7},{7,6},{8,9},{9,8},{10,11... | collective-permute-start | bytes 2211848 | tf_op jit(solution)/shard_map/ppermute | solution.py:36
  119.9 18.6 %collective-permute-start.19 = (bf16[4,120,768]{2,1,0:T(8,128)(2,1)}, bf16[4,120,768]{2,1,0:T(8,128)(2,1)S(1)}, u32[]{:S(2)}, u32[]{:S(2)}) collective-permute-start(bf16[4,120,768]{2,1,0:T(8,128)(2,1)} %collective-permute-done.15.refs_2_), channel_id=1, source_target_pairs={{0,1},{1,0},{2,3},{3,2},{4,5},{5,4},{6,7},{7,6},{8,9},{9,8},{10,11... | collective-permute-start | bytes 2211848 | tf_op jit(solution)/shard_map/ppermute | solution.py:36
  128.3 10.2 %collective-permute-start.18 = (bf16[4,120,768]{2,1,0:T(8,128)(2,1)}, bf16[4,120,768]{2,1,0:T(8,128)(2,1)}, u32[]{:S(2)}, u32[]{:S(2)}) collective-permute-start(bf16[4,120,768]{2,1,0:T(8,128)(2,1)} %collective-permute-done.14.refs_1_), channel_id=1, source_target_pairs={{0,1},{1,0},{2,3},{3,2},{4,5},{5,4},{6,7},{7,6},{8,9},{9,8},{10,11... | collective-permute-start | bytes 2211848 | tf_op jit(solution)/shard_map/ppermute | solution.py:36
  128.3 10.2 %collective-permute-start.20 = (bf16[4,120,768]{2,1,0:T(8,128)(2,1)}, bf16[4,120,768]{2,1,0:T(8,128)(2,1)}, u32[]{:S(2)}, u32[]{:S(2)}) collective-permute-start(bf16[4,120,768]{2,1,0:T(8,128)(2,1)} %collective-permute-done.16.refs_3_), channel_id=1, source_target_pairs={{0,1},{1,0},{2,3},{3,2},{4,5},{5,4},{6,7},{7,6},{8,9},{9,8},{10,11... | collective-permute-start | bytes 2211848 | tf_op jit(solution)/shard_map/ppermute | solution.py:36
  161.4 3.2 copy-start.32
  161.4 19.4 %slice-start = ((s8[4718592]{0:T(1024)(128)(4,1)}), s8[4194304]{0:T(1024)(128)(4,1)S(1)}, s32[]{:S(2)}) async-start(s8[4718592]{0:T(1024)(128)(4,1)} %bitcast.280), calls=%async_computation | async-start | bytes 8388608
  164.6 16.2 %slice-start.1 = ((s8[4718592]{0:T(1024)(128)(4,1)}), s8[524288]{0:T(1024)(128)(4,1)S(1)}, s32[]{:S(2)}) async-start(s8[4718592]{0:T(1024)(128)(4,1)} %bitcast.280), calls=%async_computation.1 | async-start | bytes 1048576
  186.6 4.8 %copy-start.10 = (bf16[512,768]{1,0:T(8,128)(2,1)}, bf16[512,768]{1,0:T(8,128)(2,1)S(1)}, u32[]{:S(2)}) copy-start(bf16[512,768]{1,0:T(8,128)(2,1)S(1)} %get-tuple-element.99) | copy-start | bytes 2359300
  222.5 20.3 %collective-permute-start.31 = (bf16[2,2,256,768]{3,2,1,0:T(8,128)(2,1)}, bf16[2,2,256,768]{3,2,1,0:T(8,128)(2,1)S(1)}, u32[]{:S(2)}, u32[]{:S(2)}) collective-permute-start(bf16[2,2,256,768]{3,2,1,0:T(8,128)(2,1)} %get-tuple-element.47), channel_id=1, source_target_pairs={{0,1},{1,0},{2,3},{3,2},{4,5},{5,4},{6,7},{7,6},{8,9},{9,8},{10,11... | collective-permute-start | bytes 4718600 | tf_op jit(solution)/shard_map/ppermute | solution.py:36
  230.8 3.2 copy-start.39
  232.6 30.9 %collective-permute-start.38 = (bf16[4,2,2,120,768]{4,3,0,2,1:T(8,128)(2,1)}, bf16[4,2,2,120,768]{4,3,0,2,1:T(8,128)(2,1)}, u32[]{:S(2)}, u32[]{:S(2)}) collective-permute-start(bf16[4,2,2,120,768]{4,3,0,2,1:T(8,128)(2,1)} %bitcast.262), channel_id=1, source_target_pairs={{0,1},{1,0},{2,3},{3,2},{4,5},{5,4},{6,7},{7,6},{8,9},{9,8},{10,11... | collective-permute-start | bytes 8847368 | tf_op jit(solution)/shard_map/ppermute | solution.py:36
  240.3 18.3 %collective-permute-start.44 = (bf16[4,2,2,96,768]{4,3,0,1,2:T(8,128)(2,1)}, bf16[4,2,2,96,768]{4,3,0,1,2:T(8,128)(2,1)}, u32[]{:S(2)}, u32[]{:S(2)}) collective-permute-start(bf16[4,2,2,96,768]{4,3,0,1,2:T(8,128)(2,1)} %bitcast.263), channel_id=1, source_target_pairs={{0,1},{1,0},{2,3},{3,2},{4,5},{5,4},{6,7},{7,6},{8,9},{9,8},{10,11... | collective-permute-start | bytes 7077896 | tf_op jit(solution)/shard_map/ppermute | solution.py:36
  252.3 14.7 %collective-permute-start.32 = (bf16[4,2,2,80,768]{4,3,0,1,2:T(8,128)(2,1)S(1)}, bf16[4,2,2,80,768]{4,3,0,1,2:T(8,128)(2,1)S(1)}, u32[]{:S(2)}, u32[]{:S(2)}) collective-permute-start(bf16[4,2,2,80,768]{4,3,0,1,2:T(8,128)(2,1)S(1)} %bitcast.288), channel_id=1, source_target_pairs={{0,1},{1,0},{2,3},{3,2},{4,5},{5,4},{6,7},{7,6},{8,9},{9,8},{10,11... | collective-permute-start | bytes 5898248 | tf_op jit(solution)/shard_map/ppermute | solution.py:36
  261.1 28.8 %collective-permute-start.45 = (bf16[4,2,96,768]{3,2,0,1:T(8,128)(2,1)S(1)}, bf16[4,2,96,768]{3,2,0,1:T(8,128)(2,1)S(1)}, u32[]{:S(2)}, u32[]{:S(2)}) collective-permute-start(bf16[4,2,96,768]{3,2,0,1:T(8,128)(2,1)S(1)} %dynamic-slice_bitcast_fusion.1), channel_id=1, source_target_pairs={{0,2},{2,0},{1,3},{3,1},{4,6},{6,4},{5,7},{7,5},{8,10},{10,8},{9,1... | collective-permute-start | bytes 3538952 | tf_op jit(solution)/shard_map/ppermute | solution.py:36
  267.6 43.7 %collective-permute-start.33 = (bf16[4,2,80,768]{3,2,0,1:T(8,128)(2,1)S(1)}, bf16[4,2,80,768]{3,2,0,1:T(8,128)(2,1)S(1)}, u32[]{:S(2)}, u32[]{:S(2)}) collective-permute-start(bf16[4,2,80,768]{3,2,0,1:T(8,128)(2,1)S(1)} %dynamic-slice_bitcast_fusion.2), channel_id=1, source_target_pairs={{0,2},{2,0},{1,3},{3,1},{4,6},{6,4},{5,7},{7,5},{8,10},{10,8},{9,1... | collective-permute-start | bytes 2949128 | tf_op jit(solution)/shard_map/ppermute | solution.py:36
  290.4 16.3 %collective-permute-start.46 = (bf16[4,96,768]{2,1,0:T(8,128)(2,1)S(1)}, bf16[4,96,768]{2,1,0:T(8,128)(2,1)S(1)}, u32[]{:S(2)}, u32[]{:S(2)}) collective-permute-start(bf16[4,96,768]{2,1,0:T(8,128)(2,1)S(1)} %dynamic-slice_bitcast_fusion.4), channel_id=1, source_target_pairs={{0,4},{4,0},{1,5},{5,1},{2,6},{6,2},{3,7},{7,3},{8,12},{12,8},{9,1... | collective-permute-start | bytes 1769480 | tf_op jit(solution)/shard_map/ppermute | solution.py:36
  292.1 46.2 %collective-permute-start.39 = (bf16[4,2,120,768]{3,2,0,1:T(8,128)(2,1)S(1)}, bf16[4,2,120,768]{3,2,0,1:T(8,128)(2,1)S(1)}, u32[]{:S(2)}, u32[]{:S(2)}) collective-permute-start(bf16[4,2,120,768]{3,2,0,1:T(8,128)(2,1)S(1)} %dynamic-slice_bitcast_fusion), channel_id=1, source_target_pairs={{0,4},{4,0},{1,5},{5,1},{2,6},{6,2},{3,7},{7,3},{8,12},{12,8},{9,1... | collective-permute-start | bytes 4423688 | tf_op jit(solution)/shard_map/ppermute | solution.py:36
  306.9 7.5 %collective-permute-start.49 = (bf16[96,768]{1,0:T(8,128)(2,1)S(1)}, bf16[96,768]{1,0:T(8,128)(2,1)S(1)}, u32[]{:S(2)}, u32[]{:S(2)}) collective-permute-start(bf16[96,768]{1,0:T(8,128)(2,1)S(1)} %get-tuple-element.128), channel_id=1, source_target_pairs={{0,24},{8,16},{16,8},{24,0},{1,25},{9,17},{17,9},{25,1},{2,26},{10... | collective-permute-start | bytes 442376 | tf_op jit(solution)/shard_map/ppermute | solution.py:36
  309.2 9.7 %collective-permute-start.48 = (bf16[96,768]{1,0:T(8,128)(2,1)S(1)}, bf16[96,768]{1,0:T(8,128)(2,1)S(1)}, u32[]{:S(2)}, u32[]{:S(2)}) collective-permute-start(bf16[96,768]{1,0:T(8,128)(2,1)S(1)} %get-tuple-element.129), channel_id=1, source_target_pairs={{0,16},{8,24},{16,0},{24,8},{1,17},{9,25},{17,1},{25,9},{2,18},{10... | collective-permute-start | bytes 442376 | tf_op jit(solution)/shard_map/ppermute | solution.py:36
  309.2 9.7 %collective-permute-start.47 = (bf16[96,768]{1,0:T(8,128)(2,1)S(1)}, bf16[96,768]{1,0:T(8,128)(2,1)S(1)}, u32[]{:S(2)}, u32[]{:S(2)}) collective-permute-start(bf16[96,768]{1,0:T(8,128)(2,1)S(1)} %get-tuple-element.127), channel_id=1, source_target_pairs={{0,8},{8,0},{16,24},{24,16},{1,9},{9,1},{17,25},{25,17},{2,10},{10... | collective-permute-start | bytes 442376 | tf_op jit(solution)/shard_map/ppermute | solution.py:36
  311.7 35.3 %collective-permute-start.34 = (bf16[4,80,768]{2,1,0:T(8,128)(2,1)S(1)}, bf16[4,80,768]{2,1,0:T(8,128)(2,1)S(1)}, u32[]{:S(2)}, u32[]{:S(2)}) collective-permute-start(bf16[4,80,768]{2,1,0:T(8,128)(2,1)S(1)} %dynamic-slice_bitcast_fusion.5), channel_id=1, source_target_pairs={{0,4},{4,0},{1,5},{5,1},{2,6},{6,2},{3,7},{7,3},{8,12},{12,8},{9,1... | collective-permute-start | bytes 1474568 | tf_op jit(solution)/shard_map/ppermute | solution.py:36
  347.2 8.1 %collective-permute-start.37 = (bf16[80,768]{1,0:T(8,128)(2,1)S(1)}, bf16[80,768]{1,0:T(8,128)(2,1)S(1)}, u32[]{:S(2)}, u32[]{:S(2)}) collective-permute-start(bf16[80,768]{1,0:T(8,128)(2,1)S(1)} %get-tuple-element.137), channel_id=1, source_target_pairs={{0,24},{8,16},{16,8},{24,0},{1,25},{9,17},{17,9},{25,1},{2,26},{10... | collective-permute-start | bytes 368648 | tf_op jit(solution)/shard_map/ppermute | solution.py:36
  349.5 9.5 %collective-permute-start.36 = (bf16[80,768]{1,0:T(8,128)(2,1)S(1)}, bf16[80,768]{1,0:T(8,128)(2,1)S(1)}, u32[]{:S(2)}, u32[]{:S(2)}) collective-permute-start(bf16[80,768]{1,0:T(8,128)(2,1)S(1)} %get-tuple-element.138), channel_id=1, source_target_pairs={{0,16},{8,24},{16,0},{24,8},{1,17},{9,25},{17,1},{25,9},{2,18},{10... | collective-permute-start | bytes 368648 | tf_op jit(solution)/shard_map/ppermute | solution.py:36
  349.5 9.5 %collective-permute-start.35 = (bf16[80,768]{1,0:T(8,128)(2,1)S(1)}, bf16[80,768]{1,0:T(8,128)(2,1)S(1)}, u32[]{:S(2)}, u32[]{:S(2)}) collective-permute-start(bf16[80,768]{1,0:T(8,128)(2,1)S(1)} %get-tuple-element.136), channel_id=1, source_target_pairs={{0,8},{8,0},{16,24},{24,16},{1,9},{9,1},{17,25},{25,17},{2,10},{10... | collective-permute-start | bytes 368648 | tf_op jit(solution)/shard_map/ppermute | solution.py:36
  351.7 15.9 %collective-permute-start.40 = (bf16[4,120,768]{2,1,0:T(8,128)(2,1)S(1)}, bf16[4,120,768]{2,1,0:T(8,128)(2,1)S(1)}, u32[]{:S(2)}, u32[]{:S(2)}) collective-permute-start(bf16[4,120,768]{2,1,0:T(8,128)(2,1)S(1)} %dynamic-slice_bitcast_fusion.3), channel_id=1, source_target_pairs={{0,2},{2,0},{1,3},{3,1},{4,6},{6,4},{5,7},{7,5},{8,10},{10,8},{9,1... | collective-permute-start | bytes 2211848 | tf_op jit(solution)/shard_map/ppermute | solution.py:36
  367.9 9.0 %collective-permute-start.43 = (bf16[120,768]{1,0:T(8,128)(2,1)S(1)}, bf16[120,768]{1,0:T(8,128)(2,1)S(1)}, u32[]{:S(2)}, u32[]{:S(2)}) collective-permute-start(bf16[120,768]{1,0:T(8,128)(2,1)S(1)} %get-tuple-element.119), channel_id=1, source_target_pairs={{0,24},{8,16},{16,8},{24,0},{1,25},{9,17},{17,9},{25,1},{2,26},{10... | collective-permute-start | bytes 552968 | tf_op jit(solution)/shard_map/ppermute | solution.py:36
  370.3 12.6 %collective-permute-start.42 = (bf16[120,768]{1,0:T(8,128)(2,1)S(1)}, bf16[120,768]{1,0:T(8,128)(2,1)S(1)}, u32[]{:S(2)}, u32[]{:S(2)}) collective-permute-start(bf16[120,768]{1,0:T(8,128)(2,1)S(1)} %get-tuple-element.120), channel_id=1, source_target_pairs={{0,16},{8,24},{16,0},{24,8},{1,17},{9,25},{17,1},{25,9},{2,18},{10... | collective-permute-start | bytes 552968 | tf_op jit(solution)/shard_map/ppermute | solution.py:36
  370.3 12.6 %collective-permute-start.41 = (bf16[120,768]{1,0:T(8,128)(2,1)S(1)}, bf16[120,768]{1,0:T(8,128)(2,1)S(1)}, u32[]{:S(2)}, u32[]{:S(2)}) collective-permute-start(bf16[120,768]{1,0:T(8,128)(2,1)S(1)} %get-tuple-element.118), channel_id=1, source_target_pairs={{0,8},{8,0},{16,24},{24,16},{1,9},{9,1},{17,25},{25,17},{2,10},{10... | collective-permute-start | bytes 552968 | tf_op jit(solution)/shard_map/ppermute | solution.py:36
  (28 other events, 49.4 us)

commit v2 on v0

--- a/solution.py
+++ b/solution.py
@@ -1,16 +1,21 @@
+import functools
+
 import jax
 import jax.numpy as jnp
 from jax import lax
+from jax.experimental import pallas as pl
+from jax.experimental.pallas import tpu as pltpu
+from jax.sharding import Mesh
 from jax.sharding import PartitionSpec as P
 
 H = 12
-MICRO = 2
-
-
 epsilon = 1e-12
 keep_scale = 8.0 / 7.0
 root_half = 0.7071067811865476
 inverse_root_tau = 0.3989422804014327
+every = ("z", "y", "x", "seq")
+f32 = jnp.float32
+bf16 = jnp.bfloat16
 
 
 def unpack_keep(packed_words):
@@ -44,7 +49,7 @@
     return jnp.dot(left_side, right_side, preferred_element_type=jnp.float32)
 
 
-def local(
+def plain_local(
     hidden_in,
     cotangent,
     attention_keep,
@@ -70,23 +75,23 @@
     head_count = H
     head_size = model_width // head_count
     held_params = (
-        lax.all_gather(qkv_weight, ("dp", "seq"), axis=0, tiled=True),
-        lax.all_gather(qkv_bias, ("dp", "seq"), axis=0, tiled=True),
-        lax.all_gather(out_weight, ("dp", "seq"), axis=0, tiled=True),
-        lax.all_gather(out_bias, ("dp", "seq"), axis=0, tiled=True),
-        lax.all_gather(first_gain, ("dp", "seq"), axis=0, tiled=True),
-        lax.all_gather(first_shift, ("dp", "seq"), axis=0, tiled=True),
-        lax.all_gather(up_weight, ("dp", "seq"), axis=0, tiled=True),
-        lax.all_gather(up_bias, ("dp", "seq"), axis=0, tiled=True),
-        lax.all_gather(down_weight, ("dp", "seq"), axis=0, tiled=True),
-        lax.all_gather(down_bias, ("dp", "seq"), axis=0, tiled=True),
-        lax.all_gather(second_gain, ("dp", "seq"), axis=0, tiled=True),
-        lax.all_gather(second_shift, ("dp", "seq"), axis=0, tiled=True),
+        lax.all_gather(qkv_weight, every, axis=0, tiled=True),
+        lax.all_gather(qkv_bias, every, axis=0, tiled=True),
+        lax.all_gather(out_weight, every, axis=0, tiled=True),
+        lax.all_gather(out_bias, every, axis=0, tiled=True),
+        lax.all_gather(first_gain, every, axis=0, tiled=True),
+        lax.all_gather(first_shift, every, axis=0, tiled=True),
+        lax.all_gather(up_weight, every, axis=0, tiled=True),
+        lax.all_gather(up_bias, every, axis=0, tiled=True),
+        lax.all_gather(down_weight, every, axis=0, tiled=True),
+        lax.all_gather(down_bias, every, axis=0, tiled=True),
+        lax.all_gather(second_gain, every, axis=0, tiled=True),
+        lax.all_gather(second_shift, every, axis=0, tiled=True),
     )
     totals = None
     outputs = []
     inputs_grad = []
-    for micro_step in range(MICRO):
+    for micro_step in range(hidden_in.shape[0]):
         (
             full_qkv_w,
             full_qkv_b,
@@ -276,18 +281,18 @@
         else:
             totals = tuple((before + added for before, added in zip(totals, grads_now)))
     summed = (
-        lax.psum_scatter(totals[0], ("dp", "seq"), scatter_dimension=0, tiled=True),
-        lax.psum_scatter(totals[1], ("dp", "seq"), scatter_dimension=0, tiled=True),
-        lax.psum_scatter(totals[2], ("dp", "seq"), scatter_dimension=0, tiled=True),
-        lax.psum_scatter(totals[3], ("dp", "seq"), scatter_dimension=0, tiled=True),
-        lax.psum_scatter(totals[4], ("dp", "seq"), scatter_dimension=0, tiled=True),
-        lax.psum_scatter(totals[5], ("dp", "seq"), scatter_dimension=0, tiled=True),
-        lax.psum_scatter(totals[6], ("dp", "seq"), scatter_dimension=0, tiled=True),
-        lax.psum_scatter(totals[7], ("dp", "seq"), scatter_dimension=0, tiled=True),
-        lax.psum_scatter(totals[8], ("dp", "seq"), scatter_dimension=0, tiled=True),
-        lax.psum_scatter(totals[9], ("dp", "seq"), scatter_dimension=0, tiled=True),
-        lax.psum_scatter(totals[10], ("dp", "seq"), scatter_dimension=0, tiled=True),
-        lax.psum_scatter(totals[11], ("dp", "seq"), scatter_dimension=0, tiled=True),
+        lax.psum_scatter(totals[0], every, scatter_dimension=0, tiled=True),
+        lax.psum_scatter(totals[1], every, scatter_dimension=0, tiled=True),
+        lax.psum_scatter(totals[2], every, scatter_dimension=0, tiled=True),
+        lax.psum_scatter(totals[3], every, scatter_dimension=0, tiled=True),
+        lax.psum_scatter(totals[4], every, scatter_dimension=0, tiled=True),
+        lax.psum_scatter(totals[5], every, scatter_dimension=0, tiled=True),
+        lax.psum_scatter(totals[6], every, scatter_dimension=0, tiled=True),
+        lax.psum_scatter(totals[7], every, scatter_dimension=0, tiled=True),
+        lax.psum_scatter(totals[8], every, scatter_dimension=0, tiled=True),
+        lax.psum_scatter(totals[9], every, scatter_dimension=0, tiled=True),
+        lax.psum_scatter(totals[10], every, scatter_dimension=0, tiled=True),
+        lax.psum_scatter(totals[11], every, scatter_dimension=0, tiled=True),
     )
     return (
         jnp.stack(outputs, axis=0),
@@ -307,44 +312,992 @@
     )
 
 
+ANY = pl.BlockSpec(memory_space=pl.ANY)
+WHOLE = pl.BlockSpec(memory_space=pltpu.VMEM)
+MIB = 2**20
+
+
+def dot_t(left_side, right_side):
+    return lax.dot_general(left_side, right_side, (((1,), (1,)), ((), ())), preferred_element_type=f32)
+
+
+def t_dot(left_side, right_side):
+    return lax.dot_general(left_side, right_side, (((0,), (0,)), ((), ())), preferred_element_type=f32)
+
+
+def iota(shape, axis):
+    return lax.broadcasted_iota(jnp.int32, shape, axis)
+
+
+def pp(value, axis, step=1):
+    size = lax.axis_size(axis)
+    return lax.ppermute(value, axis, [(i, i ^ step) for i in range(size)])
+
+
+def pick(value, axis, index):
+    return lax.dynamic_index_in_dim(value, index, axis, keepdims=False)
+
+
+def swap_if(flag, value, axis):
+    low = lax.slice_in_dim(value, 0, 1, axis=axis)
+    high = lax.slice_in_dim(value, 1, 2, axis=axis)
+    return jnp.where(flag, lax.concatenate([high, low], axis), value)
+
+
+def after(value, *earlier):
+    return lax.optimization_barrier((value,) + earlier)[0]
+
+
+def hold(values, *earlier):
+    return lax.optimization_barrier(tuple(values) + earlier)[: len(values)]
+
+
+def gather_z(own, other):
+    return jnp.stack([own, other])
+
+
+def order_z(pair, received):
+    z = lax.axis_index("z")
+    square = jnp.stack([pair, received], axis=1)
+    square = swap_if((z & 1) == 1, square, 1)
+    square = swap_if((z & 2) == 2, square, 0)
+    return square.reshape((4,) + pair.shape[1:])
+
+
+def select_z(shard, received):
+    z = lax.axis_index("z")
+    square = jnp.stack([shard, *received]).reshape((2, 2) + shard.shape)
+    square = swap_if((z & 1) == 1, square, 1)
+    square = swap_if((z & 2) == 2, square, 0)
+    return square.reshape((4,) + shard.shape)
+
+
+def add_up(terms):
+    total = terms[0].astype(f32)
+    for term in terms[1:]:
+        total = total + term.astype(f32)
+    return total
+
+
+class Weights:
+    def __init__(self, pieces, plan, shapes):
+        self.spans = [(number, first, array.shape[1]) for number, first, array in pieces]
+        self.operands = [pltpu.with_memory_space_constraint(array, pltpu.HBM) for _, _, array in pieces]
+        self.plan, self.shapes = plan, shapes
+        self.specs = [pl.BlockSpec(memory_space=pltpu.HBM)] * len(pieces)
+        self.scratch = [pltpu.VMEM((4, 2, 2, 2, rows, columns), bf16) for rows, columns in shapes]
+        self.scratch.append(pltpu.SemaphoreType.DMA((8 * len(plan),)))
+
+    def copies(self, ids, sources, places, sems):
+        found = [[] for _ in self.shapes]
+        count = 0
+        for start, rows, out, row, column in self.plan:
+            for (number, first, held), source in zip(self.spans, sources):
+                if first <= start and start + rows <= first + held:
+                    c = ids[0] ^ (number >> 2)
+                    y = ids[1] ^ ((number >> 1) & 1)
+                    x = ids[2] ^ (number & 1)
+                    src = source.at[:, pl.ds(start - first, rows), :]
+                    dst = places[out].at[:, y, x, c, pl.ds(row, rows), pl.ds(column, source.shape[2])]
+                    found[out].append(pltpu.make_async_copy(src, dst, sems.at[count]))
+                    count += 1
+        return found
+
+    def matrix(self, places, out):
+        rows, columns = self.shapes[out]
+        return places[out].reshape(32 * rows, columns)
+
+
+def begin(copies):
+    for group in copies:
+        for copy in group:
+            copy.start()
+
+
+def finish(group):
+    for copy in group:
+        copy.wait()
+
+
+def spread(block, row, count, per):
+    values = block[:, : -(-per // 128) * 128]
+    lanes = values.shape[1]
+    select = (iota((lanes, count), 1) % per == iota((lanes, count), 0)).astype(bf16)
+    wide = jnp.dot(values, select, preferred_element_type=f32)
+    own = (iota(wide.shape, 1) // per) * 8 + row == iota(wide.shape, 0)
+    return jnp.sum(jnp.where(own, wide, 0.0), axis=0, keepdims=True)
+
+
+def unspread(vectors, pers, width):
+    total = jnp.zeros((256, width), f32)
+    for row, (vector, per) in enumerate(zip(vectors, pers)):
+        count = vector.shape[1]
+        lanes = -(-per // 128) * 128
+        own = (iota((256, count), 1) // per) * 8 + row == iota((256, count), 0)
+        wide = jnp.where(own, vector, 0.0).astype(bf16)
+        select = (iota((count, lanes), 0) % per == iota((count, lanes), 1)).astype(bf16)
+        narrow = jnp.dot(wide, select, preferred_element_type=f32)
+        total = total + jnp.concatenate([narrow, jnp.zeros((256, width - lanes), f32)], axis=1)
+    return total
+
+
+def layer_norm(values):
+    centred = values - jnp.mean(values, axis=-1, keepdims=True)
+    inverse = lax.rsqrt(jnp.mean(centred * centred, axis=-1, keepdims=True) + epsilon)
+    return centred * inverse, inverse
+
+
+def turn_matrix(tokens):
+    place = iota((tokens, tokens), 0)
+    quarter = tokens // 4
+    return (iota((tokens, tokens), 1) == 4 * (place % quarter) + place // quarter).astype(bf16)
+
+
+def call(body, name, grid, operands, specs, outs, out_specs, scratch, room, load, aliases=None):
+    return pl.pallas_call(
+        body,
+        grid_spec=pltpu.PrefetchScalarGridSpec(
+            num_scalar_prefetch=1, grid=grid, in_specs=specs, out_specs=out_specs, scratch_shapes=scratch
+        ),
+        out_shape=outs,
+        compiler_params=pltpu.CompilerParams(vmem_limit_bytes=room * MIB),
+        cost_estimate=pl.CostEstimate(flops=1024, bytes_accessed=load * MIB, transcendentals=0),
+        input_output_aliases=aliases or {},
+        name=name,
+    )(*operands)
+
+
+def shaped(shape, dtype):
+    return jax.ShapeDtypeStruct(shape, dtype)
+
+
+def rows_spec(rows, columns):
+    return pl.BlockSpec((rows, columns), lambda i, ids: (i, 0))
+
+
+def fixed_spec(shape):
+    return pl.BlockSpec(shape, lambda i, ids: (0,) * len(shape))
+
+
+def prepare_body(ids, hidden, output_words, feed_words, turned, keep_output, keep_feed):
+    tokens, width = hidden.shape
+    turned[...] = jnp.dot(turn_matrix(tokens), hidden[...], preferred_element_type=f32).astype(bf16)
+    quarter = width // 4
+    for words, keep in ((output_words, keep_output), (feed_words, keep_feed)):
+        packed = words[...]
+        total = jnp.zeros((tokens, width), f32)
+        for i in range(4):
+            bit = ((packed & (7 << (3 * i))) != 0).astype(f32).astype(bf16)
+            place = (iota((quarter, width), 1) == 4 * iota((quarter, width), 0) + i).astype(bf16)
+            total = total + jnp.dot(bit, place, preferred_element_type=f32)
+        keep[...] = total.astype(bf16)
+
+
+def prepare(ids, hidden, output_words, feed_words, tokens):
+    rows, width = hidden.shape
+    wide, narrow = rows_spec(tokens, width), rows_spec(tokens, width // 4)
+    return call(
+        prepare_body,
+        "prepare",
+        (rows // tokens,),
+        (ids, hidden, output_words, feed_words),
+        [wide, narrow, narrow],
+        [shaped((rows, width), bf16)] * 3,
+        [wide] * 3,
+        [],
+        12,
+        6,
+    )
+
+
+def project_body(weights, per, ids, *refs):
+    count = len(weights.operands)
+    sources, (hidden, turned, queries), rest = refs[:count], refs[count : count + 3], refs[count + 3 :]
+    micro, tokens, width = queries.shape
+    near, rest = rest[: 2 * micro], rest[2 * micro :]
+    places, sems = rest[:-1], rest[-1]
+    copies = weights.copies(ids, sources, places, sems)
+    begin(copies)
+    finish(copies[3])
+    bias = spread(weights.matrix(places, 3)[...], 0, 2 * width, per)
+    for n in range(3):
+        finish(copies[n])
+    for m in range(micro):
+        natural, other = hidden[m * tokens : (m + 1) * tokens, :], turned[m * tokens : (m + 1) * tokens, :]
+        q = jnp.dot(natural, weights.matrix(places, 0)[...], preferred_element_type=f32) + bias[:, :width]
+        queries[m] = q.astype(bf16)
+        k = jnp.dot(other, weights.matrix(places, 1)[...], preferred_element_type=f32)
+        near[2 * m][...] = k.astype(bf16)
+        v = jnp.dot(other, weights.matrix(places, 2)[...], preferred_element_type=f32) + bias[:, width:]
+        near[2 * m + 1][...] = v.astype(bf16)
+
+
+def project(ids, weights, hidden, turned, micro, per):
+    rows, width = hidden.shape
+    return call(
+        functools.partial(project_body, weights, per),
+        "project",
+        (1,),
+        (ids, *weights.operands, hidden, turned),
+        weights.specs + [WHOLE] * 2,
+        [shaped((micro, rows // micro, width), bf16)] + [shaped((rows // micro, width), bf16)] * (2 * micro),
+        [WHOLE] * (1 + 2 * micro),
+        weights.scratch,
+        16,
+        10,
+    )
+
+
+def lane_half(shape):
+    return iota(shape, len(shape) - 1) < 64
+
+
+def join_keys(core, near, far, buffer):
+    quarter = near.shape[0] // 4
+    for i in range(4):
+        here = pl.multiple_of((2 * i + core) * quarter, quarter)
+        there = pl.multiple_of((2 * i + 1 - core) * quarter, quarter)
+        buffer[pl.ds(here, quarter), :] = near[i * quarter : (i + 1) * quarter, :]
+        buffer[pl.ds(there, quarter), :] = far[i * quarter : (i + 1) * quarter, :]
+
+
+def attention_body(ids, q, k_near, v_near, k_far, v_far, words, *refs):
+    context, signed, keys, values = refs[-4:]
+    core = ids[0]
+    join_keys(core, k_near, k_far, keys)
+    join_keys(core, v_near, v_far, values)
+    queries = q[0]
+    left = lane_half(queries.shape)
+    zero = jnp.zeros_like(queries)
+    outs = []
+    for h in range(2):
+        masked = jnp.where(left if h == 0 else ~left, queries, zero) * 0.125
+        scores = dot_t(masked, keys[...])
+        blocks = [scores[:, i * 128 : (i + 1) * 128] for i in range(4)]
+        peak = jnp.maximum(jnp.maximum(blocks[0], blocks[1]), jnp.maximum(blocks[2], blocks[3]))
+        peak = jnp.max(peak, axis=1, keepdims=True)
+        blocks = [jnp.exp(block - peak) for block in blocks]
+        total = jnp.sum((blocks[0] + blocks[1]) + (blocks[2] + blocks[3]), axis=1, keepdims=True)
+        scale = 1.0 / total
+        word = words[0, h]
+        dropped = []
+        for i in range(4):
+            weight = blocks[i] * scale
+            keep = (word & (7 << (3 * i))) != 0
+            weight = jnp.where(keep, weight, -weight).astype(bf16)
+            signed[0, 0, h, i] = weight
+            dropped.append(jnp.maximum(weight, jnp.zeros_like(weight)))
+        outs.append(
+            jnp.dot(jnp.concatenate(dropped, axis=1), values[...], preferred_element_type=f32) * keep_scale
+        )
+    context[0] = jnp.where(left, outs[0], outs[1]).astype(bf16)
+
+
+def attention(ids, m, queries, near, far, words, earlier=()):
+    micro, tokens, width = queries.shape
+    pairs = width // 128
+    part = pl.BlockSpec((1, tokens, 128), lambda p, ids: (m, 0, p))
+    flat = pl.BlockSpec((tokens, 128), lambda p, ids: (0, p))
+    operands = (ids, queries, *near[2 * m : 2 * m + 2], *far[2 * m : 2 * m + 2], words)
+    return call(
+        attention_body,
+        "attention",
+        (pairs,),
+        operands + tuple(earlier),
+        [part] + [flat] * 4
+        + [pl.BlockSpec((1, 2, tokens, 128), lambda p, ids: (m, p, 0, 0))]
+        + [ANY] * len(earlier),
+        [shaped((micro, tokens, width), bf16), shaped((micro, pairs, 2, 4, tokens, 128), bf16)],
+        [part, pl.BlockSpec((1, 1, 2, 4, tokens, 128), lambda p, ids: (m, p, 0, 0, 0, 0))],
+        [pltpu.VMEM((2 * tokens, 128), bf16)] * 2,
+        8,
+        14,
+        {len(operands) + i: i for i in range(len(earlier))},
+    )
+
+
+def attention_back_body(ids, q, k_near, v_near, k_far, v_far, signed, upstream, *refs):
+    g_q, g_near, g_far, keys, values, sums = refs[-6:]
+    core = ids[0]
+    join_keys(core, k_near, k_far, keys)
+    join_keys(core, v_near, v_far, values)
+    queries = q[0]
+    above = upstream[...]
+    left = lane_half(queries.shape)
+    left_long = lane_half(keys.shape)
+    zero = jnp.zeros_like(queries)
+    grads = []
+    for h in range(2):
+        masked = jnp.where(left if h == 0 else ~left, above, zero)
+        g_dropped = dot_t(masked, values[...])
+        weights, kept, g_weights = [], [], []
+        delta = None
+        for i in range(4):
+            both = signed[0, 0, h, i].astype(f32)
+            weight = jnp.abs(both)
+            g_weight = jnp.where(both > 0.0, g_dropped[:, i * 128 : (i + 1) * 128], 0.0)
+            term = g_weight * weight
+            delta = term if delta is None else delta + term
+            weights.append(weight)
+            g_weights.append(g_weight)
+            kept.append(jnp.maximum(both, 0.0).astype(bf16))
+        delta = jnp.sum(delta, axis=1, keepdims=True)
+        g_scores = jnp.concatenate(
+            [(weights[i] * (g_weights[i] - delta)).astype(bf16) for i in range(4)], axis=1
+        )
+        dropped = jnp.concatenate(kept, axis=1)
+        grads.append(
+            (
+                jnp.dot(g_scores, keys[...], preferred_element_type=f32),
+                t_dot(g_scores, queries),
+                t_dot(dropped, above),
+            )
+        )
+    g_q[0] = (jnp.where(left, grads[0][0], grads[1][0]) * (0.125 * keep_scale)).astype(bf16)
+    quarter = keys.shape[0] // 8
+    for kind, factor in ((0, 0.125 * keep_scale), (1, keep_scale)):
+        sums[...] = jnp.where(left_long, grads[0][kind + 1], grads[1][kind + 1]) * factor
+        for i in range(4):
+            here = pl.multiple_of((2 * i + core) * quarter, quarter)
+            there = pl.multiple_of((2 * i + 1 - core) * quarter, quarter)
+            g_near[kind, 0, i * quarter : (i + 1) * quarter, :] = sums[pl.ds(here, quarter), :]
+            g_far[kind, 0, i * quarter : (i + 1) * quarter, :] = sums[pl.ds(there, quarter), :].astype(bf16)
+
+
+def attention_back(ids, m, queries, near, far, signed, upstream, earlier=()):
+    micro, tokens, width = queries.shape
+    pairs = width // 128
+    part = pl.BlockSpec((1, tokens, 128), lambda p, ids: (m, 0, p))
+    flat = pl.BlockSpec((tokens, 128), lambda p, ids: (0, p))
+    both = pl.BlockSpec((2, 1, tokens, 128), lambda p, ids: (0, m, 0, p))
+    operands = (ids, queries, *near[2 * m : 2 * m + 2], *far[2 * m : 2 * m + 2], signed, upstream)
+    return call(
+        attention_back_body,
+        "attention_back",
+        (pairs,),
+        operands + tuple(earlier),
+        [part] + [flat] * 4
+        + [pl.BlockSpec((1, 1, 2, 4, tokens, 128), lambda p, ids: (m, p, 0, 0, 0, 0))]
+        + [pl.BlockSpec((tokens, 128), lambda p, ids: (m, p))]
+        + [ANY] * len(earlier),
+        [
+            shaped((micro, tokens, width), bf16),
+            shaped((2, micro, tokens, width), f32),
+            shaped((2, micro, tokens, width), bf16),
+        ],
+        [part, both, both],
+        [pltpu.VMEM((2 * tokens, 128), bf16)] * 2 + [pltpu.VMEM((2 * tokens, 128), f32)],
+        12,
+        20,
+        {len(operands) + i: i for i in range(len(earlier))},
+    )
+
+
+def up_body(weights, pers, ids, *refs):
+    count = len(weights.operands)
+    sources = refs[:count]
+    context, hidden, keep, vectors, scaled, inverse, activated, slope = refs[count : count + 8]
+    places, sems = refs[count + 8 : -1], refs[-1]
+    copies = weights.copies(ids, sources, places, sems)
+    width, wide = scaled.shape[1], activated.shape[1]
+
+    @pl.when(pl.program_id(0) == 0)
+    def _():
+        begin([copies[0], copies[2], copies[1]])
+        finish(copies[2])
+        block = weights.matrix(places, 2)[...]
+        for row, per in enumerate(pers):
+            vectors[row : row + 1, : 32 * per] = spread(block, row, 32 * per, per)
+        finish(copies[0])
+
+    attended = jnp.dot(context[...], weights.matrix(places, 0)[...], preferred_element_type=f32)
+    attended = attended + vectors[0:1, :width]
+    first_sum = hidden[...].astype(f32) + attended * (keep[...].astype(f32) * keep_scale)
+    normal, scale = layer_norm(first_sum)
+    scaled[...] = normal
+    inverse[...] = jnp.broadcast_to(scale, inverse.shape)
+    low = (normal * vectors[1:2, :width] + vectors[2:3, :width]).astype(bf16)
+
+    @pl.when(pl.program_id(0) == 0)
+    def _():
+        finish(copies[1])
+
+    up = weights.matrix(places, 1)
+    step = 512
+
+    def part(n, carry):
+        at = pl.ds(pl.multiple_of(n * step, step), step)
+        inner = jnp.dot(low, up[:, at], preferred_element_type=f32) + vectors[3:4, at]
+        cdf = 0.5 * (1.0 + lax.erf(inner * root_half))
+        density = jnp.exp(-0.5 * inner * inner) * inverse_root_tau
+        activated[:, at] = (inner * cdf).astype(bf16)
+        slope[:, at] = (cdf + inner * density).astype(bf16)
+        return carry
+
+    lax.fori_loop(0, wide // step, part, 0)
+
+
+def feed_up(ids, weights, pers, context, hidden, keep, tokens, wide):
+    rows, width = hidden.shape
+    narrow, broad = rows_spec(tokens, width), rows_spec(tokens, wide)
+    return call(
+        functools.partial(up_body, weights, pers),
+        "feed_up",
+        (rows // tokens,),
+        (ids, *weights.operands, context, hidden, keep),
+        weights.specs + [narrow] * 3,
+        [
+            shaped((8, wide), f32),
+            shaped((rows, width), f32),
+            shaped((rows, 128), f32),
+            shaped((rows, wide), bf16),
+            shaped((rows, wide), bf16),
+        ],
+        [fixed_spec((8, wide)), narrow, rows_spec(tokens, 128), broad, broad],
+        weights.scratch,
+        28,
+        24,
+    )
+
+
+def hand_out(core, total, rows, own, send, first, at):
+    def one(n, carry):
+        here = pl.multiple_of((2 * n + core) * rows, 8)
+        there = pl.multiple_of((2 * n + 1 - core) * rows, 8)
+        own[first + n, at : at + rows, :] = total[pl.ds(here, rows), :].astype(bf16)
+        send[first + n, at : at + rows, :] = total[pl.ds(there, rows), :].astype(bf16)
+        return carry
+
+    lax.fori_loop(0, total.shape[0] // (2 * rows), one, 0)
+
+
+def down_body(weights, ids, *refs):
+    count = len(weights.operands)
+    sources = refs[:count]
+    activated, slope, scaled, keep, cotangent, vectors = refs[count : count + 6]
+    layer_out, g_second_out, g_inner, own, send, sums = refs[count + 6 : count + 12]
+    places, (sems, total, g_outers) = refs[count + 12 : -3], refs[-3:]
+    copies = weights.copies(ids, sources, places, sems)
+    tokens, width = scaled.shape
+    wide = activated.shape[1]
+    first = pl.program_id(0) == 0
+    mine = pl.ds(pl.multiple_of(pl.program_id(0) * tokens, tokens), tokens)
+
+    @pl.when(first)
+    def _():
+        begin(copies)
+        sums[...] = jnp.zeros_like(sums)
+        finish(copies[0])
+
+    down = weights.matrix(places, 0)
+    outer = jnp.dot(activated[mine, :], down[...], preferred_element_type=f32) + vectors[4:5, :width]
+    factor = keep[...].astype(f32) * keep_scale
+    normed = scaled[...] * vectors[1:2, :width] + vectors[2:3, :width]
+    normal, scale = layer_norm(normed + outer * factor)
+    gain = vectors[5:6, :width]
+    layer_out[...] = (normal * gain + vectors[6:7, :width]).astype(bf16)
+    above = cotangent[...].astype(f32)
+    weighted = above * gain
+    g_second = scale * (
+        weighted
+        - jnp.mean(weighted, axis=-1, keepdims=True)
+        - normal * jnp.mean(weighted * normal, axis=-1, keepdims=True)
+    )
+    g_second_out[...] = g_second
+    g_outer = (g_second * factor).astype(bf16)
+    g_outers[mine, :] = g_outer
+    sums[0:1, :width] += jnp.sum(g_outer.astype(f32), axis=0, keepdims=True)
+    sums[1:2, :width] += jnp.sum(above * normal, axis=0, keepdims=True)
+    sums[2:3, :width] += jnp.sum(above, axis=0, keepdims=True)
+    step = 512
+
+    def part(n, carry):
+        at = pl.ds(pl.multiple_of(n * step, step), step)
+        g_in = (dot_t(g_outer, down[at, :]) * slope[:, at].astype(f32)).astype(bf16)
+        g_inner[:, at] = g_in
+        sums[3:4, at] += jnp.sum(g_in.astype(f32), axis=0, keepdims=True)
+        return carry
+
+    lax.fori_loop(0, wide // step, part, 0)
+
+    @pl.when(pl.program_id(0) == pl.num_programs(0) - 1)
+    def _():
+        def grads(n, carry):
+            at = pl.ds(pl.multiple_of(n * width, width), width)
+            total[...] = t_dot(activated[:, at], g_outers[...])
+            hand_out(ids[0], total, wide // 32, own, send, n * (16 * width // wide), 0)
+            return carry
+
+        lax.fori_loop(0, wide // width, grads, 0)
+
+
+def feed_down(ids, weights, activated, slope, scaled, keep, cotangent, vectors, tokens):
+    rows, width = scaled.shape
+    wide = activated.shape[1]
+    narrow, broad = rows_spec(tokens, width), rows_spec(tokens, wide)
+    halves = (16, wide // 32, width)
+    return call(
+        functools.partial(down_body, weights),
+        "feed_down",
+        (rows // tokens,),
+        (ids, *weights.operands, activated, slope, scaled, keep, cotangent, vectors),
+        weights.specs + [WHOLE, broad, narrow, narrow, narrow, WHOLE],
+        [
+            shaped((rows, width), bf16),
+            shaped((rows, width), f32),
+            shaped((rows, wide), bf16),
+            shaped(halves, bf16),
+            shaped(halves, bf16),
+            shaped((8, wide), f32),
+        ],
+        [narrow, narrow, broad, WHOLE, WHOLE, WHOLE],
+        weights.scratch + [pltpu.VMEM((width, width), f32), pltpu.VMEM((rows, width), bf16)],
+        40,
+        36,
+    )
+
+
+def middle_body(weights, ids, *refs):
+    count = len(weights.operands)
+    sources = refs[:count]
+    g_inner, g_second, scaled, inverse, keep, vectors = refs[count : count + 6]
+    g_first_out, g_attended_out, g_context, sums = refs[count + 6 : count + 10]
+    places, sems = refs[count + 10 : -1], refs[-1]
+    copies = weights.copies(ids, sources, places, sems)
+    width = scaled.shape[1]
+
+    @pl.when(pl.program_id(0) == 0)
+    def _():
+        begin([copies[1], copies[0]])
+        sums[...] = jnp.zeros_like(sums)
+        finish(copies[1])
+        finish(copies[0])
+
+    normal = scaled[...]
+    g_normed = g_second[...] + dot_t(g_inner[...], weights.matrix(places, 1)[...])
+    weighted = g_normed * vectors[1:2, :width]
+    g_first = inverse[:, 0:1] * (
+        weighted
+        - jnp.mean(weighted, axis=-1, keepdims=True)
+        - normal * jnp.mean(weighted * normal, axis=-1, keepdims=True)
+    )
+    g_first_out[...] = g_first
+    g_attended = (g_first * (keep[...].astype(f32) * keep_scale)).astype(bf16)
+    g_attended_out[...] = g_attended
+    sums[0:1, :] += jnp.sum(g_attended.astype(f32), axis=0, keepdims=True)
+    sums[1:2, :] += jnp.sum(g_normed * normal, axis=0, keepdims=True)
+    sums[2:3, :] += jnp.sum(g_normed, axis=0, keepdims=True)
+    g_context[...] = dot_t(g_attended, weights.matrix(places, 0)[...]).astype(bf16)
+
+
+def middle(ids, weights, g_inner, g_second, scaled, inverse, keep, vectors, tokens):
+    rows, width = scaled.shape
+    wide = g_inner.shape[1]
+    narrow, broad = rows_spec(tokens, width), rows_spec(tokens, wide)
+    return call(
+        functools.partial(middle_body, weights),
+        "middle",
+        (rows // tokens,),
+        (ids, *weights.operands, g_inner, g_second, scaled, inverse, keep, vectors),
+        weights.specs + [broad, narrow, narrow, rows_spec(tokens, 128), narrow, WHOLE],
+        [
+            shaped((rows, width), f32),
+            shaped((rows, width), bf16),
+            shaped((rows, width), bf16),
+            shaped((8, width), f32),
+        ],
+        [narrow, narrow, narrow, WHOLE],
+        weights.scratch,
+        24,
+        14,
+    )
+
+
+def grads_body(pers, ids, g_inner, scaled, context, g_attended, vectors, sums, more, own, send, total, low, bias):
+    n = pl.program_id(0)
+    width = scaled.shape[1]
+    rows = width // 32
+
+    @pl.when(n == 0)
+    def _():
+        low[...] = (scaled[...] * vectors[1:2, :width] + vectors[2:3, :width]).astype(bf16)
+        vector_sums = [more[i : i + 1, :] for i in range(3)]
+        vector_sums += [sums[3:4, :]] + [sums[i : i + 1, :width] for i in range(3)]
+        bias[...] = unspread(vector_sums, pers, width)
+        hand_out(ids[0], bias, 8, own, send, 0, (1 + sums.shape[1] // width) * rows)
+        total[...] = t_dot(context[...], g_attended[...])
+        hand_out(ids[0], total, rows, own, send, 0, 0)
+
+    total[...] = t_dot(low[...], g_inner[...])
+    for block in range(sums.shape[1] // width):
+
+        @pl.when(n == block)
+        def _():
+            hand_out(ids[0], total, rows, own, send, 0, (block + 1) * rows)
+
+
+def middle_grads(ids, pers, g_inner, scaled, context, g_attended, vectors, sums, more):
+    rows, width = scaled.shape
+    wide = g_inner.shape[1]
+    halves = (16, (width + wide) // 32 + 8, width)
+    return call(
+        functools.partial(grads_body, pers),
+        "middle_grads",
+        (wide // width,),
+        (ids, g_inner, scaled, context, g_attended, vectors, sums, more),
+        [pl.BlockSpec((rows, width), lambda i, ids: (0, i))] + [WHOLE] * 6,
+        [shaped(halves, bf16), shaped(halves, bf16)],
+        [WHOLE] * 2,
+        [pltpu.VMEM((width, width), f32), pltpu.VMEM((rows, width), bf16), pltpu.VMEM((256, width), f32)],
+        24,
+        20,
+    )
+
+
+def inputs_body(per, ids, hidden, turned, g_q, g_near, g_far, own, send, g_keys, g_values, total, bias):
+    rows, width = hidden.shape
+    sums = []
+    for n in range(3):
+        if n == 0:
+            grad = g_q[...].reshape(rows, width)
+        else:
+            grad = (g_near[n - 1] + g_far[n - 1].astype(f32)).astype(bf16).reshape(rows, width)
+            (g_keys, g_values)[n - 1][...] = grad
+        if n != 1:
+            sums.append(jnp.sum(grad.astype(f32), axis=0, keepdims=True))
+        left = hidden if n == 0 else turned
+        for start in range(0, width, 256):
+            total[start : start + 256, :] = t_dot(left[:, start : start + 256], grad)
+        hand_out(ids[0], total, width // 32, own, send, 0, n * (width // 32))
+    bias[...] = unspread([jnp.concatenate(sums, axis=1)], [per], width)
+    hand_out(ids[0], bias, 8, own, send, 0, 3 * (width // 32))
+
+
+def input_grads(ids, hidden, turned, g_q, g_near, g_far, per):
+    rows, width = hidden.shape
+    halves = (16, 3 * width // 32 + 8, width)
+    return call(
+        functools.partial(inputs_body, per),
+        "input_grads",
+        (1,),
+        (ids, hidden, turned, g_q, g_near, g_far),
+        [WHOLE] * 5,
+        [shaped(halves, bf16)] * 2 + [shaped((rows, width), bf16)] * 2,
+        [WHOLE] * 4,
+        [pltpu.VMEM((width, width), f32), pltpu.VMEM((256, width), f32)],
+        28,
+        12,
+    )
+
+
+def last_body(weights, ids, *refs):
+    count = len(weights.operands)
+    sources = refs[:count]
+    g_first, g_q, g_keys, g_values, out = refs[count : count + 5]
+    places, sems = refs[count + 5 : -1], refs[-1]
+    copies = weights.copies(ids, sources, places, sems)
+
+    @pl.when(pl.program_id(0) == 0)
+    def _():
+        begin(copies)
+        for group in copies:
+            finish(group)
+
+    turn = turn_matrix(g_q.shape[0])
+    total = g_first[...] + dot_t(g_q[...], weights.matrix(places, 0)[...])
+    total = total + dot_t(t_dot(turn, g_keys[...]).astype(bf16), weights.matrix(places, 1)[...])
+    total = total + dot_t(t_dot(turn, g_values[...]).astype(bf16), weights.matrix(places, 2)[...])
+    out[...] = total.astype(bf16)
+
+
+def last(ids, weights, g_first, g_q, g_keys, g_values, tokens):
+    rows, width = g_first.shape
+    narrow = rows_spec(tokens, width)
+    return call(
+        functools.partial(last_body, weights),
+        "input_back",
+        (rows // tokens,),
+        (ids, *weights.operands, g_first, g_q, g_keys, g_values),
+        weights.specs + [narrow] * 4,
+        [shaped((rows, width), bf16)],
+        [narrow],
+        weights.scratch,
+        16,
+        10,
+    )[0]
+
+
+def beside(shape, y, x):
+    return pl.BlockSpec((4, 1, 1) + shape[3:], lambda i, ids: (0, ids[1] ^ y, ids[2] ^ x, 0, 0))
+
+
+def corner_body(ids, one, two, low, high):
+    cut = low.shape[1]
+    low[...] = (one[:, 0, 0, :cut].astype(f32) + two[:, 0, 0, :cut].astype(f32)).astype(bf16)
+    high[...] = (one[:, 0, 0, cut:].astype(f32) + two[:, 0, 0, cut:].astype(f32)).astype(bf16)
+
+
+def reduce_corner(ids, terms, cut):
+    _, _, _, rows, width = terms[0].shape
+    return call(
+        corner_body,
+        "reduce_corner",
+        (1,),
+        (ids, *terms),
+        [beside(terms[0].shape, 1, 1)] * 2,
+        [shaped((4, cut, width), bf16), shaped((4, rows - cut, width), bf16)],
+        [WHOLE] * 2,
+        [],
+        8,
+        2,
+    )
+
+
+def sides_body(ids, one_y, two_y, one_x, two_x, low, high, to_y, to_x):
+    cut = low.shape[1]
+    to_y[:, :cut] = (
+        one_y[:, 0, 0, :cut].astype(f32) + two_y[:, 0, 0, :cut].astype(f32) + low[...].astype(f32)
+    ).astype(bf16)
+    to_y[:, cut:] = (one_y[:, 0, 0, cut:].astype(f32) + two_y[:, 0, 0, cut:].astype(f32)).astype(bf16)
+    to_x[:, :cut] = (one_x[:, 0, 0, :cut].astype(f32) + two_x[:, 0, 0, :cut].astype(f32)).astype(bf16)
+    to_x[:, cut:] = (
+        one_x[:, 0, 0, cut:].astype(f32) + two_x[:, 0, 0, cut:].astype(f32) + high[...].astype(f32)
+    ).astype(bf16)
+
+
+def reduce_sides(ids, terms, low, high):
+    shape = terms[0].shape
+    return call(
+        sides_body,
+        "reduce_sides",
+        (1,),
+        (ids, *terms, *terms, low, high),
+        [beside(shape, 1, 0)] * 2 + [beside(shape, 0, 1)] * 2 + [WHOLE] * 2,
+        [shaped((4,) + shape[3:], bf16)] * 2,
+        [WHOLE] * 2,
+        [],
+        10,
+        3,
+    )
+
+
+def depth_body(ids, one, two, from_y, from_x, near, middle, far, mine):
+    for k, out in enumerate((mine, near, middle, far)):
+        z = ids[3] ^ k
+        total = one[z, 0, 0].astype(f32) + two[z, 0, 0].astype(f32)
+        total = total + from_y[z].astype(f32) + from_x[z].astype(f32)
+        out[...] = total.astype(out.dtype)
+
+
+def reduce_depth(ids, terms, from_y, from_x):
+    shape = terms[0].shape
+    return call(
+        depth_body,
+        "reduce_depth",
+        (1,),
+        (ids, *terms, from_y, from_x),
+        [beside(shape, 0, 0)] * 2 + [WHOLE] * 2,
+        [shaped(shape[3:], bf16)] * 3 + [shaped(shape[3:], f32)],
+        [WHOLE] * 4,
+        [],
+        10,
+        3,
+    )
+
+
+def exchange_z(sends):
+    return [pp(send, "z", k) for send, k in zip(sends, (1, 2, 3))]
+
+
+def local(
+    hidden_in,
+    cotangent,
+    attention_keep,
+    output_keep,
+    feed_keep,
+    qkv_weight,
+    qkv_bias,
+    out_weight,
+    out_bias,
+    first_gain,
+    first_shift,
+    up_weight,
+    up_bias,
+    down_weight,
+    down_bias,
+    second_gain,
+    second_shift,
+):
+    micro, _, tokens, width = hidden_in.shape
+    rows = micro * tokens
+    own = qkv_weight.shape[0]
+    wide = up_weight.shape[1]
+    blocks = wide // width
+    c, y, x = lax.axis_index("seq"), lax.axis_index("y"), lax.axis_index("x")
+    ids = jnp.stack([c, y, x, lax.axis_index("z")]).astype(jnp.int32)
+    bias_parts = (out_bias, first_gain, first_shift, up_bias, down_bias, second_gain, second_shift)
+    pers = [part.shape[0] for part in bias_parts]
+    per = qkv_bias.shape[0]
+
+    column = lambda weight, i: weight[:, i * width : (i + 1) * width]
+    bias_rows = lambda parts: jnp.concatenate(
+        [jnp.pad(part.reshape(1, -1), ((0, 0), (0, width - part.shape[0]))) for part in parts]
+        + [jnp.zeros((8 - len(parts), width), bf16)]
+    )
+    square = (own, width)
+    hidden = hidden_in.reshape(rows, width)
+
+    shard_a = jnp.concatenate([column(qkv_weight, i) for i in range(3)] + [bias_rows((qkv_bias,))])
+    own_a = select_z(shard_a, [pp(shard_a, "z", k) for k in (1, 2, 3)])
+    x_a, y_a = pp(own_a, "x"), pp(own_a, "y")
+    shard_b = jnp.concatenate(
+        [out_weight] + [column(up_weight, i) for i in range(blocks)] + [bias_rows(bias_parts)]
+    )
+    shard_b = after(shard_b, own_a)
+    far_b = pp(shard_b, "z", 2)
+    x_a, y_a, far_b = hold((x_a, y_a, far_b))
+    cut_a = 2 * own
+    low_a, high_a = pp(x_a[:, :cut_a], "y"), pp(y_a[:, cut_a:], "x")
+    pieces = [(0, 0, own_a), (1, 0, x_a), (2, 0, y_a), (3, 0, low_a), (3, cut_a, high_a)]
+    pieces += [(number + 4, first, pp(piece, "seq")) for number, first, piece in pieces]
+    pair_b = gather_z(shard_b, far_b)
+    near_b = pp(pair_b, "z", 1)
+    turned, keep_output, keep_feed = prepare(
+        ids, after(hidden, far_b), output_keep.reshape(rows, -1), feed_keep.reshape(rows, -1), tokens
+    )
+    plan = [(i * own, own, i, 0, 0) for i in range(3)]
+    weights = Weights(pieces, plan + [(3 * own, 8, 3, 0, 0)], [square] * 3 + [(8, width)])
+    weights_again = Weights(pieces, plan, [square] * 3)
+    queries, *near = project(ids, weights, hidden, turned, micro, per)
+    far = [pp(value, "seq") for value in near]
+    own_b = order_z(pair_b, after(near_b, *near))
+    x_b, y_b = pp(own_b, "x"), pp(own_b, "y")
+    shard_c = after(down_weight, own_b)
+    far_c = pp(shard_c, "z", 2)
+    words = attention_keep.reshape(micro, H, tokens, -1)
+    far[0], far[1], far_c = hold((far[0], far[1], far_c), own_b)
+    pair_c = gather_z(shard_c, far_c)
+    near_c = pp(pair_c, "z", 1)
+    context, signed = attention(ids, 0, queries, near, far, words)
+    far[2], far[3] = hold((far[2], far[3]), context)
+    context, signed = attention(ids, 1, queries, near, far, words, (context, signed))
+    own_b, x_b, y_b, near_c = hold((own_b, x_b, y_b, near_c), context)
+    cut_b = 3 * own
+    low_b, high_b = pp(x_b[:, :cut_b], "y"), pp(y_b[:, cut_b:], "x")
+    pieces = [(0, 0, own_b), (1, 0, x_b), (2, 0, y_b)]
+    pieces += [(number + 4, first, pp(piece, "seq")) for number, first, piece in pieces]
+    pieces += [(3, 0, low_b), (3, cut_b, high_b), (7, 0, pp(low_b, "seq")), (7, cut_b, pp(high_b, "seq"))]
+    plan = [(0, own, 0, 0, 0)] + [((i + 1) * own, own, 1, 0, i * width) for i in range(blocks)]
+    weights = Weights(
+        pieces, plan + [((blocks + 1) * own, 8, 2, 0, 0)], [square, (own, wide), (8, width)]
+    )
+    back_weights = Weights(pieces, plan, [square, (own, wide)])
+    own_c = order_z(pair_c, hold((near_c,), low_b, high_b)[0])
+    x_c, y_c = pp(own_c, "x"), pp(own_c, "y")
+    context = context.reshape(rows, width)
+    vectors, scaled, inverse, activated, slope = feed_up(
+        ids, weights, pers, context, hidden, keep_output, tokens, wide
+    )
+    x_c, y_c = hold((x_c, y_c), activated)
+    down_rows = down_weight.shape[0]
+    cut_c = down_rows // 2
+    low_c, high_c = pp(x_c[:, :cut_c], "y"), pp(y_c[:, cut_c:], "x")
+    pieces = [(0, 0, own_c), (1, 0, x_c), (2, 0, y_c), (3, 0, low_c), (3, cut_c, high_c)]
+    pieces += [(number + 4, first, pp(piece, "seq")) for number, first, piece in pieces]
+    weights = Weights(
+        pieces, [(0, cut_c, 0, 0, 0), (cut_c, cut_c, 0, cut_c, 0)], [(down_rows, width)]
+    )
+    layer_out, g_second, g_inner, down_own, down_send, sums = feed_down(
+        ids, weights, activated, slope, scaled, keep_feed, cotangent.reshape(rows, width), vectors, tokens
+    )
+
+    unit = lambda value: value.reshape((4, 2, 2) + value.shape[1:])
+    down_core = pp(down_send, "seq")
+    g_first, g_attended, g_context, more = middle(
+        ids, back_weights, g_inner, g_second, scaled, inverse, keep_output, vectors, tokens
+    )
+    down = [unit(down_own), unit(after(down_core, g_context))]
+    corner = reduce_corner(ids, down, cut_c)
+    low, high = pp(corner[0], "x"), pp(corner[1], "y")
+    mid_own, mid_send = middle_grads(
+        ids, pers, g_inner, scaled, context, after(g_attended, *corner), vectors, sums, more
+    )
+    low, high = hold((low, high), mid_send)
+    to_y, to_x = reduce_sides(ids, down, low, high)
+    down_y, down_x = pp(to_y, "y"), pp(to_x, "x")
+    mid_core = pp(after(mid_send, low, high), "seq")
+    grads = attention_back(ids, 0, queries, near, far, signed, after(g_context, to_y, to_x))
+    mid = [unit(mid_own), unit(after(mid_core, *grads))]
+    corner = reduce_corner(ids, mid, cut_b)
+    low, high = pp(corner[0], "x"), pp(corner[1], "y")
+    g_q, g_near, g_far = attention_back(
+        ids, 1, queries, near, far, signed, after(g_context, *corner), tuple(grads)
+    )
+    low, high, down_y, down_x = hold((low, high, down_y, down_x), g_q)
+    far_grads = pp(after(g_far, low, high, down_y, down_x), "seq")
+    to_y, to_x = reduce_sides(ids, mid, low, high)
+    mid_y, mid_x = pp(to_y, "y"), pp(to_x, "x")
+    *sends, down_mine = reduce_depth(ids, down, down_y, down_x)
+    down_z = exchange_z(sends)
+    a_own, a_send, g_keys, g_values = input_grads(
+        ids, hidden, turned, g_q, g_near, after(far_grads, to_y, to_x, *sends), per
+    )
+    grad_in = last(ids, weights_again, g_first, g_q.reshape(rows, width), g_keys, g_values, tokens)
+    mid_y, mid_x = hold((mid_y, mid_x), grad_in)
+    core_sums = pp(after(a_send, mid_y, mid_x), "seq")
+    part = [unit(a_own), unit(core_sums)]
+    corner = reduce_corner(ids, part, cut_a)
+    low, high = pp(corner[0], "x"), pp(corner[1], "y")
+    *sends, mid_mine = reduce_depth(ids, mid, after(mid_y, *corner), mid_x)
+    mid_z = exchange_z(sends)
+    grad_down = add_up([down_mine, *hold(down_z, *sends)])
+    low, high = hold((low, high), grad_down)
+    to_y, to_x = reduce_sides(ids, part, low, high)
+    side_y, side_x = pp(to_y, "y"), pp(to_x, "x")
+    mid = add_up([mid_mine, *hold(mid_z, to_y, to_x)])
+    side_y, side_x = hold((side_y, side_x), mid)
+    *sends, part_mine = reduce_depth(ids, part, side_y, side_x)
+    part = add_up([part_mine, *exchange_z(sends)])
+
+    stripe = lambda value, i: value[i * own : (i + 1) * own]
+    grad_qkv = jnp.concatenate([stripe(part, i) for i in range(3)], axis=1)
+    grad_up = jnp.concatenate([stripe(mid, i + 1) for i in range(blocks)], axis=1)
+    vector_grads = [mid[(blocks + 1) * own + i, :length] for i, length in enumerate(pers)]
+    return (
+        layer_out.reshape(hidden_in.shape),
+        grad_in.reshape(hidden_in.shape),
+        grad_qkv,
+        part[3 * own, :per],
+        stripe(mid, 0),
+        vector_grads[0],
+        vector_grads[1],
+        vector_grads[2],
+        grad_up,
+        vector_grads[3],
+        grad_down,
+        vector_grads[4],
+        vector_grads[5],
+        vector_grads[6],
+    )
+
+
 def solution(mesh):
+    groups, cores = mesh.devices.shape
+    split = Mesh(mesh.devices.reshape(groups // 4, 2, 2, cores), ("z", "y", "x", "seq"))
+    dp = ("z", "y", "x")
+    token_rows = P(None, dp, "seq", None)
+    matrix = P(every, None)
+    vector = P(every)
+    params = (matrix, vector, matrix, vector, vector, vector, matrix, vector, matrix, vector, vector, vector)
+
+    def layer(*arrays):
+        tiled = groups == 16 and cores == 2 and arrays[5].shape[0] % 8 == 0
+        return (local if tiled else plain_local)(*arrays)
+
     return jax.shard_map(
-        local,
-        mesh=mesh,
-        in_specs=(
-            P(None, "dp", "seq", None),
-            P(None, "dp", "seq", None),
-            P(None, "dp", None, "seq", None),
-            P(None, "dp", "seq", None),
-            P(None, "dp", "seq", None),
-            P(("dp", "seq"), None),
-            P(("dp", "seq")),
-            P(("dp", "seq"), None),
-            P(("dp", "seq")),
-            P(("dp", "seq")),
-            P(("dp", "seq")),
-            P(("dp", "seq"), None),
-            P(("dp", "seq")),
-            P(("dp", "seq"), None),
-            P(("dp", "seq")),
-            P(("dp", "seq")),
-            P(("dp", "seq")),
-        ),
-        out_specs=(
-            P(None, "dp", "seq", None),
-            P(None, "dp", "seq", None),
-            P(("dp", "seq"), None),
-            P(("dp", "seq")),
-            P(("dp", "seq"), None),
-            P(("dp", "seq")),
-            P(("dp", "seq")),
-            P(("dp", "seq")),
-            P(("dp", "seq"), None),
-            P(("dp", "seq")),
-            P(("dp", "seq"), None),
-            P(("dp", "seq")),
-            P(("dp", "seq")),
-            P(("dp", "seq")),
-        ),
+        layer,
+        mesh=split,
+        in_specs=(token_rows, token_rows, P(None, dp, None, "seq", None), token_rows, token_rows) + params,
+        out_specs=(token_rows, token_rows) + params,
         check_vma=False,
     )

time: 891 us -> 272 us (0.31); the launches traced: 880 us -> 271 us
  waiting for transfers between devices: 503 us -> 90.8 us
  matrix products: 130 us -> 0 us
  Pallas kernels: 0 us -> 110 us
  blocking collectives: 96.7 us -> 0 us
  local copies, waits for them, and re-layouts: 93.9 us -> 12.7 us
  starting transfers between devices: 1.06 us -> 49.4 us
  other arithmetic: 39.9 us -> 6.54 us
  between operations: 15.8 us -> 1.8 us
    reduce_scatter x7 -> x0, waiting for transfers between devices: 301 us -> none  [the longest x1 142 us: local(): lax.psum_scatter(totals[8], ('dp', 'seq'), scatter_dimension=0, tiled=True)]
    dot_general x36 -> x0, matrix products: 130 us -> none  [the longest x24 86.6 us: matmul(): return jnp.dot(left_side, right_side, preferred_element_type=jnp.float32)]
    unnamed x13 -> x0, waiting for transfers between devices: 128 us -> none
    pallas_call x0 -> x21, Pallas kernels: none -> 110 us  [call(): pl.pallas_call(body, grid_spec=pltpu.PrefetchScalarGridSpec(num_scalar_pr...]
    ppermute x0 -> x63, waiting for transfers between devices: none -> 90.8 us  [pp(): return lax.ppermute(value, axis, [(i, i ^ step) for i in range(size)])]
    unnamed x2 -> x0, blocking collectives: 84.7 us -> none
    all_gather x4 -> x0, waiting for transfers between devices: 74.1 us -> none  [the longest x1 54 us: local(): lax.all_gather(down_weight, ('dp', 'seq'), axis=0, tiled=True)]
    ppermute x0 -> x63, starting transfers between devices: none -> 49.4 us  [pp(): return lax.ppermute(value, axis, [(i, i ^ step) for i in range(size)])]
  transfers between devices with their start and end apart: 12 -> 63, of which waited for: 7 -> 19; matrix products, arithmetic and copies ran while one was open for 24% -> 4% of each run, Pallas kernels for 0% -> 33%
where the time goes in v2:
time: 272 us; the launch traced here: 271 us
  Pallas kernels  110 us (40%)
  waiting for transfers between devices  90.8 us (33%)
  starting transfers between devices  49.4 us (18%)
  local copies, waits for them, and re-layouts  12.7 us (5%)
  other arithmetic  6.54 us (2%)
    pallas_call x21, Pallas kernels, call(): pl.pallas_call(body, grid_spec=pltpu.PrefetchScalarGridSpec(num_scalar_pr...  110 us
    ppermute x63, waiting for transfers between devices, pp(): return lax.ppermute(value, axis, [(i, i ^ step) for i in range(size)])  90.8 us
    ppermute x63, starting transfers between devices, pp(): return lax.ppermute(value, axis, [(i, i ^ step) for i in range(size)])  49.4 us
    unnamed x114, local copies, waits for them, and re-layouts  7.47 us
  transfers between devices with their start and end apart: 63, of which 19 were waited for; matrix products, arithmetic and copies ran while one was open for 4% of the time, Pallas kernels for 33%

profile of v2, /device:TPU:0, one launch (start us, length us, event | category | flops | bytes accessed | tf_op | source)
XLA Modules:
  0.0 271.4 jit_solution(17648641238437149757)
XLA Ops:
  0.6 0.8 fusion.10
  2.2 5.1 %collective-permute-start.2 = (bf16[80,768]{1,0:T(8,128)(2,1)S(1)}, bf16[80,768]{1,0:T(8,128)(2,1)S(1)}, u32[]{:S(2)}, u32[]{:S(2)}) collective-permute-start(bf16[80,768]{1,0:T(8,128)(2,1)S(1)} %concatenate.35), channel_id=1, source_target_pairs={{0,24},{8,16},{16,8},{24,0},{1,25},{9,17},{17,9},{25,1},{2,26},{10... | collective-permute-start | bytes 368648 | tf_op jit(solution)/shard_map/ppermute | solution.py:334
  7.9 3.6 %collective-permute-done.2 = bf16[80,768]{1,0:T(8,128)(2,1)S(1)} collective-permute-done((bf16[80,768]{1,0:T(8,128)(2,1)S(1)}, bf16[80,768]{1,0:T(8,128)(2,1)S(1)}, u32[]{:S(2)}, u32[]{:S(2)}) %collective-permute-start.2) | collective-permute-done | bytes 122912 | tf_op jit(solution)/shard_map/ppermute | solution.py:334
  11.5 6.1 %collective-permute-done.1 = bf16[80,768]{1,0:T(8,128)(2,1)S(1)} collective-permute-done((bf16[80,768]{1,0:T(8,128)(2,1)S(1)}, bf16[80,768]{1,0:T(8,128)(2,1)S(1)}, u32[]{:S(2)}, u32[]{:S(2)}) %collective-permute-start.1) | collective-permute-done | bytes 122912 | tf_op jit(solution)/shard_map/ppermute | solution.py:334
  18.2 1.6 collective-permute-start.4
  19.8 1.5 collective-permute-start.3
  21.8 12.2 %collective-permute-done.5 = bf16[128,768]{1,0:T(8,128)(2,1)S(1)} collective-permute-done((bf16[128,768]{1,0:T(8,128)(2,1)S(1)}, bf16[128,768]{1,0:T(8,128)(2,1)S(1)}, u32[]{:S(2)}, u32[]{:S(2)}) %collective-permute-start.5) | collective-permute-done | bytes 196640 | tf_op jit(solution)/shard_map/ppermute | solution.py:334
  34.5 0.9 slice.123
  36.6 0.8 pad_maximum_fusion.3
  37.4 5.6 %collective-permute-done.7.refs_3_ = bf16[4,48,768]{2,1,0:T(8,128)(2,1)S(1)} collective-permute-done((bf16[4,48,768]{2,1,0:T(8,128)(2,1)S(1)}, bf16[4,48,768]{2,1,0:T(8,128)(2,1)S(1)}, u32[]{:S(2)}, u32[]{:S(2)}) %collective-permute-start.7) | collective-permute-done | bytes 294944 | tf_op jit(solution)/shard_map/ppermute | solution.py:334
  43.5 1.2 copy.36
  44.7 1.2 copy.37
  46.0 3.1 %prepare.1 = (bf16[512,768]{1,0:T(8,128)(2,1)S(1)}, bf16[512,768]{1,0:T(8,128)(2,1)S(1)}, bf16[512,768]{1,0:T(8,128)(2,1)S(1)}) custom-call(s32[4]{0:T(128)S(1)} %pad_add_fusion.ids, bf16[512,768]{1,0:T(8,128)(2,1)S(1)} %bitcast.94, s32[512,192]{1,0:T(8,128)S(1)} %bitcast.103, s32[512,192]{1,0:T(8,128)S(1)} %bitcast.104), custom_call_target="tpu_custom_call" | custom-call | flops 1024 | bytes 6291456 | tf_op jit(solution)/shard_map/prepare/pallas_call | solution.py:457
  49.2 5.3 %project.1 = (bf16[2,256,768]{2,1,0:T(8,128)(2,1)S(1)}, bf16[256,768]{1,0:T(8,128)(2,1)S(1)}, bf16[256,768]{1,0:T(8,128)(2,1)S(1)}, bf16[256,768]{1,0:T(8,128)(2,1)S(1)}, bf16[256,768]{1,0:T(8,128)(2,1)S(1)}) custom-call(s32[4]{0:T(128)S(1)} %pad_add_fusion.ids, bf16[4,80,768]{2,1,0:T(8,128)(2,1)} %copy-done.25, bf16[4,80,768]{2,1,0:T(8,128)(2,1)} %copy-done.26, ...), custom_call_target="tpu_custom_call" | custom-call | flops 1024 | bytes 10485760 | tf_op jit(solution)/shard_map/project/pallas_call | solution.py:457
  55.2 1.2 maximum_select_fusion
  56.5 1.4 maximum_select_fusion.1
  58.0 1.2 collective-permute-start.15
  59.8 8.4 %collective-permute-done.18 = bf16[96,768]{1,0:T(8,128)(2,1)S(1)} collective-permute-done((bf16[96,768]{1,0:T(8,128)(2,1)S(1)}, bf16[96,768]{1,0:T(8,128)(2,1)S(1)}, u32[]{:S(2)}, u32[]{:S(2)}) %collective-permute-start.18) | collective-permute-done | bytes 147488 | tf_op jit(solution)/shard_map/ppermute | solution.py:334
  68.8 7.2 %attention.2 = (bf16[2,256,768]{2,1,0:T(8,128)(2,1)S(1)}, bf16[2,6,2,4,256,128]{5,4,3,2,1,0:T(8,128)(2,1)S(1)}) custom-call(s32[4]{0:T(128)S(1)} %pad_add_fusion.ids, bf16[2,256,768]{2,1,0:T(8,128)(2,1)S(1)} %get-tuple-element.137.q, bf16[256,768]{1,0:T(8,128)(2,1)S(1)} %get-tuple-element.130.k_near, bf16[256,768]{1,0:T(8,128)(2,1)S(1)} %get-tuple-element.131.v_near, ...), custom_call_target="tpu_custom_call" | custom-call | flops 1024 | bytes 14680064 | tf_op jit(solution)/shard_map/attention/pallas_call | solution.py:457
  76.1 7.2 %attention.3 = (bf16[2,256,768]{2,1,0:T(8,128)(2,1)S(1)}, bf16[2,6,2,4,256,128]{5,4,3,2,1,0:T(8,128)(2,1)S(1)}) custom-call(s32[4]{0:T(128)S(1)} %pad_add_fusion.ids, bf16[2,256,768]{2,1,0:T(8,128)(2,1)S(1)} %get-tuple-element.137.q, bf16[256,768]{1,0:T(8,128)(2,1)S(1)} %get-tuple-element.132.k_near, ...), custom_call_target="tpu_custom_call", output_to_operand_aliasing={{0}: (7, {}), {1}: (8, {})} | custom-call | flops 1024 | bytes 14680064 | tf_op jit(solution)/shard_map/attention/pallas_call | solution.py:457
  84.1 1.6 collective-permute-start.23
  86.1 7.8 %collective-permute-done.23.refs_7_ = bf16[4,56,768]{2,1,0:T(8,128)(2,1)S(1)} collective-permute-done((bf16[4,56,768]{2,1,0:T(8,128)(2,1)S(1)}, bf16[4,56,768]{2,1,0:T(8,128)(2,1)S(1)}, u32[]{:S(2)}, u32[]{:S(2)}) %collective-permute-start.23) | collective-permute-done | bytes 344096 | tf_op jit(solution)/shard_map/ppermute | solution.py:334
  93.9 1.7 collective-permute-done.22.refs_6_
  96.7 1.5 collective-permute-start.24
  98.8 1.3 collective-permute-done.29.refs_8_
  100.0 0.7 copy-done.33
  100.8 12.4 %feed_up.1 = (f32[8,3072]{1,0:T(8,128)S(1)}, f32[512,768]{1,0:T(8,128)S(1)}, f32[512,128]{1,0:T(8,128)S(1)}, bf16[512,3072]{1,0:T(8,128)(2,1)S(1)}, bf16[512,3072]{1,0:T(8,128)(2,1)S(1)}) custom-call(s32[4]{0:T(128)S(1)} %pad_add_fusion.ids, bf16[4,128,768]{2,1,0:T(8,128)(2,1)} %bitcast.109, bf16[4,128,768]{2,1,0:T(8,128)(2,1)} %copy-done.23, ...), custom_call_target="tpu_custom_call" | custom-call | flops 1024 | bytes 25165824 | tf_op jit(solution)/shard_map/feed_up/pallas_call | solution.py:457
  113.2 1.7 copy-done.3
  114.9 1.7 copy-done.4
  117.6 1.5 collective-permute-start.31
  119.1 7.1 %collective-permute-done.32.refs_4_ = bf16[4,48,768]{2,1,0:T(8,128)(2,1)S(1)} collective-permute-done((bf16[4,48,768]{2,1,0:T(8,128)(2,1)S(1)}, bf16[4,48,768]{2,1,0:T(8,128)(2,1)S(1)}, u32[]{:S(2)}, u32[]{:S(2)}) %collective-permute-start.32) | collective-permute-done | bytes 294944 | tf_op jit(solution)/shard_map/ppermute | solution.py:334
  127.0 0.8 collective-permute-done.37.refs_9_
  129.3 20.0 %feed_down.1 = (bf16[512,768]{1,0:T(8,128)(2,1)}, f32[512,768]{1,0:T(8,128)S(1)}, bf16[512,3072]{1,0:T(8,128)(2,1)S(1)}, bf16[16,96,768]{2,1,0:T(8,128)(2,1)S(1)...) custom-call(s32[4]{0:T(128)S(1)} %pad_add_fusion.ids, bf16[4,96,768]{2,1,0:T(8,128)(2,1)} %bitcast.116, ...), custom_call_target="tpu_custom_call" | custom-call | flops 1024 | bytes 37748736 | tf_op jit(solution)/shard_map/feed_down/pallas_call | solution.py:457
  149.5 9.1 %middle.1 = (f32[512,768]{1,0:T(8,128)S(1)}, bf16[512,768]{1,0:T(8,128)(2,1)S(1)}, bf16[512,768]{1,0:T(8,128)(2,1)S(1)}, f32[8,768]{1,0:T(8,128)S(1)}) custom-call(s32[4]{0:T(128)S(1)} %pad_add_fusion.ids, bf16[4,128,768]{2,1,0:T(8,128)(2,1)} %bitcast.110, bf16[4,128,768]{2,1,0:T(8,128)(2,1)} %copy-done.23, bf16[4,128,768]{2,1,0:T(8,128)(2,1)} %copy-done.24, ...), custom_call_target="tpu_custom_call" | custom-call | flops 1024 | bytes 14680064 | tf_op jit(solution)/shard_map/middle/pallas_call | solution.py:457
  159.2 1.6 collective-permute-start.39
  160.8 1.5 collective-permute-start.40
  162.3 8.4 %middle_grads.1 = (bf16[16,128,768]{2,1,0:T(8,128)(2,1)S(1)}, bf16[16,128,768]{2,1,0:T(8,128)(2,1)S(1)}) custom-call(s32[4]{0:T(128)S(1)} %pad_add_fusion.ids, bf16[512,3072]{1,0:T(8,128)(2,1)S(1)} %get-tuple-element.159.refs_10_.g_inner, f32[512,768]{1,0:T(8,128)S(1)} %get-tuple-element.155.refs_12_.scaled, bf16[512,768]{1,0:T(8,128)(2,1)S(1)} %bitcast.102, ...), custom_call_target="tpu_custom_call" | custom-call | flops 1024 | bytes 20971520 | tf_op jit(solution)/shard_map/middle_grads/pallas_call | solution.py:457
  170.8 0.9 reduce_sides.3
  172.9 9.1 %attention_back.2 = (bf16[2,256,768]{2,1,0:T(8,128)(2,1)S(1)}, f32[2,2,256,768]{3,2,1,0:T(8,128)S(1)}, bf16[2,2,256,768]{3,2,1,0:T(8,128)(2,1)S(1)}) custom-call(s32[4]{0:T(128)S(1)} %pad_add_fusion.ids, bf16[2,256,768]{2,1,0:T(8,128)(2,1)S(1)} %get-tuple-element.137.q, bf16[256,768]{1,0:T(8,128)(2,1)S(1)} %get-tuple-element.130.k_near, ...), custom_call_target="tpu_custom_call" | custom-call | flops 1024 | bytes 20971520 | tf_op jit(solution)/shard_map/attention_back/pallas_call | solution.py:457
  182.8 1.5 collective-permute-start.42
  184.3 1.5 collective-permute-start.43
  185.8 9.4 %attention_back.3 = (bf16[2,256,768]{2,1,0:T(8,128)(2,1)S(1)}, f32[2,2,256,768]{3,2,1,0:T(8,128)S(1)}, bf16[2,2,256,768]{3,2,1,0:T(8,128)(2,1)S(1)}) custom-call(s32[4]{0:T(128)S(1)} %pad_add_fusion.ids, bf16[2,256,768]{2,1,0:T(8,128)(2,1)S(1)} %get-tuple-element.137.q, ...), custom_call_target="tpu_custom_call", output_to_operand_aliasing={{0}: (8, {}), {1}: (9, {}), {2}: (10, {})} | custom-call | flops 1024 | bytes 20971520 | tf_op jit(solution)/shard_map/attention_back/pallas_call | solution.py:457
  195.2 2.0 collective-permute-done.42.low
  197.2 1.0 reduce_sides.4
  198.3 1.5 collective-permute-start.47
  200.4 1.0 reduce_depth.3
  201.4 4.7 %input_grads.1 = (bf16[16,80,768]{2,1,0:T(8,128)(2,1)S(1)}, bf16[16,80,768]{2,1,0:T(8,128)(2,1)S(1)}, bf16[512,768]{1,0:T(8,128)(2,1)S(1)}, bf16[512,768]{1,0:T(8,128)(2,1)S(1)}) custom-call(s32[4]{0:T(128)S(1)} %pad_add_fusion.ids, bf16[512,768]{1,0:T(8,128)(2,1)S(1)} %bitcast.97, bf16[512,768]{1,0:T(8,128)(2,1)S(1)} %copy-done.6, ...), custom_call_target="tpu_custom_call" | custom-call | flops 1024 | bytes 12582912 | tf_op jit(solution)/shard_map/input_grads/pallas_call | solution.py:457
  206.1 6.4 %input_back.1 = bf16[512,768]{1,0:T(8,128)(2,1)} custom-call(s32[4]{0:T(128)S(1)} %pad_add_fusion.ids, bf16[4,80,768]{2,1,0:T(8,128)(2,1)} %copy-done.25, bf16[4,80,768]{2,1,0:T(8,128)(2,1)} %copy-done.26, bf16[4,80,768]{2,1,0:T(8,128)(2,1)} %collective-permute-done.4.refs_2_, bf16[4,48,768]{2,1,0:T(8,128)(2,1)} %copy-done.38, ...), custom_call_target="tpu_custom_call" | custom-call | flops 1024 | bytes 10485760 | tf_op jit(solution)/shard_map/input_back/pallas_call | solution.py:457
  212.5 5.8 %collective-permute-done.47.from_y = bf16[4,128,768]{2,1,0:T(8,128)(2,1)S(1)} collective-permute-done((bf16[4,128,768]{2,1,0:T(8,128)(2,1)S(1)}, bf16[4,128,768]{2,1,0:T(8,128)(2,1)S(1)}, u32[]{:S(2)}, u32[]{:S(2)}) %collective-permute-start.47) | collective-permute-done | bytes 786464 | tf_op jit(solution)/shard_map/ppermute | solution.py:334
  218.3 1.2 collective-permute-done.48.from_x
  219.5 1.7 collective-permute-start.52
  221.2 1.3 collective-permute-start.53
  222.5 1.3 collective-permute-start.54
  225.7 1.3 reduce_depth.4
  226.9 1.5 collective-permute-done.52
  228.5 6.7 %collective-permute-done.53 = bf16[96,768]{1,0:T(8,128)(2,1)S(1)} collective-permute-done((bf16[96,768]{1,0:T(8,128)(2,1)S(1)}, bf16[96,768]{1,0:T(8,128)(2,1)S(1)}, u32[]{:S(2)}, u32[]{:S(2)}) %collective-permute-start.53) | collective-permute-done | bytes 147488 | tf_op jit(solution)/shard_map/ppermute | solution.py:334
  235.2 2.5 collective-permute-start.59
  237.7 0.8 convert_add_fusion.1
  238.5 0.8 reduce_sides.5
  240.4 10.9 %collective-permute-done.58 = bf16[128,768]{1,0:T(8,128)(2,1)S(1)} collective-permute-done((bf16[128,768]{1,0:T(8,128)(2,1)S(1)}, bf16[128,768]{1,0:T(8,128)(2,1)S(1)}, u32[]{:S(2)}, u32[]{:S(2)}) %collective-permute-start.58) | collective-permute-done | bytes 196640 | tf_op jit(solution)/shard_map/ppermute | solution.py:334
  253.4 0.9 reduce_depth.5
  254.3 6.4 %collective-permute-start.60 = (bf16[80,768]{1,0:T(8,128)(2,1)S(1)}, bf16[80,768]{1,0:T(8,128)(2,1)S(1)}, u32[]{:S(2)}, u32[]{:S(2)}) collective-permute-start(bf16[80,768]{1,0:T(8,128)(2,1)S(1)} %get-tuple-element.231), channel_id=1, source_target_pairs={{0,8},{8,0},{16,24},{24,16},{1,9},{9,1},{17,25},{25,17},{2,10},{10... | collective-permute-start | bytes 368648 | tf_op jit(solution)/shard_map/ppermute | solution.py:334
  260.7 2.4 collective-permute-start.62
  263.6 6.4 %collective-permute-done.61 = bf16[80,768]{1,0:T(8,128)(2,1)S(1)} collective-permute-done((bf16[80,768]{1,0:T(8,128)(2,1)S(1)}, bf16[80,768]{1,0:T(8,128)(2,1)S(1)}, u32[]{:S(2)}, u32[]{:S(2)}) %collective-permute-start.61) | collective-permute-done | bytes 122912 | tf_op jit(solution)/shard_map/ppermute | solution.py:334
  (244 shorter events, 22.5 us)
Async XLA Ops:
  2.2 9.4 %collective-permute-start.2 = (bf16[80,768]{1,0:T(8,128)(2,1)S(1)}, bf16[80,768]{1,0:T(8,128)(2,1)S(1)}, u32[]{:S(2)}, u32[]{:S(2)}) collective-permute-start(bf16[80,768]{1,0:T(8,128)(2,1)S(1)} %concatenate.35), channel_id=1, source_target_pairs={{0,24},{8,16},{16,8},{24,0},{1,25},{9,17},{17,9},{25,1},{2,26},{10... | collective-permute-start | bytes 368648 | tf_op jit(solution)/shard_map/ppermute | solution.py:334
  7.3 10.4 %collective-permute-start.1 = (bf16[80,768]{1,0:T(8,128)(2,1)S(1)}, bf16[80,768]{1,0:T(8,128)(2,1)S(1)}, u32[]{:S(2)}, u32[]{:S(2)}) collective-permute-start(bf16[80,768]{1,0:T(8,128)(2,1)S(1)} %concatenate.35), channel_id=1, source_target_pairs={{0,16},{8,24},{16,0},{24,8},{1,17},{9,25},{17,1},{25,9},{2,18},{10... | collective-permute-start | bytes 368648 | tf_op jit(solution)/shard_map/ppermute | solution.py:334
  7.3 10.4 %collective-permute-start = (bf16[80,768]{1,0:T(8,128)(2,1)S(1)}, bf16[80,768]{1,0:T(8,128)(2,1)S(1)}, u32[]{:S(2)}, u32[]{:S(2)}) collective-permute-start(bf16[80,768]{1,0:T(8,128)(2,1)S(1)} %concatenate.35), channel_id=1, source_target_pairs={{0,8},{8,0},{16,24},{24,16},{1,9},{9,1},{17,25},{25,17},{2,10},{10... | collective-permute-start | bytes 368648 | tf_op jit(solution)/shard_map/ppermute | solution.py:334
  18.2 15.7 %collective-permute-start.4 = (bf16[4,80,768]{2,1,0:T(8,128)(2,1)S(1)}, bf16[4,80,768]{2,1,0:T(8,128)(2,1)}, u32[]{:S(2)}, u32[]{:S(2)}) collective-permute-start(bf16[4,80,768]{2,1,0:T(8,128)(2,1)S(1)} %fusion.refs_0_), channel_id=1, source_target_pairs={{0,4},{4,0},{1,5},{5,1},{2,6},{6,2},{3,7},{7,3},{8,12},{12,8},{9,1... | collective-permute-start | bytes 1474568 | tf_op jit(solution)/shard_map/ppermute | solution.py:334
  19.8 14.1 %collective-permute-start.3 = (bf16[4,80,768]{2,1,0:T(8,128)(2,1)S(1)}, bf16[4,80,768]{2,1,0:T(8,128)(2,1)S(1)}, u32[]{:S(2)}, u32[]{:S(2)}) collective-permute-start(bf16[4,80,768]{2,1,0:T(8,128)(2,1)S(1)} %fusion.refs_0_), channel_id=1, source_target_pairs={{0,2},{2,0},{1,3},{3,1},{4,6},{6,4},{5,7},{7,5},{8,10},{10,8},{9,1... | collective-permute-start | bytes 1474568 | tf_op jit(solution)/shard_map/ppermute | solution.py:334
  21.3 16.1 %collective-permute-start.9 = (bf16[4,80,768]{2,1,0:T(8,128)(2,1)S(1)}, bf16[4,80,768]{2,1,0:T(8,128)(2,1)S(1)}, u32[]{:S(2)}, u32[]{:S(2)}) collective-permute-start(bf16[4,80,768]{2,1,0:T(8,128)(2,1)S(1)} %fusion.refs_0_), channel_id=1, source_target_pairs={{0,1},{1,0},{2,3},{3,2},{4,5},{5,4},{6,7},{7,6},{8,9},{9,8},{10,11... | collective-permute-start | bytes 1474568 | tf_op jit(solution)/shard_map/ppermute | solution.py:334
  21.6 12.3 %collective-permute-start.5 = (bf16[128,768]{1,0:T(8,128)(2,1)S(1)}, bf16[128,768]{1,0:T(8,128)(2,1)S(1)}, u32[]{:S(2)}, u32[]{:S(2)}) collective-permute-start(bf16[128,768]{1,0:T(8,128)(2,1)S(1)} %concatenate.34), channel_id=1, source_target_pairs={{0,16},{8,24},{16,0},{24,8},{1,17},{9,25},{17,1},{25,9},{2,18},{10... | collective-permute-start | bytes 589832 | tf_op jit(solution)/shard_map/ppermute | solution.py:334
  34.0 9.1 %collective-permute-start.7 = (bf16[4,48,768]{2,1,0:T(8,128)(2,1)S(1)}, bf16[4,48,768]{2,1,0:T(8,128)(2,1)S(1)}, u32[]{:S(2)}, u32[]{:S(2)}) collective-permute-start(bf16[4,48,768]{2,1,0:T(8,128)(2,1)S(1)} %slice.122), channel_id=1, source_target_pairs={{0,4},{4,0},{1,5},{5,1},{2,6},{6,2},{3,7},{7,3},{8,12},{12,8},{9,1... | collective-permute-start | bytes 884744 | tf_op jit(solution)/shard_map/ppermute | solution.py:334
  34.5 14.7 %collective-permute-start.10 = (bf16[4,80,768]{2,1,0:T(8,128)(2,1)S(1)}, bf16[4,80,768]{2,1,0:T(8,128)(2,1)}, u32[]{:S(2)}, u32[]{:S(2)}) collective-permute-start(bf16[4,80,768]{2,1,0:T(8,128)(2,1)S(1)} %collective-permute-done.3.refs_1_), channel_id=1, source_target_pairs={{0,1},{1,0},{2,3},{3,2},{4,5},{5,4},{6,7},{7,6},{8,9},{9,8},{10,11... | collective-permute-start | bytes 1474568 | tf_op jit(solution)/shard_map/ppermute | solution.py:334
  35.5 13.7 %collective-permute-start.11 = (bf16[4,80,768]{2,1,0:T(8,128)(2,1)}, bf16[4,80,768]{2,1,0:T(8,128)(2,1)}, u32[]{:S(2)}, u32[]{:S(2)}) collective-permute-start(bf16[4,80,768]{2,1,0:T(8,128)(2,1)} %collective-permute-done.4.refs_2_), channel_id=1, source_target_pairs={{0,1},{1,0},{2,3},{3,2},{4,5},{5,4},{6,7},{7,6},{8,9},{9,8},{10,11... | collective-permute-start | bytes 1474568 | tf_op jit(solution)/shard_map/ppermute | solution.py:334
  36.1 7.0 %collective-permute-start.8 = (bf16[4,32,768]{2,1,0:T(8,128)(2,1)S(1)}, bf16[4,32,768]{2,1,0:T(8,128)(2,1)}, u32[]{:S(2)}, u32[]{:S(2)}) collective-permute-start(bf16[4,32,768]{2,1,0:T(8,128)(2,1)S(1)} %slice.123), channel_id=1, source_target_pairs={{0,2},{2,0},{1,3},{3,1},{4,6},{6,4},{5,7},{7,5},{8,10},{10,8},{9,1... | collective-permute-start | bytes 589832 | tf_op jit(solution)/shard_map/ppermute | solution.py:334
  37.4 17.8 %collective-permute-start.6 = (bf16[2,128,768]{2,1,0:T(8,128)(2,1)}, bf16[2,128,768]{2,1,0:T(8,128)(2,1)}, u32[]{:S(2)}, u32[]{:S(2)}) collective-permute-start(bf16[2,128,768]{2,1,0:T(8,128)(2,1)} %get-tuple-element.269), channel_id=1, source_target_pairs={{0,8},{8,0},{16,24},{24,16},{1,9},{9,1},{17,25},{25,17},{2,10},{10... | collective-permute-start | bytes 1179656 | tf_op jit(solution)/shard_map/ppermute | solution.py:334
  43.0 6.2 %collective-permute-start.12 = (bf16[4,48,768]{2,1,0:T(8,128)(2,1)S(1)}, bf16[4,48,768]{2,1,0:T(8,128)(2,1)}, u32[]{:S(2)}, u32[]{:S(2)}) collective-permute-start(bf16[4,48,768]{2,1,0:T(8,128)(2,1)S(1)} %collective-permute-done.7.refs_3_), channel_id=1, source_target_pairs={{0,1},{1,0},{2,3},{3,2},{4,5},{5,4},{6,7},{7,6},{8,9},{9,8},{10,11... | collective-permute-start | bytes 884744 | tf_op jit(solution)/shard_map/ppermute | solution.py:334
  43.0 6.1 %collective-permute-start.13 = (bf16[4,32,768]{2,1,0:T(8,128)(2,1)}, bf16[4,32,768]{2,1,0:T(8,128)(2,1)}, u32[]{:S(2)}, u32[]{:S(2)}) collective-permute-start(bf16[4,32,768]{2,1,0:T(8,128)(2,1)} %collective-permute-done.8.refs_4_), channel_id=1, source_target_pairs={{0,1},{1,0},{2,3},{3,2},{4,5},{5,4},{6,7},{7,6},{8,9},{9,8},{10,11... | collective-permute-start | bytes 589832 | tf_op jit(solution)/shard_map/ppermute | solution.py:334
  54.6 13.6 %collective-permute-start.16 = (bf16[256,768]{1,0:T(8,128)(2,1)S(1)}, bf16[256,768]{1,0:T(8,128)(2,1)S(1)}, u32[]{:S(2)}, u32[]{:S(2)}) collective-permute-start(bf16[256,768]{1,0:T(8,128)(2,1)S(1)} %get-tuple-element.130.k_near), channel_id=1, source_target_pairs={{0,1},{1,0},{2,3},{3,2},{4,5},{5,4},{6,7},{7,6},{8,9},{9,8},{10,11... | collective-permute-start | bytes 1179656 | tf_op jit(solution)/shard_map/ppermute | solution.py:334
  54.8 13.9 %collective-permute-start.17 = (bf16[256,768]{1,0:T(8,128)(2,1)S(1)}, bf16[256,768]{1,0:T(8,128)(2,1)S(1)}, u32[]{:S(2)}, u32[]{:S(2)}) collective-permute-start(bf16[256,768]{1,0:T(8,128)(2,1)S(1)} %get-tuple-element.131.v_near), channel_id=1, source_target_pairs={{0,1},{1,0},{2,3},{3,2},{4,5},{5,4},{6,7},{7,6},{8,9},{9,8},{10,11... | collective-permute-start | bytes 1179656 | tf_op jit(solution)/shard_map/ppermute | solution.py:334
  58.0 25.3 %collective-permute-start.15 = (bf16[4,128,768]{2,1,0:T(8,128)(2,1)S(1)}, bf16[4,128,768]{2,1,0:T(8,128)(2,1)S(1)}, u32[]{:S(2)}, u32[]{:S(2)}) collective-permute-start(bf16[4,128,768]{2,1,0:T(8,128)(2,1)S(1)} %bitcast.106), channel_id=1, source_target_pairs={{0,4},{4,0},{1,5},{5,1},{2,6},{6,2},{3,7},{7,3},{8,12},{12,8},{9,1... | collective-permute-start | bytes 2359304 | tf_op jit(solution)/shard_map/ppermute | solution.py:334
  59.2 24.2 %collective-permute-start.14 = (bf16[4,128,768]{2,1,0:T(8,128)(2,1)S(1)}, bf16[4,128,768]{2,1,0:T(8,128)(2,1)S(1)}, u32[]{:S(2)}, u32[]{:S(2)}) collective-permute-start(bf16[4,128,768]{2,1,0:T(8,128)(2,1)S(1)} %bitcast.107), channel_id=1, source_target_pairs={{0,2},{2,0},{1,3},{3,1},{4,6},{6,4},{5,7},{7,5},{8,10},{10,8},{9,1... | collective-permute-start | bytes 2359304 | tf_op jit(solution)/shard_map/ppermute | solution.py:334
  59.8 8.4 %collective-permute-start.18 = (bf16[96,768]{1,0:T(8,128)(2,1)S(1)}, bf16[96,768]{1,0:T(8,128)(2,1)S(1)}, u32[]{:S(2)}, u32[]{:S(2)}) collective-permute-start(bf16[96,768]{1,0:T(8,128)(2,1)S(1)} %copy-done.46), channel_id=1, source_target_pairs={{0,16},{8,24},{16,0},{24,8},{1,17},{9,25},{17,1},{25,9},{2,18},{10... | collective-permute-start | bytes 442376 | tf_op jit(solution)/shard_map/ppermute | solution.py:334
  68.2 7.9 %collective-permute-start.20 = (bf16[256,768]{1,0:T(8,128)(2,1)S(1)}, bf16[256,768]{1,0:T(8,128)(2,1)S(1)}, u32[]{:S(2)}, u32[]{:S(2)}) collective-permute-start(bf16[256,768]{1,0:T(8,128)(2,1)S(1)} %get-tuple-element.132.k_near), channel_id=1, source_target_pairs={{0,1},{1,0},{2,3},{3,2},{4,5},{5,4},{6,7},{7,6},{8,9},{9,8},{10,11... | collective-permute-start | bytes 1179656 | tf_op jit(solution)/shard_map/ppermute | solution.py:334
  68.2 7.9 %collective-permute-start.21 = (bf16[256,768]{1,0:T(8,128)(2,1)S(1)}, bf16[256,768]{1,0:T(8,128)(2,1)S(1)}, u32[]{:S(2)}, u32[]{:S(2)}) collective-permute-start(bf16[256,768]{1,0:T(8,128)(2,1)S(1)} %get-tuple-element.133.v_near), channel_id=1, source_target_pairs={{0,1},{1,0},{2,3},{3,2},{4,5},{5,4},{6,7},{7,6},{8,9},{9,8},{10,11... | collective-permute-start | bytes 1179656 | tf_op jit(solution)/shard_map/ppermute | solution.py:334
  68.7 14.6 %collective-permute-start.19 = (bf16[2,96,768]{2,1,0:T(8,128)(2,1)S(1)}, bf16[2,96,768]{2,1,0:T(8,128)(2,1)S(1)}, u32[]{:S(2)}, u32[]{:S(2)}) collective-permute-start(bf16[2,96,768]{2,1,0:T(8,128)(2,1)S(1)} %get-tuple-element.271), channel_id=1, source_target_pairs={{0,8},{8,0},{16,24},{24,16},{1,9},{9,1},{17,25},{25,17},{2,10},{10... | collective-permute-start | bytes 884744 | tf_op jit(solution)/shard_map/ppermute | solution.py:334
  83.4 12.2 %collective-permute-start.22 = (bf16[4,72,768]{2,1,0:T(8,128)(2,1)S(1)}, bf16[4,72,768]{2,1,0:T(8,128)(2,1)S(1)}, u32[]{:S(2)}, u32[]{:S(2)}) collective-permute-start(bf16[4,72,768]{2,1,0:T(8,128)(2,1)S(1)} %slice.126), channel_id=1, source_target_pairs={{0,4},{4,0},{1,5},{5,1},{2,6},{6,2},{3,7},{7,3},{8,12},{12,8},{9,1... | collective-permute-start | bytes 1327112 | tf_op jit(solution)/shard_map/ppermute | solution.py:334
  84.1 9.9 %collective-permute-start.23 = (bf16[4,56,768]{2,1,0:T(8,128)(2,1)S(1)}, bf16[4,56,768]{2,1,0:T(8,128)(2,1)S(1)}, u32[]{:S(2)}, u32[]{:S(2)}) collective-permute-start(bf16[4,56,768]{2,1,0:T(8,128)(2,1)S(1)} %slice.127), channel_id=1, source_target_pairs={{0,2},{2,0},{1,3},{3,1},{4,6},{6,4},{5,7},{7,5},{8,10},{10,8},{9,1... | collective-permute-start | bytes 1032200 | tf_op jit(solution)/shard_map/ppermute | solution.py:334
  85.6 12.5 %collective-permute-start.26 = (bf16[4,128,768]{2,1,0:T(8,128)(2,1)S(1)}, bf16[4,128,768]{2,1,0:T(8,128)(2,1)S(1)}, u32[]{:S(2)}, u32[]{:S(2)}) collective-permute-start(bf16[4,128,768]{2,1,0:T(8,128)(2,1)S(1)} %bitcast.108), channel_id=1, source_target_pairs={{0,1},{1,0},{2,3},{3,2},{4,5},{5,4},{6,7},{7,6},{8,9},{9,8},{10,11... | collective-permute-start | bytes 2359304 | tf_op jit(solution)/shard_map/ppermute | solution.py:334
  85.6 12.6 %collective-permute-start.27 = (bf16[4,128,768]{2,1,0:T(8,128)(2,1)S(1)}, bf16[4,128,768]{2,1,0:T(8,128)(2,1)S(1)}, u32[]{:S(2)}, u32[]{:S(2)}) collective-permute-start(bf16[4,128,768]{2,1,0:T(8,128)(2,1)S(1)} %collective-permute-done.14.refs_1_), channel_id=1, source_target_pairs={{0,1},{1,0},{2,3},{3,2},{4,5},{5,4},{6,7},{7,6},{8,9},{9,8},{10,11... | collective-permute-start | bytes 2359304 | tf_op jit(solution)/shard_map/ppermute | solution.py:334
  86.1 12.6 %collective-permute-start.28 = (bf16[4,128,768]{2,1,0:T(8,128)(2,1)S(1)}, bf16[4,128,768]{2,1,0:T(8,128)(2,1)S(1)}, u32[]{:S(2)}, u32[]{:S(2)}) collective-permute-start(bf16[4,128,768]{2,1,0:T(8,128)(2,1)S(1)} %collective-permute-done.15.refs_2_), channel_id=1, source_target_pairs={{0,1},{1,0},{2,3},{3,2},{4,5},{5,4},{6,7},{7,6},{8,9},{9,8},{10,11... | collective-permute-start | bytes 2359304 | tf_op jit(solution)/shard_map/ppermute | solution.py:334
  93.9 2.7 %collective-permute-start.30 = (bf16[4,56,768]{2,1,0:T(8,128)(2,1)S(1)}, bf16[4,56,768]{2,1,0:T(8,128)(2,1)S(1)}, u32[]{:S(2)}, u32[]{:S(2)}) collective-permute-start(bf16[4,56,768]{2,1,0:T(8,128)(2,1)S(1)} %collective-permute-done.23.refs_7_), channel_id=1, source_target_pairs={{0,1},{1,0},{2,3},{3,2},{4,5},{5,4},{6,7},{7,6},{8,9},{9,8},{10,11... | collective-permute-start | bytes 1032200 | tf_op jit(solution)/shard_map/ppermute | solution.py:334
  96.0 32.5 %copy-start.30 = (bf16[2,2,96,768]{3,2,1,0:T(8,128)(2,1)}, bf16[2,2,96,768]{3,2,1,0:T(8,128)(2,1)S(1)}, u32[]{:S(2)}) copy-start(bf16[2,2,96,768]{3,2,1,0:T(8,128)(2,1)S(1)} %copy.39) | copy-start | bytes 1769476
  96.1 20.5 %collective-permute-start.25 = (bf16[4,96,768]{2,1,0:T(8,128)(2,1)S(1)}, bf16[4,96,768]{2,1,0:T(8,128)(2,1)S(1)}, u32[]{:S(2)}, u32[]{:S(2)}) collective-permute-start(bf16[4,96,768]{2,1,0:T(8,128)(2,1)S(1)} %bitcast.113), channel_id=1, source_target_pairs={{0,4},{4,0},{1,5},{5,1},{2,6},{6,2},{3,7},{7,3},{8,12},{12,8},{9,1... | collective-permute-start | bytes 1769480 | tf_op jit(solution)/shard_map/ppermute | solution.py:334
  96.7 19.9 %collective-permute-start.24 = (bf16[4,96,768]{2,1,0:T(8,128)(2,1)S(1)}, bf16[4,96,768]{2,1,0:T(8,128)(2,1)S(1)}, u32[]{:S(2)}, u32[]{:S(2)}) collective-permute-start(bf16[4,96,768]{2,1,0:T(8,128)(2,1)S(1)} %bitcast.114), channel_id=1, source_target_pairs={{0,2},{2,0},{1,3},{3,1},{4,6},{6,4},{5,7},{7,5},{8,10},{10,8},{9,1... | collective-permute-start | bytes 1769480 | tf_op jit(solution)/shard_map/ppermute | solution.py:334
  98.2 1.9 collective-permute-start.29
  98.3 28.7 %collective-permute-start.33 = (bf16[4,96,768]{2,1,0:T(8,128)(2,1)S(1)}, bf16[4,96,768]{2,1,0:T(8,128)(2,1)S(1)}, u32[]{:S(2)}, u32[]{:S(2)}) collective-permute-start(bf16[4,96,768]{2,1,0:T(8,128)(2,1)S(1)} %bitcast.115), channel_id=1, source_target_pairs={{0,1},{1,0},{2,3},{3,2},{4,5},{5,4},{6,7},{7,6},{8,9},{9,8},{10,11... | collective-permute-start | bytes 1769480 | tf_op jit(solution)/shard_map/ppermute | solution.py:334
  116.6 10.3 %collective-permute-start.34 = (bf16[4,96,768]{2,1,0:T(8,128)(2,1)S(1)}, bf16[4,96,768]{2,1,0:T(8,128)(2,1)S(1)}, u32[]{:S(2)}, u32[]{:S(2)}) collective-permute-start(bf16[4,96,768]{2,1,0:T(8,128)(2,1)S(1)} %collective-permute-done.24.refs_1_), channel_id=1, source_target_pairs={{0,1},{1,0},{2,3},{3,2},{4,5},{5,4},{6,7},{7,6},{8,9},{9,8},{10,11... | collective-permute-start | bytes 1769480 | tf_op jit(solution)/shard_map/ppermute | solution.py:334
  116.9 9.3 %collective-permute-start.32 = (bf16[4,48,768]{2,1,0:T(8,128)(2,1)S(1)}, bf16[4,48,768]{2,1,0:T(8,128)(2,1)S(1)}, u32[]{:S(2)}, u32[]{:S(2)}) collective-permute-start(bf16[4,48,768]{2,1,0:T(8,128)(2,1)S(1)} %slice.131), channel_id=1, source_target_pairs={{0,2},{2,0},{1,3},{3,1},{4,6},{6,4},{5,7},{7,5},{8,10},{10,8},{9,1... | collective-permute-start | bytes 884744 | tf_op jit(solution)/shard_map/ppermute | solution.py:334
  117.5 9.5 %collective-permute-start.35 = (bf16[4,96,768]{2,1,0:T(8,128)(2,1)S(1)}, bf16[4,96,768]{2,1,0:T(8,128)(2,1)S(1)}, u32[]{:S(2)}, u32[]{:S(2)}) collective-permute-start(bf16[4,96,768]{2,1,0:T(8,128)(2,1)S(1)} %collective-permute-done.25.refs_2_), channel_id=1, source_target_pairs={{0,1},{1,0},{2,3},{3,2},{4,5},{5,4},{6,7},{7,6},{8,9},{9,8},{10,11... | collective-permute-start | bytes 1769480 | tf_op jit(solution)/shard_map/ppermute | solution.py:334
  117.6 9.4 %collective-permute-start.31 = (bf16[4,48,768]{2,1,0:T(8,128)(2,1)S(1)}, bf16[4,48,768]{2,1,0:T(8,128)(2,1)S(1)}, u32[]{:S(2)}, u32[]{:S(2)}) collective-permute-start(bf16[4,48,768]{2,1,0:T(8,128)(2,1)S(1)} %slice.130), channel_id=1, source_target_pairs={{0,4},{4,0},{1,5},{5,1},{2,6},{6,2},{3,7},{7,3},{8,12},{12,8},{9,1... | collective-permute-start | bytes 884744 | tf_op jit(solution)/shard_map/ppermute | solution.py:334
  126.2 1.6 collective-permute-start.37
  126.9 1.6 collective-permute-start.36
  149.3 9.3 %collective-permute-start.38 = (bf16[16,96,768]{2,1,0:T(8,128)(2,1)S(1)}, bf16[16,96,768]{2,1,0:T(8,128)(2,1)S(1)}, u32[]{:S(2)}, u32[]{:S(2)}) collective-permute-start(bf16[16,96,768]{2,1,0:T(8,128)(2,1)S(1)} %get-tuple-element.167), channel_id=1, source_target_pairs={{0,1},{1,0},{2,3},{3,2},{4,5},{5,4},{6,7},{7,6},{8,9},{9,8},{10,11... | collective-permute-start | bytes 7077896 | tf_op jit(solution)/shard_map/ppermute | solution.py:334
  159.2 11.4 %collective-permute-start.39 = (bf16[4,48,768]{2,1,0:T(8,128)(2,1)S(1)}, bf16[4,48,768]{2,1,0:T(8,128)(2,1)S(1)}, u32[]{:S(2)}, u32[]{:S(2)}) collective-permute-start(bf16[4,48,768]{2,1,0:T(8,128)(2,1)S(1)} %get-tuple-element.169), channel_id=1, source_target_pairs={{0,2},{2,0},{1,3},{3,1},{4,6},{6,4},{5,7},{7,5},{8,10},{10,8},{9,1... | collective-permute-start | bytes 884744 | tf_op jit(solution)/shard_map/ppermute | solution.py:334
  160.8 9.9 %collective-permute-start.40 = (bf16[4,48,768]{2,1,0:T(8,128)(2,1)S(1)}, bf16[4,48,768]{2,1,0:T(8,128)(2,1)S(1)}, u32[]{:S(2)}, u32[]{:S(2)}) collective-permute-start(bf16[4,48,768]{2,1,0:T(8,128)(2,1)S(1)} %get-tuple-element.170), channel_id=1, source_target_pairs={{0,4},{4,0},{1,5},{5,1},{2,6},{6,2},{3,7},{7,3},{8,12},{12,8},{9,1... | collective-permute-start | bytes 884744 | tf_op jit(solution)/shard_map/ppermute | solution.py:334
  170.7 11.3 %collective-permute-start.41 = (bf16[16,128,768]{2,1,0:T(8,128)(2,1)S(1)}, bf16[16,128,768]{2,1,0:T(8,128)(2,1)S(1)}, u32[]{:S(2)}, u32[]{:S(2)}) collective-permute-start(bf16[16,128,768]{2,1,0:T(8,128)(2,1)S(1)} %get-tuple-element.178), channel_id=1, source_target_pairs={{0,1},{1,0},{2,3},{3,2},{4,5},{5,4},{6,7},{7,6},{8,9},{9,8},{10,11... | collective-permute-start | bytes 9437192 | tf_op jit(solution)/shard_map/ppermute | solution.py:334
  171.7 23.5 %collective-permute-start.44 = (bf16[4,96,768]{2,1,0:T(8,128)(2,1)S(1)}, bf16[4,96,768]{2,1,0:T(8,128)(2,1)S(1)}, u32[]{:S(2)}, u32[]{:S(2)}) collective-permute-start(bf16[4,96,768]{2,1,0:T(8,128)(2,1)S(1)} %get-tuple-element.179), channel_id=1, source_target_pairs={{0,4},{4,0},{1,5},{5,1},{2,6},{6,2},{3,7},{7,3},{8,12},{12,8},{9,1... | collective-permute-start | bytes 1769480 | tf_op jit(solution)/shard_map/ppermute | solution.py:334
  172.3 22.9 %collective-permute-start.45 = (bf16[4,96,768]{2,1,0:T(8,128)(2,1)S(1)}, bf16[4,96,768]{2,1,0:T(8,128)(2,1)S(1)}, u32[]{:S(2)}, u32[]{:S(2)}) collective-permute-start(bf16[4,96,768]{2,1,0:T(8,128)(2,1)S(1)} %get-tuple-element.180), channel_id=1, source_target_pairs={{0,2},{2,0},{1,3},{3,1},{4,6},{6,4},{5,7},{7,5},{8,10},{10,8},{9,1... | collective-permute-start | bytes 1769480 | tf_op jit(solution)/shard_map/ppermute | solution.py:334
  182.8 14.5 %collective-permute-start.42 = (bf16[4,72,768]{2,1,0:T(8,128)(2,1)S(1)}, bf16[4,72,768]{2,1,0:T(8,128)(2,1)S(1)}, u32[]{:S(2)}, u32[]{:S(2)}) collective-permute-start(bf16[4,72,768]{2,1,0:T(8,128)(2,1)S(1)} %get-tuple-element.186), channel_id=1, source_target_pairs={{0,2},{2,0},{1,3},{3,1},{4,6},{6,4},{5,7},{7,5},{8,10},{10,8},{9,1... | collective-permute-start | bytes 1327112 | tf_op jit(solution)/shard_map/ppermute | solution.py:334
  184.3 10.9 %collective-permute-start.43 = (bf16[4,56,768]{2,1,0:T(8,128)(2,1)S(1)}, bf16[4,56,768]{2,1,0:T(8,128)(2,1)S(1)}, u32[]{:S(2)}, u32[]{:S(2)}) collective-permute-start(bf16[4,56,768]{2,1,0:T(8,128)(2,1)S(1)} %get-tuple-element.187), channel_id=1, source_target_pairs={{0,4},{4,0},{1,5},{5,1},{2,6},{6,2},{3,7},{7,3},{8,12},{12,8},{9,1... | collective-permute-start | bytes 1032200 | tf_op jit(solution)/shard_map/ppermute | solution.py:334
  197.2 4.1 %collective-permute-start.46 = (bf16[2,2,256,768]{3,2,1,0:T(8,128)(2,1)S(1)}, bf16[2,2,256,768]{3,2,1,0:T(8,128)(2,1)S(1)}, u32[]{:S(2)}, u32[]{:S(2)}) collective-permute-start(bf16[2,2,256,768]{3,2,1,0:T(8,128)(2,1)S(1)} %get-tuple-element.196), channel_id=1, source_target_pairs={{0,1},{1,0},{2,3},{3,2},{4,5},{5,4},{6,7},{7,6},{8,9},{9,8},{10,11... | collective-permute-start | bytes 4718600 | tf_op jit(solution)/shard_map/ppermute | solution.py:334
  198.3 20.0 %collective-permute-start.47 = (bf16[4,128,768]{2,1,0:T(8,128)(2,1)S(1)}, bf16[4,128,768]{2,1,0:T(8,128)(2,1)S(1)}, u32[]{:S(2)}, u32[]{:S(2)}) collective-permute-start(bf16[4,128,768]{2,1,0:T(8,128)(2,1)S(1)} %get-tuple-element.197), channel_id=1, source_target_pairs={{0,4},{4,0},{1,5},{5,1},{2,6},{6,2},{3,7},{7,3},{8,12},{12,8},{9,1... | collective-permute-start | bytes 2359304 | tf_op jit(solution)/shard_map/ppermute | solution.py:334
  199.8 19.7 %collective-permute-start.48 = (bf16[4,128,768]{2,1,0:T(8,128)(2,1)S(1)}, bf16[4,128,768]{2,1,0:T(8,128)(2,1)S(1)}, u32[]{:S(2)}, u32[]{:S(2)}) collective-permute-start(bf16[4,128,768]{2,1,0:T(8,128)(2,1)S(1)} %get-tuple-element.198), channel_id=1, source_target_pairs={{0,2},{2,0},{1,3},{3,1},{4,6},{6,4},{5,7},{7,5},{8,10},{10,8},{9,1... | collective-permute-start | bytes 2359304 | tf_op jit(solution)/shard_map/ppermute | solution.py:334
  219.5 4.4 %collective-permute-start.49 = (bf16[16,80,768]{2,1,0:T(8,128)(2,1)S(1)}, bf16[16,80,768]{2,1,0:T(8,128)(2,1)S(1)}, u32[]{:S(2)}, u32[]{:S(2)}) collective-permute-start(bf16[16,80,768]{2,1,0:T(8,128)(2,1)S(1)} %get-tuple-element.209), channel_id=1, source_target_pairs={{0,1},{1,0},{2,3},{3,2},{4,5},{5,4},{6,7},{7,6},{8,9},{9,8},{10,11... | collective-permute-start | bytes 5898248 | tf_op jit(solution)/shard_map/ppermute | solution.py:334
  219.5 9.0 %collective-permute-start.52 = (bf16[96,768]{1,0:T(8,128)(2,1)S(1)}, bf16[96,768]{1,0:T(8,128)(2,1)S(1)}, u32[]{:S(2)}, u32[]{:S(2)}) collective-permute-start(bf16[96,768]{1,0:T(8,128)(2,1)S(1)} %get-tuple-element.199), channel_id=1, source_target_pairs={{0,8},{8,0},{16,24},{24,16},{1,9},{9,1},{17,25},{25,17},{2,10},{10... | collective-permute-start | bytes 442376 | tf_op jit(solution)/shard_map/ppermute | solution.py:334
  221.2 14.0 %collective-permute-start.53 = (bf16[96,768]{1,0:T(8,128)(2,1)S(1)}, bf16[96,768]{1,0:T(8,128)(2,1)S(1)}, u32[]{:S(2)}, u32[]{:S(2)}) collective-permute-start(bf16[96,768]{1,0:T(8,128)(2,1)S(1)} %get-tuple-element.200), channel_id=1, source_target_pairs={{0,16},{8,24},{16,0},{24,8},{1,17},{9,25},{17,1},{25,9},{2,18},{10... | collective-permute-start | bytes 442376 | tf_op jit(solution)/shard_map/ppermute | solution.py:334
  222.5 12.7 %collective-permute-start.54 = (bf16[96,768]{1,0:T(8,128)(2,1)S(1)}, bf16[96,768]{1,0:T(8,128)(2,1)S(1)}, u32[]{:S(2)}, u32[]{:S(2)}) collective-permute-start(bf16[96,768]{1,0:T(8,128)(2,1)S(1)} %get-tuple-element.201), channel_id=1, source_target_pairs={{0,24},{8,16},{16,8},{24,0},{1,25},{9,17},{17,9},{25,1},{2,26},{10... | collective-permute-start | bytes 442376 | tf_op jit(solution)/shard_map/ppermute | solution.py:334
  224.5 13.9 %collective-permute-start.50 = (bf16[4,48,768]{2,1,0:T(8,128)(2,1)S(1)}, bf16[4,48,768]{2,1,0:T(8,128)(2,1)S(1)}, u32[]{:S(2)}, u32[]{:S(2)}) collective-permute-start(bf16[4,48,768]{2,1,0:T(8,128)(2,1)S(1)} %get-tuple-element.210), channel_id=1, source_target_pairs={{0,2},{2,0},{1,3},{3,1},{4,6},{6,4},{5,7},{7,5},{8,10},{10,8},{9,1... | collective-permute-start | bytes 884744 | tf_op jit(solution)/shard_map/ppermute | solution.py:334
  225.2 13.3 %collective-permute-start.51 = (bf16[4,32,768]{2,1,0:T(8,128)(2,1)S(1)}, bf16[4,32,768]{2,1,0:T(8,128)(2,1)S(1)}, u32[]{:S(2)}, u32[]{:S(2)}) collective-permute-start(bf16[4,32,768]{2,1,0:T(8,128)(2,1)S(1)} %get-tuple-element.211), channel_id=1, source_target_pairs={{0,4},{4,0},{1,5},{5,1},{2,6},{6,2},{3,7},{7,3},{8,12},{12,8},{9,1... | collective-permute-start | bytes 589832 | tf_op jit(solution)/shard_map/ppermute | solution.py:334
  228.5 12.0 %collective-permute-start.57 = (bf16[128,768]{1,0:T(8,128)(2,1)S(1)}, bf16[128,768]{1,0:T(8,128)(2,1)S(1)}, u32[]{:S(2)}, u32[]{:S(2)}) collective-permute-start(bf16[128,768]{1,0:T(8,128)(2,1)S(1)} %get-tuple-element.214), channel_id=1, source_target_pairs={{0,8},{8,0},{16,24},{24,16},{1,9},{9,1},{17,25},{25,17},{2,10},{10... | collective-permute-start | bytes 589832 | tf_op jit(solution)/shard_map/ppermute | solution.py:334
  235.2 16.1 %collective-permute-start.58 = (bf16[128,768]{1,0:T(8,128)(2,1)S(1)}, bf16[128,768]{1,0:T(8,128)(2,1)S(1)}, u32[]{:S(2)}, u32[]{:S(2)}) collective-permute-start(bf16[128,768]{1,0:T(8,128)(2,1)S(1)} %get-tuple-element.215), channel_id=1, source_target_pairs={{0,16},{8,24},{16,0},{24,8},{1,17},{9,25},{17,1},{25,9},{2,18},{10... | collective-permute-start | bytes 589832 | tf_op jit(solution)/shard_map/ppermute | solution.py:334
  235.2 16.1 %collective-permute-start.59 = (bf16[128,768]{1,0:T(8,128)(2,1)S(1)}, bf16[128,768]{1,0:T(8,128)(2,1)S(1)}, u32[]{:S(2)}, u32[]{:S(2)}) collective-permute-start(bf16[128,768]{1,0:T(8,128)(2,1)S(1)} %get-tuple-element.216), channel_id=1, source_target_pairs={{0,24},{8,16},{16,8},{24,0},{1,25},{9,17},{17,9},{25,1},{2,26},{10... | collective-permute-start | bytes 589832 | tf_op jit(solution)/shard_map/ppermute | solution.py:334
  239.3 14.1 %collective-permute-start.55 = (bf16[4,80,768]{2,1,0:T(8,128)(2,1)S(1)}, bf16[4,80,768]{2,1,0:T(8,128)(2,1)S(1)}, u32[]{:S(2)}, u32[]{:S(2)}) collective-permute-start(bf16[4,80,768]{2,1,0:T(8,128)(2,1)S(1)} %get-tuple-element.222), channel_id=1, source_target_pairs={{0,4},{4,0},{1,5},{5,1},{2,6},{6,2},{3,7},{7,3},{8,12},{12,8},{9,1... | collective-permute-start | bytes 1474568 | tf_op jit(solution)/shard_map/ppermute | solution.py:334
  239.9 13.4 %collective-permute-start.56 = (bf16[4,80,768]{2,1,0:T(8,128)(2,1)S(1)}, bf16[4,80,768]{2,1,0:T(8,128)(2,1)S(1)}, u32[]{:S(2)}, u32[]{:S(2)}) collective-permute-start(bf16[4,80,768]{2,1,0:T(8,128)(2,1)S(1)} %get-tuple-element.223), channel_id=1, source_target_pairs={{0,2},{2,0},{1,3},{3,1},{4,6},{6,4},{5,7},{7,5},{8,10},{10,8},{9,1... | collective-permute-start | bytes 1474568 | tf_op jit(solution)/shard_map/ppermute | solution.py:334
  254.3 9.3 %collective-permute-start.60 = (bf16[80,768]{1,0:T(8,128)(2,1)S(1)}, bf16[80,768]{1,0:T(8,128)(2,1)S(1)}, u32[]{:S(2)}, u32[]{:S(2)}) collective-permute-start(bf16[80,768]{1,0:T(8,128)(2,1)S(1)} %get-tuple-element.231), channel_id=1, source_target_pairs={{0,8},{8,0},{16,24},{24,16},{1,9},{9,1},{17,25},{25,17},{2,10},{10... | collective-permute-start | bytes 368648 | tf_op jit(solution)/shard_map/ppermute | solution.py:334
  260.7 9.4 %collective-permute-start.61 = (bf16[80,768]{1,0:T(8,128)(2,1)S(1)}, bf16[80,768]{1,0:T(8,128)(2,1)S(1)}, u32[]{:S(2)}, u32[]{:S(2)}) collective-permute-start(bf16[80,768]{1,0:T(8,128)(2,1)S(1)} %get-tuple-element.232), channel_id=1, source_target_pairs={{0,16},{8,24},{16,0},{24,8},{1,17},{9,25},{17,1},{25,9},{2,18},{10... | collective-permute-start | bytes 368648 | tf_op jit(solution)/shard_map/ppermute | solution.py:334
  260.7 9.4 %collective-permute-start.62 = (bf16[80,768]{1,0:T(8,128)(2,1)S(1)}, bf16[80,768]{1,0:T(8,128)(2,1)S(1)}, u32[]{:S(2)}, u32[]{:S(2)}) collective-permute-start(bf16[80,768]{1,0:T(8,128)(2,1)S(1)} %get-tuple-element.233), channel_id=1, source_target_pairs={{0,24},{8,16},{16,8},{24,0},{1,25},{9,17},{17,9},{25,1},{2,26},{10... | collective-permute-start | bytes 368648 | tf_op jit(solution)/shard_map/ppermute | solution.py:334
  (55 other events, 384.3 us)

commit v3 on v2

--- a/solution.py
+++ b/solution.py
@@ -315,6 +315,7 @@
 ANY = pl.BlockSpec(memory_space=pl.ANY)
 WHOLE = pl.BlockSpec(memory_space=pltpu.VMEM)
 MIB = 2**20
+PARTS = (2, 1)
 
 
 def dot_t(left_side, right_side):
@@ -350,18 +351,6 @@
 
 def hold(values, *earlier):
     return lax.optimization_barrier(tuple(values) + earlier)[: len(values)]
-
-
-def gather_z(own, other):
-    return jnp.stack([own, other])
-
-
-def order_z(pair, received):
-    z = lax.axis_index("z")
-    square = jnp.stack([pair, received], axis=1)
-    square = swap_if((z & 1) == 1, square, 1)
-    square = swap_if((z & 2) == 2, square, 0)
-    return square.reshape((4,) + pair.shape[1:])
 
 
 def select_z(shard, received):
@@ -377,6 +366,15 @@
     for term in terms[1:]:
         total = total + term.astype(f32)
     return total
+
+
+def divide(plan, cut):
+    parts = []
+    for start, rows, out, row, column in plan:
+        ends = [start, cut, start + rows] if start < cut < start + rows else [start, start + rows]
+        for first, last in zip(ends, ends[1:]):
+            parts.append((first, last - first, out, row + first - start, column))
+    return parts
 
 
 class Weights:
@@ -484,18 +482,19 @@
     turned[...] = jnp.dot(turn_matrix(tokens), hidden[...], preferred_element_type=f32).astype(bf16)
     quarter = width // 4
     for words, keep in ((output_words, keep_output), (feed_words, keep_feed)):
-        packed = words[...]
+        packed = words[0, 0]
         total = jnp.zeros((tokens, width), f32)
         for i in range(4):
             bit = ((packed & (7 << (3 * i))) != 0).astype(f32).astype(bf16)
             place = (iota((quarter, width), 1) == 4 * iota((quarter, width), 0) + i).astype(bf16)
-            total = total + jnp.dot(bit, place, preferred_element_type=f32)
+            total = total + t_dot(bit, place)
         keep[...] = total.astype(bf16)
 
 
 def prepare(ids, hidden, output_words, feed_words, tokens):
     rows, width = hidden.shape
-    wide, narrow = rows_spec(tokens, width), rows_spec(tokens, width // 4)
+    wide = rows_spec(tokens, width)
+    narrow = pl.BlockSpec((1, 1, width // 4, tokens), lambda i, ids: (i, 0, 0, 0))
     return call(
         prepare_body,
         "prepare",
@@ -514,8 +513,8 @@
     count = len(weights.operands)
     sources, (hidden, turned, queries), rest = refs[:count], refs[count : count + 3], refs[count + 3 :]
     micro, tokens, width = queries.shape
-    near, rest = rest[: 2 * micro], rest[2 * micro :]
-    places, sems = rest[:-1], rest[-1]
+    places, sems = rest[len(rest) - 1 - len(weights.shapes) : -1], rest[-1]
+    near = iter(rest[: len(rest) - 1 - len(weights.shapes)])
     copies = weights.copies(ids, sources, places, sems)
     begin(copies)
     finish(copies[3])
@@ -526,10 +525,12 @@
         natural, other = hidden[m * tokens : (m + 1) * tokens, :], turned[m * tokens : (m + 1) * tokens, :]
         q = jnp.dot(natural, weights.matrix(places, 0)[...], preferred_element_type=f32) + bias[:, :width]
         queries[m] = q.astype(bf16)
-        k = jnp.dot(other, weights.matrix(places, 1)[...], preferred_element_type=f32)
-        near[2 * m][...] = k.astype(bf16)
+        k = jnp.dot(other, weights.matrix(places, 1)[...], preferred_element_type=f32).astype(bf16)
         v = jnp.dot(other, weights.matrix(places, 2)[...], preferred_element_type=f32) + bias[:, width:]
-        near[2 * m + 1][...] = v.astype(bf16)
+        for value in (k, v.astype(bf16)):
+            rows = tokens // PARTS[m]
+            for part in range(PARTS[m]):
+                next(near)[...] = value[part * rows : (part + 1) * rows]
 
 
 def project(ids, weights, hidden, turned, micro, per):
@@ -540,8 +541,9 @@
         (1,),
         (ids, *weights.operands, hidden, turned),
         weights.specs + [WHOLE] * 2,
-        [shaped((micro, rows // micro, width), bf16)] + [shaped((rows // micro, width), bf16)] * (2 * micro),
-        [WHOLE] * (1 + 2 * micro),
+        [shaped((micro, rows // micro, width), bf16)]
+        + [shaped((rows // micro // PARTS[m], width), bf16) for m in range(micro) for _ in range(2 * PARTS[m])],
+        [WHOLE] * (1 + 2 * sum(PARTS)),
         weights.scratch,
         16,
         10,
@@ -553,19 +555,22 @@
 
 
 def join_keys(core, near, far, buffer):
-    quarter = near.shape[0] // 4
+    quarter = buffer.shape[0] // 8
+    parts = len(near)
     for i in range(4):
         here = pl.multiple_of((2 * i + core) * quarter, quarter)
         there = pl.multiple_of((2 * i + 1 - core) * quarter, quarter)
-        buffer[pl.ds(here, quarter), :] = near[i * quarter : (i + 1) * quarter, :]
-        buffer[pl.ds(there, quarter), :] = far[i * quarter : (i + 1) * quarter, :]
-
-
-def attention_body(ids, q, k_near, v_near, k_far, v_far, words, *refs):
+        at = (i * parts % 4) // parts * quarter
+        buffer[pl.ds(here, quarter), :] = near[i * parts // 4][at : at + quarter, :]
+        buffer[pl.ds(there, quarter), :] = far[i * parts // 4][at : at + quarter, :]
+
+
+def attention_body(parts, ids, q, *refs):
+    ours, words = refs[: 4 * parts], refs[4 * parts]
     context, signed, keys, values = refs[-4:]
     core = ids[0]
-    join_keys(core, k_near, k_far, keys)
-    join_keys(core, v_near, v_far, values)
+    join_keys(core, ours[:parts], ours[2 * parts : 3 * parts], keys)
+    join_keys(core, ours[parts : 2 * parts], ours[3 * parts :], values)
     queries = q[0]
     left = lane_half(queries.shape)
     zero = jnp.zeros_like(queries)
@@ -597,14 +602,14 @@
     micro, tokens, width = queries.shape
     pairs = width // 128
     part = pl.BlockSpec((1, tokens, 128), lambda p, ids: (m, 0, p))
-    flat = pl.BlockSpec((tokens, 128), lambda p, ids: (0, p))
-    operands = (ids, queries, *near[2 * m : 2 * m + 2], *far[2 * m : 2 * m + 2], words)
-    return call(
-        attention_body,
+    flat = pl.BlockSpec((tokens // PARTS[m], 128), lambda p, ids: (0, p))
+    operands = (ids, queries, *near[m], *far[m], words)
+    return call(
+        functools.partial(attention_body, PARTS[m]),
         "attention",
         (pairs,),
         operands + tuple(earlier),
-        [part] + [flat] * 4
+        [part] + [flat] * (4 * PARTS[m])
         + [pl.BlockSpec((1, 2, tokens, 128), lambda p, ids: (m, p, 0, 0))]
         + [ANY] * len(earlier),
         [shaped((micro, tokens, width), bf16), shaped((micro, pairs, 2, 4, tokens, 128), bf16)],
@@ -616,11 +621,12 @@
     )
 
 
-def attention_back_body(ids, q, k_near, v_near, k_far, v_far, signed, upstream, *refs):
+def attention_back_body(parts, ids, q, *refs):
+    ours, signed, upstream = refs[: 4 * parts], refs[4 * parts], refs[4 * parts + 1]
     g_q, g_near, g_far, keys, values, sums = refs[-6:]
     core = ids[0]
-    join_keys(core, k_near, k_far, keys)
-    join_keys(core, v_near, v_far, values)
+    join_keys(core, ours[:parts], ours[2 * parts : 3 * parts], keys)
+    join_keys(core, ours[parts : 2 * parts], ours[3 * parts :], values)
     queries = q[0]
     above = upstream[...]
     left = lane_half(queries.shape)
@@ -668,15 +674,15 @@
     micro, tokens, width = queries.shape
     pairs = width // 128
     part = pl.BlockSpec((1, tokens, 128), lambda p, ids: (m, 0, p))
-    flat = pl.BlockSpec((tokens, 128), lambda p, ids: (0, p))
+    flat = pl.BlockSpec((tokens // PARTS[m], 128), lambda p, ids: (0, p))
     both = pl.BlockSpec((2, 1, tokens, 128), lambda p, ids: (0, m, 0, p))
-    operands = (ids, queries, *near[2 * m : 2 * m + 2], *far[2 * m : 2 * m + 2], signed, upstream)
-    return call(
-        attention_back_body,
+    operands = (ids, queries, *near[m], *far[m], signed, upstream)
+    return call(
+        functools.partial(attention_back_body, PARTS[m]),
         "attention_back",
         (pairs,),
         operands + tuple(earlier),
-        [part] + [flat] * 4
+        [part] + [flat] * (4 * PARTS[m])
         + [pl.BlockSpec((1, 1, 2, 4, tokens, 128), lambda p, ids: (m, p, 0, 0, 0, 0))]
         + [pl.BlockSpec((tokens, 128), lambda p, ids: (m, p))]
         + [ANY] * len(earlier),
@@ -852,7 +858,7 @@
         ],
         [narrow, narrow, broad, WHOLE, WHOLE, WHOLE],
         weights.scratch + [pltpu.VMEM((width, width), f32), pltpu.VMEM((rows, width), bf16)],
-        40,
+        30,
         36,
     )
 
@@ -1103,6 +1109,47 @@
         10,
         3,
     )
+
+
+def pair_body(ids, one, two, out):
+    out[0] = one[...]
+    out[1] = two[...]
+
+
+def pair_z(ids, one, two):
+    return call(
+        pair_body,
+        "pair_z",
+        (1,),
+        (ids, one, two),
+        [WHOLE] * 2,
+        [shaped((2,) + one.shape, bf16)],
+        [WHOLE],
+        [],
+        4,
+        1,
+    )[0]
+
+
+def order_body(ids, pair, received, out):
+    for k in range(2):
+        out[ids[3] ^ (2 * k)] = pair[k]
+        out[ids[3] ^ (2 * k + 1)] = received[k]
+
+
+def order_z(ids, pair, received):
+    return call(
+        order_body,
+        "order_z",
+        (1,),
+        (ids, pair, received),
+        [WHOLE] * 2,
+        [shaped((4,) + pair.shape[1:], bf16)],
+        [WHOLE],
+        [],
+        6,
+        1,
+    )[0]
 
 
 def exchange_z(sends):
@@ -1155,44 +1202,46 @@
     )
     shard_b = after(shard_b, own_a)
     far_b = pp(shard_b, "z", 2)
-    x_a, y_a, far_b = hold((x_a, y_a, far_b))
-    cut_a = 2 * own
+    turned, keep_output, keep_feed = prepare(
+        ids, after(hidden, own_a), output_keep.transpose(0, 1, 3, 2), feed_keep.transpose(0, 1, 3, 2), tokens
+    )
+    x_a, y_a, far_b = hold((x_a, y_a, far_b), turned)
+    cut_a = shard_a.shape[0] // 2
     low_a, high_a = pp(x_a[:, :cut_a], "y"), pp(y_a[:, cut_a:], "x")
     pieces = [(0, 0, own_a), (1, 0, x_a), (2, 0, y_a), (3, 0, low_a), (3, cut_a, high_a)]
     pieces += [(number + 4, first, pp(piece, "seq")) for number, first, piece in pieces]
-    pair_b = gather_z(shard_b, far_b)
+    pair_b = pair_z(ids, shard_b, far_b)
     near_b = pp(pair_b, "z", 1)
-    turned, keep_output, keep_feed = prepare(
-        ids, after(hidden, far_b), output_keep.reshape(rows, -1), feed_keep.reshape(rows, -1), tokens
-    )
     plan = [(i * own, own, i, 0, 0) for i in range(3)]
+    plan = divide(plan, cut_a)
     weights = Weights(pieces, plan + [(3 * own, 8, 3, 0, 0)], [square] * 3 + [(8, width)])
     weights_again = Weights(pieces, plan, [square] * 3)
-    queries, *near = project(ids, weights, hidden, turned, micro, per)
-    far = [pp(value, "seq") for value in near]
-    own_b = order_z(pair_b, after(near_b, *near))
+    own_b = order_z(ids, pair_b, after(near_b, low_a, high_a))
     x_b, y_b = pp(own_b, "x"), pp(own_b, "y")
+    queries, *near = project(ids, weights, hidden, after(turned, own_b), micro, per)
+    near = (near[: 2 * PARTS[0]], near[2 * PARTS[0] :])
+    far = [[pp(value, "seq") for value in values] for values in near]
     shard_c = after(down_weight, own_b)
     far_c = pp(shard_c, "z", 2)
     words = attention_keep.reshape(micro, H, tokens, -1)
-    far[0], far[1], far_c = hold((far[0], far[1], far_c), own_b)
-    pair_c = gather_z(shard_c, far_c)
+    context, signed = attention(ids, 0, queries, near, far, words)
+    far_c, own_b, x_b, y_b, *far[1] = hold((far_c, own_b, x_b, y_b, *far[1]), context)
+    pair_c = pair_z(ids, shard_c, far_c)
     near_c = pp(pair_c, "z", 1)
-    context, signed = attention(ids, 0, queries, near, far, words)
-    far[2], far[3] = hold((far[2], far[3]), context)
+    cut_b = shard_b.shape[0] // 2
+    low_b, high_b = pp(x_b[:, :cut_b], "y"), pp(y_b[:, cut_b:], "x")
     context, signed = attention(ids, 1, queries, near, far, words, (context, signed))
-    own_b, x_b, y_b, near_c = hold((own_b, x_b, y_b, near_c), context)
-    cut_b = 3 * own
-    low_b, high_b = pp(x_b[:, :cut_b], "y"), pp(y_b[:, cut_b:], "x")
+    low_b, high_b, near_c = hold((low_b, high_b, near_c), context)
     pieces = [(0, 0, own_b), (1, 0, x_b), (2, 0, y_b)]
     pieces += [(number + 4, first, pp(piece, "seq")) for number, first, piece in pieces]
     pieces += [(3, 0, low_b), (3, cut_b, high_b), (7, 0, pp(low_b, "seq")), (7, cut_b, pp(high_b, "seq"))]
     plan = [(0, own, 0, 0, 0)] + [((i + 1) * own, own, 1, 0, i * width) for i in range(blocks)]
+    plan = divide(plan, cut_b)
     weights = Weights(
         pieces, plan + [((blocks + 1) * own, 8, 2, 0, 0)], [square, (own, wide), (8, width)]
     )
     back_weights = Weights(pieces, plan, [square, (own, wide)])
-    own_c = order_z(pair_c, hold((near_c,), low_b, high_b)[0])
+    own_c = order_z(ids, pair_c, after(near_c, low_b, high_b))
     x_c, y_c = pp(own_c, "x"), pp(own_c, "y")
     context = context.reshape(rows, width)
     vectors, scaled, inverse, activated, slope = feed_up(
@@ -1205,7 +1254,7 @@
     pieces = [(0, 0, own_c), (1, 0, x_c), (2, 0, y_c), (3, 0, low_c), (3, cut_c, high_c)]
     pieces += [(number + 4, first, pp(piece, "seq")) for number, first, piece in pieces]
     weights = Weights(
-        pieces, [(0, cut_c, 0, 0, 0), (cut_c, cut_c, 0, cut_c, 0)], [(down_rows, width)]
+        pieces, divide([(0, down_rows, 0, 0, 0)], cut_c), [(down_rows, width)]
     )
     layer_out, g_second, g_inner, down_own, down_send, sums = feed_down(
         ids, weights, activated, slope, scaled, keep_feed, cotangent.reshape(rows, width), vectors, tokens
@@ -1243,15 +1292,15 @@
         ids, hidden, turned, g_q, g_near, after(far_grads, to_y, to_x, *sends), per
     )
     grad_in = last(ids, weights_again, g_first, g_q.reshape(rows, width), g_keys, g_values, tokens)
-    mid_y, mid_x = hold((mid_y, mid_x), grad_in)
+    mid_y, mid_x, *down_z = hold((mid_y, mid_x, *down_z), grad_in)
     core_sums = pp(after(a_send, mid_y, mid_x), "seq")
     part = [unit(a_own), unit(core_sums)]
     corner = reduce_corner(ids, part, cut_a)
     low, high = pp(corner[0], "x"), pp(corner[1], "y")
     *sends, mid_mine = reduce_depth(ids, mid, after(mid_y, *corner), mid_x)
     mid_z = exchange_z(sends)
-    grad_down = add_up([down_mine, *hold(down_z, *sends)])
-    low, high = hold((low, high), grad_down)
+    low, high = hold((low, high), *sends)
+    grad_down = add_up([down_mine, *down_z])
     to_y, to_x = reduce_sides(ids, part, low, high)
     side_y, side_x = pp(to_y, "y"), pp(to_x, "x")
     mid = add_up([mid_mine, *hold(mid_z, to_y, to_x)])

time: 272 us -> 243 us (0.89)
  waiting for transfers between devices: 90.8 us -> 65.7 us
  other arithmetic: 6.54 us -> 2.81 us
  starting transfers between devices: 49.4 us -> 52.6 us
  local copies, waits for them, and re-layouts: 12.7 us -> 9.7 us
    ppermute x63 -> x65, waiting for transfers between devices: 90.8 us -> 65.7 us  [pp(): return lax.ppermute(value, axis, [(i, i ^ step) for i in range(size)])]
    unnamed x114 -> x110, local copies, waits for them, and re-layouts: 7.47 us -> 3.74 us
    ppermute x63 -> x65, starting transfers between devices: 49.4 us -> 52.6 us  [pp(): return lax.ppermute(value, axis, [(i, i ^ step) for i in range(size)])]
    select_n x6 -> x2, other arithmetic: 3.16 us -> 0.28 us  [swap_if(): return jnp.where(flag, lax.concatenate([high, low], axis), value)]
    pallas_call x21 -> x25, Pallas kernels: 110 us -> 111 us  [call(): pl.pallas_call(body, grid_spec=pltpu.PrefetchScalarGridSpec(num_scalar_pr...]
  transfers between devices with their start and end apart: 63 -> 65, of which waited for: 19 -> 29; matrix products, arithmetic and copies ran while one was open for 4% -> 2% of each run, Pallas kernels for 33% -> 37%
where the time goes in v3:
time: 243 us
  Pallas kernels  111 us (46%)
  waiting for transfers between devices  65.7 us (27%)
  starting transfers between devices  52.6 us (22%)
  local copies, waits for them, and re-layouts  9.7 us (4%)
  other arithmetic  2.81 us (1%)
    pallas_call x25, Pallas kernels, call(): pl.pallas_call(body, grid_spec=pltpu.PrefetchScalarGridSpec(num_scalar_pr...  111 us
    ppermute x65, waiting for transfers between devices, pp(): return lax.ppermute(value, axis, [(i, i ^ step) for i in range(size)])  65.7 us
    ppermute x65, starting transfers between devices, pp(): return lax.ppermute(value, axis, [(i, i ^ step) for i in range(size)])  52.6 us
  transfers between devices with their start and end apart: 65, of which 29 were waited for; matrix products, arithmetic and copies ran while one was open for 2% of the time, Pallas kernels for 37%

profile of v3, /device:TPU:0, one launch (start us, length us, event | category | flops | bytes accessed | tf_op | source)
XLA Modules:
  0.0 243.2 jit_solution(17683087062133179062)
XLA Ops:
  0.6 0.8 fusion.6
  2.2 5.1 %collective-permute-start.2 = (bf16[80,768]{1,0:T(8,128)(2,1)S(1)}, bf16[80,768]{1,0:T(8,128)(2,1)S(1)}, u32[]{:S(2)}, u32[]{:S(2)}) collective-permute-start(bf16[80,768]{1,0:T(8,128)(2,1)S(1)} %concatenate.23), channel_id=1, source_target_pairs={{0,24},{8,16},{16,8},{24,0},{1,25},{9,17},{17,9},{25,1},{2,26},{10... | collective-permute-start | bytes 368648 | tf_op jit(solution)/shard_map/ppermute | solution.py:335
  7.9 3.6 %collective-permute-done.2 = bf16[80,768]{1,0:T(8,128)(2,1)S(1)} collective-permute-done((bf16[80,768]{1,0:T(8,128)(2,1)S(1)}, bf16[80,768]{1,0:T(8,128)(2,1)S(1)}, u32[]{:S(2)}, u32[]{:S(2)}) %collective-permute-start.2) | collective-permute-done | bytes 122912 | tf_op jit(solution)/shard_map/ppermute | solution.py:335
  11.5 6.1 %collective-permute-done.1 = bf16[80,768]{1,0:T(8,128)(2,1)S(1)} collective-permute-done((bf16[80,768]{1,0:T(8,128)(2,1)S(1)}, bf16[80,768]{1,0:T(8,128)(2,1)S(1)}, u32[]{:S(2)}, u32[]{:S(2)}) %collective-permute-start.1) | collective-permute-done | bytes 122912 | tf_op jit(solution)/shard_map/ppermute | solution.py:335
  18.3 1.6 collective-permute-start.4
  19.9 1.5 collective-permute-start.3
  21.9 3.1 %prepare.1 = (bf16[512,768]{1,0:T(8,128)(2,1)S(1)}, bf16[512,768]{1,0:T(8,128)(2,1)S(1)}, bf16[512,768]{1,0:T(8,128)(2,1)S(1)}) custom-call(s32[4]{0:T(128)S(1)} %pad_add_fusion.ids, bf16[512,768]{1,0:T(8,128)(2,1)S(1)} %bitcast.82, s32[2,1,192,256]{3,2,1,0:T(8,128)S(1)} %bitcast.92, s32[2,1,192,256]{3,2,1,0:T(8,128)S(1)} %bitcast.93), custom_call_target="tpu_custom_call" | custom-call | flops 1024 | bytes 6291456 | tf_op jit(solution)/shard_map/prepare/pallas_call | solution.py:455
  25.0 6.9 %collective-permute-done.5.two = bf16[128,768]{1,0:T(8,128)(2,1)S(1)} collective-permute-done((bf16[128,768]{1,0:T(8,128)(2,1)S(1)}, bf16[128,768]{1,0:T(8,128)(2,1)S(1)}, u32[]{:S(2)}, u32[]{:S(2)}) %collective-permute-start.5) | collective-permute-done | bytes 196640 | tf_op jit(solution)/shard_map/ppermute | solution.py:335
  32.0 1.0 slice.111
  32.9 1.6 collective-permute-start.8
  35.7 1.0 slice.110
  37.2 3.5 %collective-permute-done.8.refs_4_ = bf16[4,40,768]{2,1,0:T(8,128)(2,1)S(1)} collective-permute-done((bf16[4,40,768]{2,1,0:T(8,128)(2,1)S(1)}, bf16[4,40,768]{2,1,0:T(8,128)(2,1)S(1)}, u32[]{:S(2)}, u32[]{:S(2)}) %collective-permute-start.8) | collective-permute-done | bytes 245792 | tf_op jit(solution)/shard_map/ppermute | solution.py:335
  40.7 3.9 %collective-permute-done.7.refs_3_ = bf16[4,40,768]{2,1,0:T(8,128)(2,1)S(1)} collective-permute-done((bf16[4,40,768]{2,1,0:T(8,128)(2,1)S(1)}, bf16[4,40,768]{2,1,0:T(8,128)(2,1)S(1)}, u32[]{:S(2)}, u32[]{:S(2)}) %collective-permute-start.7) | collective-permute-done | bytes 245792 | tf_op jit(solution)/shard_map/ppermute | solution.py:335
  44.6 2.1 collective-permute-done.6.received
  50.0 5.4 %project.1 = (bf16[2,256,768]{2,1,0:T(8,128)(2,1)S(1)}, bf16[128,768]{1,0:T(8,128)(2,1)S(1)}, bf16[128,768]{1,0:T(8,128)(2,1)S(1)}, bf16[128,768]{1,0:T(8,128)(2...) custom-call(s32[4]{0:T(128)S(1)} %pad_add_fusion.ids, ...), custom_call_target="tpu_custom_call" | custom-call | flops 1024 | bytes 10485760 | tf_op jit(solution)/shard_map/project/pallas_call | solution.py:455
  56.1 0.9 collective-permute-done.19.refs_4_
  57.8 1.8 collective-permute-done.22.refs_7_
  59.6 1.1 collective-permute-start.9
  60.7 7.3 %attention.2 = (bf16[2,256,768]{2,1,0:T(8,128)(2,1)S(1)}, bf16[2,6,2,4,256,128]{5,4,3,2,1,0:T(8,128)(2,1)S(1)}) custom-call(s32[4]{0:T(128)S(1)} %pad_add_fusion.ids, bf16[2,256,768]{2,1,0:T(8,128)(2,1)S(1)} %get-tuple-element.138.q, bf16[128,768]{1,0:T(8,128)(2,1)S(1)} %get-tuple-element.139.refs_0_, bf16[128,768]{1,0:T(8,128)(2,1)S(1)} %get-tuple-element.140.refs_1_, ...), custom_call_target="tpu_custom_call" | custom-call | flops 1024 | bytes 14680064 | tf_op jit(solution)/shard_map/attention/pallas_call | solution.py:455
  68.1 1.2 collective-permute-done.9.two
  69.4 1.6 collective-permute-start.24
  70.9 1.5 collective-permute-start.23
  73.7 7.2 %attention.3 = (bf16[2,256,768]{2,1,0:T(8,128)(2,1)S(1)}, bf16[2,6,2,4,256,128]{5,4,3,2,1,0:T(8,128)(2,1)S(1)}) custom-call(s32[4]{0:T(128)S(1)} %pad_add_fusion.ids, bf16[2,256,768]{2,1,0:T(8,128)(2,1)S(1)} %get-tuple-element.138.q, bf16[256,768]{1,0:T(8,128)(2,1)S(1)} %get-tuple-element.136.refs_0_, ...), custom_call_target="tpu_custom_call", output_to_operand_aliasing={{0}: (7, {}), {1}: (8, {})} | custom-call | flops 1024 | bytes 14680064 | tf_op jit(solution)/shard_map/attention/pallas_call | solution.py:455
  83.4 1.6 collective-permute-start.27
  86.2 1.1 collective-permute-done.30.refs_5_
  87.4 0.8 copy-done.25
  88.3 12.5 %feed_up.1 = (f32[8,3072]{1,0:T(8,128)S(1)}, f32[512,768]{1,0:T(8,128)S(1)}, f32[512,128]{1,0:T(8,128)S(1)}, bf16[512,3072]{1,0:T(8,128)(2,1)S(1)}, bf16[512,3072]{1,0:T(8,128)(2,1)S(1)}) custom-call(s32[4]{0:T(128)S(1)} %pad_add_fusion.ids, bf16[4,128,768]{2,1,0:T(8,128)(2,1)} %copy-done.2, bf16[4,128,768]{2,1,0:T(8,128)(2,1)} %copy-done.21, ...), custom_call_target="tpu_custom_call" | custom-call | flops 1024 | bytes 25165824 | tf_op jit(solution)/shard_map/feed_up/pallas_call | solution.py:455
  101.5 1.6 collective-permute-start.33
  103.6 6.4 %collective-permute-done.34.refs_4_ = bf16[4,48,768]{2,1,0:T(8,128)(2,1)S(1)} collective-permute-done((bf16[4,48,768]{2,1,0:T(8,128)(2,1)S(1)}, bf16[4,48,768]{2,1,0:T(8,128)(2,1)S(1)}, u32[]{:S(2)}, u32[]{:S(2)}) %collective-permute-start.34) | collective-permute-done | bytes 294944 | tf_op jit(solution)/shard_map/ppermute | solution.py:335
  110.5 1.1 collective-permute-done.39.refs_9_
  113.2 17.5 %feed_down.1 = (bf16[512,768]{1,0:T(8,128)(2,1)}, f32[512,768]{1,0:T(8,128)S(1)}, bf16[512,3072]{1,0:T(8,128)(2,1)S(1)}, bf16[16,96,768]{2,1,0:T(8,128)(2,1)S(1)...) custom-call(s32[4]{0:T(128)S(1)} %pad_add_fusion.ids, bf16[4,96,768]{2,1,0:T(8,128)(2,1)} %copy-done.3, ...), custom_call_target="tpu_custom_call" | custom-call | flops 1024 | bytes 37748736 | tf_op jit(solution)/shard_map/feed_down/pallas_call | solution.py:455
  130.9 9.2 %middle.1 = (f32[512,768]{1,0:T(8,128)S(1)}, bf16[512,768]{1,0:T(8,128)(2,1)S(1)}, bf16[512,768]{1,0:T(8,128)(2,1)S(1)}, f32[8,768]{1,0:T(8,128)S(1)}) custom-call(s32[4]{0:T(128)S(1)} %pad_add_fusion.ids, bf16[4,128,768]{2,1,0:T(8,128)(2,1)} %copy-done.2, bf16[4,128,768]{2,1,0:T(8,128)(2,1)} %copy-done.21, bf16[4,128,768]{2,1,0:T(8,128)(2,1)} %copy-done.20, ...), custom_call_target="tpu_custom_call" | custom-call | flops 1024 | bytes 14680064 | tf_op jit(solution)/shard_map/middle/pallas_call | solution.py:455
  140.8 1.5 collective-permute-start.41
  142.3 1.5 collective-permute-start.42
  143.8 8.4 %middle_grads.1 = (bf16[16,128,768]{2,1,0:T(8,128)(2,1)S(1)}, bf16[16,128,768]{2,1,0:T(8,128)(2,1)S(1)}) custom-call(s32[4]{0:T(128)S(1)} %pad_add_fusion.ids, bf16[512,3072]{1,0:T(8,128)(2,1)S(1)} %get-tuple-element.165.refs_10_.g_inner, f32[512,768]{1,0:T(8,128)S(1)} %get-tuple-element.161.refs_12_.scaled, bf16[512,768]{1,0:T(8,128)(2,1)S(1)} %bitcast.90, ...), custom_call_target="tpu_custom_call" | custom-call | flops 1024 | bytes 20971520 | tf_op jit(solution)/shard_map/middle_grads/pallas_call | solution.py:455
  152.4 0.9 reduce_sides.3
  154.5 9.2 %attention_back.2 = (bf16[2,256,768]{2,1,0:T(8,128)(2,1)S(1)}, f32[2,2,256,768]{3,2,1,0:T(8,128)S(1)}, bf16[2,2,256,768]{3,2,1,0:T(8,128)(2,1)S(1)}) custom-call(s32[4]{0:T(128)S(1)} %pad_add_fusion.ids, bf16[2,256,768]{2,1,0:T(8,128)(2,1)S(1)} %get-tuple-element.138.q, bf16[128,768]{1,0:T(8,128)(2,1)S(1)} %get-tuple-element.139.refs_0_, ...), custom_call_target="tpu_custom_call" | custom-call | flops 1024 | bytes 20971520 | tf_op jit(solution)/shard_map/attention_back/pallas_call | solution.py:455
  164.5 1.5 collective-permute-start.44
  166.0 1.5 collective-permute-start.45
  167.5 9.4 %attention_back.3 = (bf16[2,256,768]{2,1,0:T(8,128)(2,1)S(1)}, f32[2,2,256,768]{3,2,1,0:T(8,128)S(1)}, bf16[2,2,256,768]{3,2,1,0:T(8,128)(2,1)S(1)}) custom-call(s32[4]{0:T(128)S(1)} %pad_add_fusion.ids, bf16[2,256,768]{2,1,0:T(8,128)(2,1)S(1)} %get-tuple-element.138.q, ...), custom_call_target="tpu_custom_call", output_to_operand_aliasing={{0}: (8, {}), {1}: (9, {}), {2}: (10, {})} | custom-call | flops 1024 | bytes 20971520 | tf_op jit(solution)/shard_map/attention_back/pallas_call | solution.py:455
  176.9 0.9 collective-permute-done.44.low
  177.8 1.0 reduce_sides.4
  178.8 1.5 collective-permute-start.49
  180.8 1.0 reduce_depth.3
  182.5 2.3 collective-permute-start.52
  184.8 1.5 collective-permute-start.53
  186.3 4.6 %input_grads.1 = (bf16[16,80,768]{2,1,0:T(8,128)(2,1)S(1)}, bf16[16,80,768]{2,1,0:T(8,128)(2,1)S(1)}, bf16[512,768]{1,0:T(8,128)(2,1)S(1)}, bf16[512,768]{1,0:T(8,128)(2,1)S(1)}) custom-call(s32[4]{0:T(128)S(1)} %pad_add_fusion.ids, bf16[512,768]{1,0:T(8,128)(2,1)S(1)} %bitcast.85, bf16[512,768]{1,0:T(8,128)(2,1)S(1)} %get-tuple-element.135.refs_11_.turned, ...), custom_call_target="tpu_custom_call" | custom-call | flops 1024 | bytes 12582912 | tf_op jit(solution)/shard_map/input_grads/pallas_call | solution.py:455
  190.9 6.5 %input_back.1 = bf16[512,768]{1,0:T(8,128)(2,1)} custom-call(s32[4]{0:T(128)S(1)} %pad_add_fusion.ids, bf16[4,80,768]{2,1,0:T(8,128)(2,1)} %copy-done.22, bf16[4,80,768]{2,1,0:T(8,128)(2,1)} %collective-permute-done.3.refs_1_, bf16[4,80,768]{2,1,0:T(8,128)(2,1)} %collective-permute-done.4.refs_2_, bf16[4,40,768]{2,1,0:T(8,128)(2,1)} %copy-done.36, ...), custom_call_target="tpu_custom_call" | custom-call | flops 1024 | bytes 10485760 | tf_op jit(solution)/shard_map/input_back/pallas_call | solution.py:455
  197.4 1.4 collective-permute-done.49.from_y
  198.8 1.2 collective-permute-done.50.from_x
  200.0 4.0 %collective-permute-done.54 = bf16[16,80,768]{2,1,0:T(8,128)(2,1)S(1)} collective-permute-done((bf16[16,80,768]{2,1,0:T(8,128)(2,1)S(1)}, bf16[16,80,768]{2,1,0:T(8,128)(2,1)S(1)}, u32[]{:S(2)}, u32[]{:S(2)}) %collective-permute-start.54) | collective-permute-done | bytes 1966112 | tf_op jit(solution)/shard_map/ppermute | solution.py:335
  205.8 1.3 reduce_depth.4
  207.7 2.3 collective-permute-start.60
  210.0 1.5 collective-permute-start.61
  212.9 0.8 reduce_sides.5
  213.7 0.9 collective-permute-start.57
  214.6 1.5 collective-permute-start.58
  216.8 8.1 %collective-permute-done.60 = bf16[128,768]{1,0:T(8,128)(2,1)S(1)} collective-permute-done((bf16[128,768]{1,0:T(8,128)(2,1)S(1)}, bf16[128,768]{1,0:T(8,128)(2,1)S(1)}, u32[]{:S(2)}, u32[]{:S(2)}) %collective-permute-start.60) | collective-permute-done | bytes 196640 | tf_op jit(solution)/shard_map/ppermute | solution.py:335
  226.9 0.9 reduce_depth.5
  227.9 3.2 %collective-permute-start.62 = (bf16[80,768]{1,0:T(8,128)(2,1)S(1)}, bf16[80,768]{1,0:T(8,128)(2,1)S(1)}, u32[]{:S(2)}, u32[]{:S(2)}) collective-permute-start(bf16[80,768]{1,0:T(8,128)(2,1)S(1)} %get-tuple-element.233), channel_id=1, source_target_pairs={{0,8},{8,0},{16,24},{24,16},{1,9},{9,1},{17,25},{25,17},{2,10},{10... | collective-permute-start | bytes 368648 | tf_op jit(solution)/shard_map/ppermute | solution.py:335
  231.0 0.9 collective-permute-start.63
  231.9 1.5 collective-permute-start.64
  234.0 1.0 collective-permute-done.62
  234.9 6.9 %collective-permute-done.63 = bf16[80,768]{1,0:T(8,128)(2,1)S(1)} collective-permute-done((bf16[80,768]{1,0:T(8,128)(2,1)S(1)}, bf16[80,768]{1,0:T(8,128)(2,1)S(1)}, u32[]{:S(2)}, u32[]{:S(2)}) %collective-permute-start.63) | collective-permute-done | bytes 122912 | tf_op jit(solution)/shard_map/ppermute | solution.py:335
  (238 shorter events, 29.5 us)
Async XLA Ops:
  2.2 9.4 %collective-permute-start.2 = (bf16[80,768]{1,0:T(8,128)(2,1)S(1)}, bf16[80,768]{1,0:T(8,128)(2,1)S(1)}, u32[]{:S(2)}, u32[]{:S(2)}) collective-permute-start(bf16[80,768]{1,0:T(8,128)(2,1)S(1)} %concatenate.23), channel_id=1, source_target_pairs={{0,24},{8,16},{16,8},{24,0},{1,25},{9,17},{17,9},{25,1},{2,26},{10... | collective-permute-start | bytes 368648 | tf_op jit(solution)/shard_map/ppermute | solution.py:335
  7.3 10.4 %collective-permute-start.1 = (bf16[80,768]{1,0:T(8,128)(2,1)S(1)}, bf16[80,768]{1,0:T(8,128)(2,1)S(1)}, u32[]{:S(2)}, u32[]{:S(2)}) collective-permute-start(bf16[80,768]{1,0:T(8,128)(2,1)S(1)} %concatenate.23), channel_id=1, source_target_pairs={{0,16},{8,24},{16,0},{24,8},{1,17},{9,25},{17,1},{25,9},{2,18},{10... | collective-permute-start | bytes 368648 | tf_op jit(solution)/shard_map/ppermute | solution.py:335
  7.3 10.4 %collective-permute-start = (bf16[80,768]{1,0:T(8,128)(2,1)S(1)}, bf16[80,768]{1,0:T(8,128)(2,1)S(1)}, u32[]{:S(2)}, u32[]{:S(2)}) collective-permute-start(bf16[80,768]{1,0:T(8,128)(2,1)S(1)} %concatenate.23), channel_id=1, source_target_pairs={{0,8},{8,0},{16,24},{24,16},{1,9},{9,1},{17,25},{25,17},{2,10},{10... | collective-permute-start | bytes 368648 | tf_op jit(solution)/shard_map/ppermute | solution.py:335
  18.3 13.6 %collective-permute-start.4 = (bf16[4,80,768]{2,1,0:T(8,128)(2,1)S(1)}, bf16[4,80,768]{2,1,0:T(8,128)(2,1)}, u32[]{:S(2)}, u32[]{:S(2)}) collective-permute-start(bf16[4,80,768]{2,1,0:T(8,128)(2,1)S(1)} %fusion.refs_0_), channel_id=1, source_target_pairs={{0,4},{4,0},{1,5},{5,1},{2,6},{6,2},{3,7},{7,3},{8,12},{12,8},{9,1... | collective-permute-start | bytes 1474568 | tf_op jit(solution)/shard_map/ppermute | solution.py:335
  19.9 12.1 %collective-permute-start.3 = (bf16[4,80,768]{2,1,0:T(8,128)(2,1)S(1)}, bf16[4,80,768]{2,1,0:T(8,128)(2,1)}, u32[]{:S(2)}, u32[]{:S(2)}) collective-permute-start(bf16[4,80,768]{2,1,0:T(8,128)(2,1)S(1)} %fusion.refs_0_), channel_id=1, source_target_pairs={{0,2},{2,0},{1,3},{3,1},{4,6},{6,4},{5,7},{7,5},{8,10},{10,8},{9,1... | collective-permute-start | bytes 1474568 | tf_op jit(solution)/shard_map/ppermute | solution.py:335
  21.6 10.2 %collective-permute-start.5 = (bf16[128,768]{1,0:T(8,128)(2,1)S(1)}, bf16[128,768]{1,0:T(8,128)(2,1)S(1)}, u32[]{:S(2)}, u32[]{:S(2)}) collective-permute-start(bf16[128,768]{1,0:T(8,128)(2,1)S(1)} %concatenate.22.one), channel_id=1, source_target_pairs={{0,16},{8,24},{16,0},{24,8},{1,17},{9,25},{17,1},{25,9},{2,18},{10... | collective-permute-start | bytes 589832 | tf_op jit(solution)/shard_map/ppermute | solution.py:335
  32.9 7.8 %collective-permute-start.8 = (bf16[4,40,768]{2,1,0:T(8,128)(2,1)S(1)}, bf16[4,40,768]{2,1,0:T(8,128)(2,1)S(1)}, u32[]{:S(2)}, u32[]{:S(2)}) collective-permute-start(bf16[4,40,768]{2,1,0:T(8,128)(2,1)S(1)} %slice.111), channel_id=1, source_target_pairs={{0,2},{2,0},{1,3},{3,1},{4,6},{6,4},{5,7},{7,5},{8,10},{10,8},{9,1... | collective-permute-start | bytes 737288 | tf_op jit(solution)/shard_map/ppermute | solution.py:335
  34.5 12.8 %collective-permute-start.12 = (bf16[4,80,768]{2,1,0:T(8,128)(2,1)S(1)}, bf16[4,80,768]{2,1,0:T(8,128)(2,1)S(1)}, u32[]{:S(2)}, u32[]{:S(2)}) collective-permute-start(bf16[4,80,768]{2,1,0:T(8,128)(2,1)S(1)} %fusion.refs_0_), channel_id=1, source_target_pairs={{0,1},{1,0},{2,3},{3,2},{4,5},{5,4},{6,7},{7,6},{8,9},{9,8},{10,11... | collective-permute-start | bytes 1474568 | tf_op jit(solution)/shard_map/ppermute | solution.py:335
  34.5 13.4 %collective-permute-start.13 = (bf16[4,80,768]{2,1,0:T(8,128)(2,1)}, bf16[4,80,768]{2,1,0:T(8,128)(2,1)S(1)}, u32[]{:S(2)}, u32[]{:S(2)}) collective-permute-start(bf16[4,80,768]{2,1,0:T(8,128)(2,1)} %collective-permute-done.3.refs_1_), channel_id=1, source_target_pairs={{0,1},{1,0},{2,3},{3,2},{4,5},{5,4},{6,7},{7,6},{8,9},{9,8},{10,11... | collective-permute-start | bytes 1474568 | tf_op jit(solution)/shard_map/ppermute | solution.py:335
  35.6 11.1 %collective-permute-start.6 = (bf16[2,128,768]{2,1,0:T(8,128)(2,1)S(1)}, bf16[2,128,768]{2,1,0:T(8,128)(2,1)S(1)}, u32[]{:S(2)}, u32[]{:S(2)}) collective-permute-start(bf16[2,128,768]{2,1,0:T(8,128)(2,1)S(1)} %pair_z.2.pair), channel_id=1, source_target_pairs={{0,8},{8,0},{16,24},{24,16},{1,9},{9,1},{17,25},{25,17},{2,10},{10... | collective-permute-start | bytes 1179656 | tf_op jit(solution)/shard_map/ppermute | solution.py:335
  36.6 7.9 %collective-permute-start.7 = (bf16[4,40,768]{2,1,0:T(8,128)(2,1)S(1)}, bf16[4,40,768]{2,1,0:T(8,128)(2,1)S(1)}, u32[]{:S(2)}, u32[]{:S(2)}) collective-permute-start(bf16[4,40,768]{2,1,0:T(8,128)(2,1)S(1)} %slice.110), channel_id=1, source_target_pairs={{0,4},{4,0},{1,5},{5,1},{2,6},{6,2},{3,7},{7,3},{8,12},{12,8},{9,1... | collective-permute-start | bytes 737288 | tf_op jit(solution)/shard_map/ppermute | solution.py:335
  40.7 7.8 %collective-permute-start.14 = (bf16[4,80,768]{2,1,0:T(8,128)(2,1)}, bf16[4,80,768]{2,1,0:T(8,128)(2,1)S(1)}, u32[]{:S(2)}, u32[]{:S(2)}) collective-permute-start(bf16[4,80,768]{2,1,0:T(8,128)(2,1)} %collective-permute-done.4.refs_2_), channel_id=1, source_target_pairs={{0,1},{1,0},{2,3},{3,2},{4,5},{5,4},{6,7},{7,6},{8,9},{9,8},{10,11... | collective-permute-start | bytes 1474568 | tf_op jit(solution)/shard_map/ppermute | solution.py:335
  44.6 3.9 %collective-permute-start.16 = (bf16[4,40,768]{2,1,0:T(8,128)(2,1)S(1)}, bf16[4,40,768]{2,1,0:T(8,128)(2,1)S(1)}, u32[]{:S(2)}, u32[]{:S(2)}) collective-permute-start(bf16[4,40,768]{2,1,0:T(8,128)(2,1)S(1)} %collective-permute-done.8.refs_4_), channel_id=1, source_target_pairs={{0,1},{1,0},{2,3},{3,2},{4,5},{5,4},{6,7},{7,6},{8,9},{9,8},{10,11... | collective-permute-start | bytes 737288 | tf_op jit(solution)/shard_map/ppermute | solution.py:335
  46.7 1.8 collective-permute-start.15
  47.3 21.9 %collective-permute-start.11 = (bf16[4,128,768]{2,1,0:T(8,128)(2,1)S(1)}, bf16[4,128,768]{2,1,0:T(8,128)(2,1)S(1)}, u32[]{:S(2)}, u32[]{:S(2)}) collective-permute-start(bf16[4,128,768]{2,1,0:T(8,128)(2,1)S(1)} %order_z.2.refs_0_), channel_id=1, source_target_pairs={{0,4},{4,0},{1,5},{5,1},{2,6},{6,2},{3,7},{7,3},{8,12},{12,8},{9,1... | collective-permute-start | bytes 2359304 | tf_op jit(solution)/shard_map/ppermute | solution.py:335
  47.9 21.4 %collective-permute-start.10 = (bf16[4,128,768]{2,1,0:T(8,128)(2,1)S(1)}, bf16[4,128,768]{2,1,0:T(8,128)(2,1)S(1)}, u32[]{:S(2)}, u32[]{:S(2)}) collective-permute-start(bf16[4,128,768]{2,1,0:T(8,128)(2,1)S(1)} %order_z.2.refs_0_), channel_id=1, source_target_pairs={{0,2},{2,0},{1,3},{3,1},{4,6},{6,4},{5,7},{7,5},{8,10},{10,8},{9,1... | collective-permute-start | bytes 2359304 | tf_op jit(solution)/shard_map/ppermute | solution.py:335
  55.5 1.5 collective-permute-start.19
  55.6 1.7 collective-permute-start.20
  57.0 12.2 %collective-permute-start.17 = (bf16[256,768]{1,0:T(8,128)(2,1)S(1)}, bf16[256,768]{1,0:T(8,128)(2,1)S(1)}, u32[]{:S(2)}, u32[]{:S(2)}) collective-permute-start(bf16[256,768]{1,0:T(8,128)(2,1)S(1)} %get-tuple-element.136.refs_0_), channel_id=1, source_target_pairs={{0,1},{1,0},{2,3},{3,2},{4,5},{5,4},{6,7},{7,6},{8,9},{9,8},{10,11... | collective-permute-start | bytes 1179656 | tf_op jit(solution)/shard_map/ppermute | solution.py:335
  57.3 12.0 %collective-permute-start.18 = (bf16[256,768]{1,0:T(8,128)(2,1)S(1)}, bf16[256,768]{1,0:T(8,128)(2,1)S(1)}, u32[]{:S(2)}, u32[]{:S(2)}) collective-permute-start(bf16[256,768]{1,0:T(8,128)(2,1)S(1)} %get-tuple-element.137.refs_1_), channel_id=1, source_target_pairs={{0,1},{1,0},{2,3},{3,2},{4,5},{5,4},{6,7},{7,6},{8,9},{9,8},{10,11... | collective-permute-start | bytes 1179656 | tf_op jit(solution)/shard_map/ppermute | solution.py:335
  57.6 2.0 collective-permute-start.22
  59.6 9.7 %collective-permute-start.9 = (bf16[96,768]{1,0:T(8,128)(2,1)S(1)}, bf16[96,768]{1,0:T(8,128)(2,1)S(1)}, u32[]{:S(2)}, u32[]{:S(2)}) collective-permute-start(bf16[96,768]{1,0:T(8,128)(2,1)S(1)} %copy-done.19), channel_id=1, source_target_pairs={{0,16},{8,24},{16,0},{24,8},{1,17},{9,25},{17,1},{25,9},{2,18},{10... | collective-permute-start | bytes 442376 | tf_op jit(solution)/shard_map/ppermute | solution.py:335
  69.4 12.1 %collective-permute-start.24 = (bf16[4,64,768]{2,1,0:T(8,128)(2,1)S(1)}, bf16[4,64,768]{2,1,0:T(8,128)(2,1)S(1)}, u32[]{:S(2)}, u32[]{:S(2)}) collective-permute-start(bf16[4,64,768]{2,1,0:T(8,128)(2,1)S(1)} %slice.113), channel_id=1, source_target_pairs={{0,2},{2,0},{1,3},{3,1},{4,6},{6,4},{5,7},{7,5},{8,10},{10,8},{9,1... | collective-permute-start | bytes 1179656 | tf_op jit(solution)/shard_map/ppermute | solution.py:335
  70.9 10.8 %collective-permute-start.23 = (bf16[4,64,768]{2,1,0:T(8,128)(2,1)S(1)}, bf16[4,64,768]{2,1,0:T(8,128)(2,1)S(1)}, u32[]{:S(2)}, u32[]{:S(2)}) collective-permute-start(bf16[4,64,768]{2,1,0:T(8,128)(2,1)S(1)} %slice.112), channel_id=1, source_target_pairs={{0,4},{4,0},{1,5},{5,1},{2,6},{6,2},{3,7},{7,3},{8,12},{12,8},{9,1... | collective-permute-start | bytes 1179656 | tf_op jit(solution)/shard_map/ppermute | solution.py:335
  73.0 8.5 %collective-permute-start.25 = (bf16[2,96,768]{2,1,0:T(8,128)(2,1)S(1)}, bf16[2,96,768]{2,1,0:T(8,128)(2,1)S(1)}, u32[]{:S(2)}, u32[]{:S(2)}) collective-permute-start(bf16[2,96,768]{2,1,0:T(8,128)(2,1)S(1)} %pair_z.3.pair), channel_id=1, source_target_pairs={{0,8},{8,0},{16,24},{24,16},{1,9},{9,1},{17,25},{25,17},{2,10},{10... | collective-permute-start | bytes 884744 | tf_op jit(solution)/shard_map/ppermute | solution.py:335
  81.7 1.7 collective-permute-start.31
  81.7 3.3 %collective-permute-start.32 = (bf16[4,64,768]{2,1,0:T(8,128)(2,1)S(1)}, bf16[4,64,768]{2,1,0:T(8,128)(2,1)S(1)}, u32[]{:S(2)}, u32[]{:S(2)}) collective-permute-start(bf16[4,64,768]{2,1,0:T(8,128)(2,1)S(1)} %collective-permute-done.24.refs_7_), channel_id=1, source_target_pairs={{0,1},{1,0},{2,3},{3,2},{4,5},{5,4},{6,7},{7,6},{8,9},{9,8},{10,11... | collective-permute-start | bytes 1179656 | tf_op jit(solution)/shard_map/ppermute | solution.py:335
  82.2 3.3 %collective-permute-start.28 = (bf16[4,128,768]{2,1,0:T(8,128)(2,1)S(1)}, bf16[4,128,768]{2,1,0:T(8,128)(2,1)S(1)}, u32[]{:S(2)}, u32[]{:S(2)}) collective-permute-start(bf16[4,128,768]{2,1,0:T(8,128)(2,1)S(1)} %order_z.2.refs_0_), channel_id=1, source_target_pairs={{0,1},{1,0},{2,3},{3,2},{4,5},{5,4},{6,7},{7,6},{8,9},{9,8},{10,11... | collective-permute-start | bytes 2359304 | tf_op jit(solution)/shard_map/ppermute | solution.py:335
  82.2 4.0 %collective-permute-start.29 = (bf16[4,128,768]{2,1,0:T(8,128)(2,1)S(1)}, bf16[4,128,768]{2,1,0:T(8,128)(2,1)S(1)}, u32[]{:S(2)}, u32[]{:S(2)}) collective-permute-start(bf16[4,128,768]{2,1,0:T(8,128)(2,1)S(1)} %collective-permute-done.10.refs_1_), channel_id=1, source_target_pairs={{0,1},{1,0},{2,3},{3,2},{4,5},{5,4},{6,7},{7,6},{8,9},{9,8},{10,11... | collective-permute-start | bytes 2359304 | tf_op jit(solution)/shard_map/ppermute | solution.py:335
  82.7 4.6 %collective-permute-start.30 = (bf16[4,128,768]{2,1,0:T(8,128)(2,1)S(1)}, bf16[4,128,768]{2,1,0:T(8,128)(2,1)S(1)}, u32[]{:S(2)}, u32[]{:S(2)}) collective-permute-start(bf16[4,128,768]{2,1,0:T(8,128)(2,1)S(1)} %collective-permute-done.11.refs_2_), channel_id=1, source_target_pairs={{0,1},{1,0},{2,3},{3,2},{4,5},{5,4},{6,7},{7,6},{8,9},{9,8},{10,11... | collective-permute-start | bytes 2359304 | tf_op jit(solution)/shard_map/ppermute | solution.py:335
  83.4 17.3 %collective-permute-start.27 = (bf16[4,96,768]{2,1,0:T(8,128)(2,1)S(1)}, bf16[4,96,768]{2,1,0:T(8,128)(2,1)S(1)}, u32[]{:S(2)}, u32[]{:S(2)}) collective-permute-start(bf16[4,96,768]{2,1,0:T(8,128)(2,1)S(1)} %order_z.3.refs_0_), channel_id=1, source_target_pairs={{0,4},{4,0},{1,5},{5,1},{2,6},{6,2},{3,7},{7,3},{8,12},{12,8},{9,1... | collective-permute-start | bytes 1769480 | tf_op jit(solution)/shard_map/ppermute | solution.py:335
  85.0 15.8 %collective-permute-start.26 = (bf16[4,96,768]{2,1,0:T(8,128)(2,1)S(1)}, bf16[4,96,768]{2,1,0:T(8,128)(2,1)S(1)}, u32[]{:S(2)}, u32[]{:S(2)}) collective-permute-start(bf16[4,96,768]{2,1,0:T(8,128)(2,1)S(1)} %order_z.3.refs_0_), channel_id=1, source_target_pairs={{0,2},{2,0},{1,3},{3,1},{4,6},{6,4},{5,7},{7,5},{8,10},{10,8},{9,1... | collective-permute-start | bytes 1769480 | tf_op jit(solution)/shard_map/ppermute | solution.py:335
  85.5 24.9 %collective-permute-start.35 = (bf16[4,96,768]{2,1,0:T(8,128)(2,1)S(1)}, bf16[4,96,768]{2,1,0:T(8,128)(2,1)S(1)}, u32[]{:S(2)}, u32[]{:S(2)}) collective-permute-start(bf16[4,96,768]{2,1,0:T(8,128)(2,1)S(1)} %order_z.3.refs_0_), channel_id=1, source_target_pairs={{0,1},{1,0},{2,3},{3,2},{4,5},{5,4},{6,7},{7,6},{8,9},{9,8},{10,11... | collective-permute-start | bytes 1769480 | tf_op jit(solution)/shard_map/ppermute | solution.py:335
  100.8 9.1 %collective-permute-start.34 = (bf16[4,48,768]{2,1,0:T(8,128)(2,1)S(1)}, bf16[4,48,768]{2,1,0:T(8,128)(2,1)S(1)}, u32[]{:S(2)}, u32[]{:S(2)}) collective-permute-start(bf16[4,48,768]{2,1,0:T(8,128)(2,1)S(1)} %slice.115), channel_id=1, source_target_pairs={{0,2},{2,0},{1,3},{3,1},{4,6},{6,4},{5,7},{7,5},{8,10},{10,8},{9,1... | collective-permute-start | bytes 884744 | tf_op jit(solution)/shard_map/ppermute | solution.py:335
  101.5 8.8 %collective-permute-start.33 = (bf16[4,48,768]{2,1,0:T(8,128)(2,1)S(1)}, bf16[4,48,768]{2,1,0:T(8,128)(2,1)S(1)}, u32[]{:S(2)}, u32[]{:S(2)}) collective-permute-start(bf16[4,48,768]{2,1,0:T(8,128)(2,1)S(1)} %slice.114), channel_id=1, source_target_pairs={{0,4},{4,0},{1,5},{5,1},{2,6},{6,2},{3,7},{7,3},{8,12},{12,8},{9,1... | collective-permute-start | bytes 884744 | tf_op jit(solution)/shard_map/ppermute | solution.py:335
  103.0 8.9 %collective-permute-start.36 = (bf16[4,96,768]{2,1,0:T(8,128)(2,1)S(1)}, bf16[4,96,768]{2,1,0:T(8,128)(2,1)S(1)}, u32[]{:S(2)}, u32[]{:S(2)}) collective-permute-start(bf16[4,96,768]{2,1,0:T(8,128)(2,1)S(1)} %collective-permute-done.26.refs_1_), channel_id=1, source_target_pairs={{0,1},{1,0},{2,3},{3,2},{4,5},{5,4},{6,7},{7,6},{8,9},{9,8},{10,11... | collective-permute-start | bytes 1769480 | tf_op jit(solution)/shard_map/ppermute | solution.py:335
  103.0 8.9 %collective-permute-start.37 = (bf16[4,96,768]{2,1,0:T(8,128)(2,1)S(1)}, bf16[4,96,768]{2,1,0:T(8,128)(2,1)S(1)}, u32[]{:S(2)}, u32[]{:S(2)}) collective-permute-start(bf16[4,96,768]{2,1,0:T(8,128)(2,1)S(1)} %collective-permute-done.27.refs_2_), channel_id=1, source_target_pairs={{0,1},{1,0},{2,3},{3,2},{4,5},{5,4},{6,7},{7,6},{8,9},{9,8},{10,11... | collective-permute-start | bytes 1769480 | tf_op jit(solution)/shard_map/ppermute | solution.py:335
  109.9 1.6 collective-permute-start.39
  110.3 1.7 collective-permute-start.38
  130.7 9.4 %collective-permute-start.40 = (bf16[16,96,768]{2,1,0:T(8,128)(2,1)S(1)}, bf16[16,96,768]{2,1,0:T(8,128)(2,1)S(1)}, u32[]{:S(2)}, u32[]{:S(2)}) collective-permute-start(bf16[16,96,768]{2,1,0:T(8,128)(2,1)S(1)} %get-tuple-element.173), channel_id=1, source_target_pairs={{0,1},{1,0},{2,3},{3,2},{4,5},{5,4},{6,7},{7,6},{8,9},{9,8},{10,11... | collective-permute-start | bytes 7077896 | tf_op jit(solution)/shard_map/ppermute | solution.py:335
  140.8 11.4 %collective-permute-start.41 = (bf16[4,48,768]{2,1,0:T(8,128)(2,1)S(1)}, bf16[4,48,768]{2,1,0:T(8,128)(2,1)S(1)}, u32[]{:S(2)}, u32[]{:S(2)}) collective-permute-start(bf16[4,48,768]{2,1,0:T(8,128)(2,1)S(1)} %get-tuple-element.175), channel_id=1, source_target_pairs={{0,2},{2,0},{1,3},{3,1},{4,6},{6,4},{5,7},{7,5},{8,10},{10,8},{9,1... | collective-permute-start | bytes 884744 | tf_op jit(solution)/shard_map/ppermute | solution.py:335
  142.3 9.9 %collective-permute-start.42 = (bf16[4,48,768]{2,1,0:T(8,128)(2,1)S(1)}, bf16[4,48,768]{2,1,0:T(8,128)(2,1)S(1)}, u32[]{:S(2)}, u32[]{:S(2)}) collective-permute-start(bf16[4,48,768]{2,1,0:T(8,128)(2,1)S(1)} %get-tuple-element.176), channel_id=1, source_target_pairs={{0,4},{4,0},{1,5},{5,1},{2,6},{6,2},{3,7},{7,3},{8,12},{12,8},{9,1... | collective-permute-start | bytes 884744 | tf_op jit(solution)/shard_map/ppermute | solution.py:335
  152.3 11.5 %collective-permute-start.43 = (bf16[16,128,768]{2,1,0:T(8,128)(2,1)S(1)}, bf16[16,128,768]{2,1,0:T(8,128)(2,1)S(1)}, u32[]{:S(2)}, u32[]{:S(2)}) collective-permute-start(bf16[16,128,768]{2,1,0:T(8,128)(2,1)S(1)} %get-tuple-element.184), channel_id=1, source_target_pairs={{0,1},{1,0},{2,3},{3,2},{4,5},{5,4},{6,7},{7,6},{8,9},{9,8},{10,11... | collective-permute-start | bytes 9437192 | tf_op jit(solution)/shard_map/ppermute | solution.py:335
  153.3 23.6 %collective-permute-start.46 = (bf16[4,96,768]{2,1,0:T(8,128)(2,1)S(1)}, bf16[4,96,768]{2,1,0:T(8,128)(2,1)S(1)}, u32[]{:S(2)}, u32[]{:S(2)}) collective-permute-start(bf16[4,96,768]{2,1,0:T(8,128)(2,1)S(1)} %get-tuple-element.185), channel_id=1, source_target_pairs={{0,4},{4,0},{1,5},{5,1},{2,6},{6,2},{3,7},{7,3},{8,12},{12,8},{9,1... | collective-permute-start | bytes 1769480 | tf_op jit(solution)/shard_map/ppermute | solution.py:335
  153.9 23.0 %collective-permute-start.47 = (bf16[4,96,768]{2,1,0:T(8,128)(2,1)S(1)}, bf16[4,96,768]{2,1,0:T(8,128)(2,1)S(1)}, u32[]{:S(2)}, u32[]{:S(2)}) collective-permute-start(bf16[4,96,768]{2,1,0:T(8,128)(2,1)S(1)} %get-tuple-element.186), channel_id=1, source_target_pairs={{0,2},{2,0},{1,3},{3,1},{4,6},{6,4},{5,7},{7,5},{8,10},{10,8},{9,1... | collective-permute-start | bytes 1769480 | tf_op jit(solution)/shard_map/ppermute | solution.py:335
  164.5 13.2 %collective-permute-start.44 = (bf16[4,64,768]{2,1,0:T(8,128)(2,1)S(1)}, bf16[4,64,768]{2,1,0:T(8,128)(2,1)S(1)}, u32[]{:S(2)}, u32[]{:S(2)}) collective-permute-start(bf16[4,64,768]{2,1,0:T(8,128)(2,1)S(1)} %get-tuple-element.192), channel_id=1, source_target_pairs={{0,2},{2,0},{1,3},{3,1},{4,6},{6,4},{5,7},{7,5},{8,10},{10,8},{9,1... | collective-permute-start | bytes 1179656 | tf_op jit(solution)/shard_map/ppermute | solution.py:335
  166.0 11.8 %collective-permute-start.45 = (bf16[4,64,768]{2,1,0:T(8,128)(2,1)S(1)}, bf16[4,64,768]{2,1,0:T(8,128)(2,1)S(1)}, u32[]{:S(2)}, u32[]{:S(2)}) collective-permute-start(bf16[4,64,768]{2,1,0:T(8,128)(2,1)S(1)} %get-tuple-element.193), channel_id=1, source_target_pairs={{0,4},{4,0},{1,5},{5,1},{2,6},{6,2},{3,7},{7,3},{8,12},{12,8},{9,1... | collective-permute-start | bytes 1179656 | tf_op jit(solution)/shard_map/ppermute | solution.py:335
  177.7 7.0 %collective-permute-start.48 = (bf16[2,2,256,768]{3,2,1,0:T(8,128)(2,1)S(1)}, bf16[2,2,256,768]{3,2,1,0:T(8,128)(2,1)S(1)}, u32[]{:S(2)}, u32[]{:S(2)}) collective-permute-start(bf16[2,2,256,768]{3,2,1,0:T(8,128)(2,1)S(1)} %get-tuple-element.202), channel_id=1, source_target_pairs={{0,1},{1,0},{2,3},{3,2},{4,5},{5,4},{6,7},{7,6},{8,9},{9,8},{10,11... | collective-permute-start | bytes 4718600 | tf_op jit(solution)/shard_map/ppermute | solution.py:335
  178.8 20.0 %collective-permute-start.49 = (bf16[4,128,768]{2,1,0:T(8,128)(2,1)S(1)}, bf16[4,128,768]{2,1,0:T(8,128)(2,1)S(1)}, u32[]{:S(2)}, u32[]{:S(2)}) collective-permute-start(bf16[4,128,768]{2,1,0:T(8,128)(2,1)S(1)} %get-tuple-element.203), channel_id=1, source_target_pairs={{0,4},{4,0},{1,5},{5,1},{2,6},{6,2},{3,7},{7,3},{8,12},{12,8},{9,1... | collective-permute-start | bytes 2359304 | tf_op jit(solution)/shard_map/ppermute | solution.py:335
  180.3 19.7 %collective-permute-start.50 = (bf16[4,128,768]{2,1,0:T(8,128)(2,1)S(1)}, bf16[4,128,768]{2,1,0:T(8,128)(2,1)S(1)}, u32[]{:S(2)}, u32[]{:S(2)}) collective-permute-start(bf16[4,128,768]{2,1,0:T(8,128)(2,1)S(1)} %get-tuple-element.204), channel_id=1, source_target_pairs={{0,2},{2,0},{1,3},{3,1},{4,6},{6,4},{5,7},{7,5},{8,10},{10,8},{9,1... | collective-permute-start | bytes 2359304 | tf_op jit(solution)/shard_map/ppermute | solution.py:335
  181.8 15.6 %collective-permute-start.51 = (bf16[96,768]{1,0:T(8,128)(2,1)S(1)}, bf16[96,768]{1,0:T(8,128)(2,1)S(1)}, u32[]{:S(2)}, u32[]{:S(2)}) collective-permute-start(bf16[96,768]{1,0:T(8,128)(2,1)S(1)} %get-tuple-element.205), channel_id=1, source_target_pairs={{0,8},{8,0},{16,24},{24,16},{1,9},{9,1},{17,25},{25,17},{2,10},{10... | collective-permute-start | bytes 442376 | tf_op jit(solution)/shard_map/ppermute | solution.py:335
  182.5 14.9 %collective-permute-start.52 = (bf16[96,768]{1,0:T(8,128)(2,1)S(1)}, bf16[96,768]{1,0:T(8,128)(2,1)S(1)}, u32[]{:S(2)}, u32[]{:S(2)}) collective-permute-start(bf16[96,768]{1,0:T(8,128)(2,1)S(1)} %get-tuple-element.206), channel_id=1, source_target_pairs={{0,16},{8,24},{16,0},{24,8},{1,17},{9,25},{17,1},{25,9},{2,18},{10... | collective-permute-start | bytes 442376 | tf_op jit(solution)/shard_map/ppermute | solution.py:335
  184.8 12.7 %collective-permute-start.53 = (bf16[96,768]{1,0:T(8,128)(2,1)S(1)}, bf16[96,768]{1,0:T(8,128)(2,1)S(1)}, u32[]{:S(2)}, u32[]{:S(2)}) collective-permute-start(bf16[96,768]{1,0:T(8,128)(2,1)S(1)} %get-tuple-element.207), channel_id=1, source_target_pairs={{0,24},{8,16},{16,8},{24,0},{1,25},{9,17},{17,9},{25,1},{2,26},{10... | collective-permute-start | bytes 442376 | tf_op jit(solution)/shard_map/ppermute | solution.py:335
  200.0 4.0 %collective-permute-start.54 = (bf16[16,80,768]{2,1,0:T(8,128)(2,1)S(1)}, bf16[16,80,768]{2,1,0:T(8,128)(2,1)S(1)}, u32[]{:S(2)}, u32[]{:S(2)}) collective-permute-start(bf16[16,80,768]{2,1,0:T(8,128)(2,1)S(1)} %get-tuple-element.215), channel_id=1, source_target_pairs={{0,1},{1,0},{2,3},{3,2},{4,5},{5,4},{6,7},{7,6},{8,9},{9,8},{10,11... | collective-permute-start | bytes 5898248 | tf_op jit(solution)/shard_map/ppermute | solution.py:335
  204.6 8.1 %collective-permute-start.55 = (bf16[4,40,768]{2,1,0:T(8,128)(2,1)S(1)}, bf16[4,40,768]{2,1,0:T(8,128)(2,1)S(1)}, u32[]{:S(2)}, u32[]{:S(2)}) collective-permute-start(bf16[4,40,768]{2,1,0:T(8,128)(2,1)S(1)} %get-tuple-element.216), channel_id=1, source_target_pairs={{0,2},{2,0},{1,3},{3,1},{4,6},{6,4},{5,7},{7,5},{8,10},{10,8},{9,1... | collective-permute-start | bytes 737288 | tf_op jit(solution)/shard_map/ppermute | solution.py:335
  205.2 7.7 %collective-permute-start.56 = (bf16[4,40,768]{2,1,0:T(8,128)(2,1)S(1)}, bf16[4,40,768]{2,1,0:T(8,128)(2,1)S(1)}, u32[]{:S(2)}, u32[]{:S(2)}) collective-permute-start(bf16[4,40,768]{2,1,0:T(8,128)(2,1)S(1)} %get-tuple-element.217), channel_id=1, source_target_pairs={{0,4},{4,0},{1,5},{5,1},{2,6},{6,2},{3,7},{7,3},{8,12},{12,8},{9,1... | collective-permute-start | bytes 737288 | tf_op jit(solution)/shard_map/ppermute | solution.py:335
  207.1 9.7 %collective-permute-start.59 = (bf16[128,768]{1,0:T(8,128)(2,1)S(1)}, bf16[128,768]{1,0:T(8,128)(2,1)S(1)}, u32[]{:S(2)}, u32[]{:S(2)}) collective-permute-start(bf16[128,768]{1,0:T(8,128)(2,1)S(1)} %get-tuple-element.219), channel_id=1, source_target_pairs={{0,8},{8,0},{16,24},{24,16},{1,9},{9,1},{17,25},{25,17},{2,10},{10... | collective-permute-start | bytes 589832 | tf_op jit(solution)/shard_map/ppermute | solution.py:335
  207.7 17.2 %collective-permute-start.60 = (bf16[128,768]{1,0:T(8,128)(2,1)S(1)}, bf16[128,768]{1,0:T(8,128)(2,1)S(1)}, u32[]{:S(2)}, u32[]{:S(2)}) collective-permute-start(bf16[128,768]{1,0:T(8,128)(2,1)S(1)} %get-tuple-element.220), channel_id=1, source_target_pairs={{0,16},{8,24},{16,0},{24,8},{1,17},{9,25},{17,1},{25,9},{2,18},{10... | collective-permute-start | bytes 589832 | tf_op jit(solution)/shard_map/ppermute | solution.py:335
  210.0 14.9 %collective-permute-start.61 = (bf16[128,768]{1,0:T(8,128)(2,1)S(1)}, bf16[128,768]{1,0:T(8,128)(2,1)S(1)}, u32[]{:S(2)}, u32[]{:S(2)}) collective-permute-start(bf16[128,768]{1,0:T(8,128)(2,1)S(1)} %get-tuple-element.221), channel_id=1, source_target_pairs={{0,24},{8,16},{16,8},{24,0},{1,25},{9,17},{17,9},{25,1},{2,26},{10... | collective-permute-start | bytes 589832 | tf_op jit(solution)/shard_map/ppermute | solution.py:335
  213.7 13.2 %collective-permute-start.57 = (bf16[4,80,768]{2,1,0:T(8,128)(2,1)S(1)}, bf16[4,80,768]{2,1,0:T(8,128)(2,1)S(1)}, u32[]{:S(2)}, u32[]{:S(2)}) collective-permute-start(bf16[4,80,768]{2,1,0:T(8,128)(2,1)S(1)} %get-tuple-element.224), channel_id=1, source_target_pairs={{0,4},{4,0},{1,5},{5,1},{2,6},{6,2},{3,7},{7,3},{8,12},{12,8},{9,1... | collective-permute-start | bytes 1474568 | tf_op jit(solution)/shard_map/ppermute | solution.py:335
  214.6 12.3 %collective-permute-start.58 = (bf16[4,80,768]{2,1,0:T(8,128)(2,1)S(1)}, bf16[4,80,768]{2,1,0:T(8,128)(2,1)S(1)}, u32[]{:S(2)}, u32[]{:S(2)}) collective-permute-start(bf16[4,80,768]{2,1,0:T(8,128)(2,1)S(1)} %get-tuple-element.225), channel_id=1, source_target_pairs={{0,2},{2,0},{1,3},{3,1},{4,6},{6,4},{5,7},{7,5},{8,10},{10,8},{9,1... | collective-permute-start | bytes 1474568 | tf_op jit(solution)/shard_map/ppermute | solution.py:335
  227.9 7.1 %collective-permute-start.62 = (bf16[80,768]{1,0:T(8,128)(2,1)S(1)}, bf16[80,768]{1,0:T(8,128)(2,1)S(1)}, u32[]{:S(2)}, u32[]{:S(2)}) collective-permute-start(bf16[80,768]{1,0:T(8,128)(2,1)S(1)} %get-tuple-element.233), channel_id=1, source_target_pairs={{0,8},{8,0},{16,24},{24,16},{1,9},{9,1},{17,25},{25,17},{2,10},{10... | collective-permute-start | bytes 368648 | tf_op jit(solution)/shard_map/ppermute | solution.py:335
  231.0 10.9 %collective-permute-start.63 = (bf16[80,768]{1,0:T(8,128)(2,1)S(1)}, bf16[80,768]{1,0:T(8,128)(2,1)S(1)}, u32[]{:S(2)}, u32[]{:S(2)}) collective-permute-start(bf16[80,768]{1,0:T(8,128)(2,1)S(1)} %get-tuple-element.234), channel_id=1, source_target_pairs={{0,16},{8,24},{16,0},{24,8},{1,17},{9,25},{17,1},{25,9},{2,18},{10... | collective-permute-start | bytes 368648 | tf_op jit(solution)/shard_map/ppermute | solution.py:335
  231.9 10.0 %collective-permute-start.64 = (bf16[80,768]{1,0:T(8,128)(2,1)S(1)}, bf16[80,768]{1,0:T(8,128)(2,1)S(1)}, u32[]{:S(2)}, u32[]{:S(2)}) collective-permute-start(bf16[80,768]{1,0:T(8,128)(2,1)S(1)} %get-tuple-element.235), channel_id=1, source_target_pairs={{0,24},{8,16},{16,8},{24,0},{1,25},{9,17},{17,9},{25,1},{2,26},{10... | collective-permute-start | bytes 368648 | tf_op jit(solution)/shard_map/ppermute | solution.py:335
  (56 other events, 352.3 us)
